TPU v7x, 32 devices: a whole 2x2x4 slice. The times are simulated.
32 devices in a mesh: seq: 4 (over y, x), fsdp: 8 (over z, core).
Axes of the slice: x: 2, y: 2, z: 4, core: 2. Of those that a mesh axis runs over, the one named last changes fastest.
Arguments:
- tokens: bfloat16 [16, 1024, 2048], P('fsdp', 'seq'), may hold values from -6 to 6
- cotangent: bfloat16 [16, 1024, 2048], P('fsdp', 'seq'), may hold values from -6 to 6
- lengths: int32 [16], P('fsdp'), may hold values from 512 to 1024, as said below
- decay: float32 [16, 1024], P('seq'), may hold values from -1 to 0
- query_weight: bfloat16 [2048, 2048], P('fsdp'), may hold values from -0.125 to 0.125
- key_weight: bfloat16 [2048, 2048], P('fsdp'), may hold values from -0.125 to 0.125
- value_weight: bfloat16 [2048, 2048], P('fsdp'), may hold values from -0.125 to 0.125
- outgate_weight: bfloat16 [2048, 2048], P('fsdp'), may hold values from -0.125 to 0.125
- output_weight: bfloat16 [2048, 2048], P('fsdp'), may hold values from -0.125 to 0.125
- left_weight: bfloat16 [5632, 2048], P('fsdp'), may hold values from -0.125 to 0.125
- right_weight: bfloat16 [5632, 2048], P('fsdp'), may hold values from -0.125 to 0.125
- down_weight: bfloat16 [5632, 2048], P('fsdp'), may hold values from -0.078125 to 0.078125
Outputs:
- layer_out: bfloat16 [16, 1024, 2048], P('fsdp', 'seq')
- input_grad: bfloat16 [16, 1024, 2048], P('fsdp', 'seq')
- query_grad: float32 [2048, 2048], P('fsdp')
- key_grad: float32 [2048, 2048], P('fsdp')
- value_grad: float32 [2048, 2048], P('fsdp')
- outgate_grad: float32 [2048, 2048], P('fsdp')
- output_grad: float32 [2048, 2048], P('fsdp')
- left_grad: float32 [5632, 2048], P('fsdp')
- right_grad: float32 [5632, 2048], P('fsdp')
- down_grad: float32 [5632, 2048], P('fsdp')
Inputs may be any that keep to these rules, and one draw needn't show every extreme that they name: `lengths`: some sequence has all 1024 slots valid and another exactly 512.
All inputs are finite; a program needn't handle non-finite values.
Results may differ from a plain program's by a relative error of at most 0.02.
Values may be sent and summed in bfloat16 or wider, within the bound.
No kernel may reach another device: no remote copies, remote signals or barrier semaphores. Data moves between devices by JAX's collectives and lax.ppermute only.
A program may use at most 576 MiB of HBM per device.

v0:
```python
import jax
import jax.numpy as jnp
from jax import lax
from jax.sharding import PartitionSpec as P

BLOCK = 256


highest = lax.Precision.HIGHEST
eps_norm = 1e-06


def shortened(x):

    def short(part):
        return part.astype(jnp.bfloat16) if part.dtype == jnp.float32 else part

    return jax.tree.map(short, x)


def scaled(values):
    factor = lax.rsqrt(jnp.mean(values * values, axis=-1, keepdims=True) + eps_norm)
    return (values * factor, factor)


def scaled_back(values, factor, grad_in):
    inner_mean = jnp.mean(grad_in * values, axis=-1, keepdims=True)
    return factor * grad_in - values * (factor * factor * factor) * inner_mean


def times_rows(left_side, weight):
    return lax.dot_general(
        left_side, weight, (((1,), (1,)), ((), ())), preferred_element_type=jnp.float32
    )


def rows_outer(left_side, right_side):
    return lax.dot_general(
        left_side, right_side, (((0,), (0,)), ((), ())), preferred_element_type=jnp.float32
    )


def block_step(state_now, query_block, key_block, value_block, decay_sums):
    size_block = decay_sums.shape[-1]
    row_ids = lax.broadcasted_iota(jnp.int32, (size_block, size_block), 0)
    col_ids = lax.broadcasted_iota(jnp.int32, (size_block, size_block), 1)
    causal = (row_ids >= col_ids)[None]
    spread = decay_sums[:, :, None] - decay_sums[:, None, :]
    weights = jnp.where(causal, jnp.exp(jnp.where(causal, spread, 0.0)), 0.0)
    scores = jnp.einsum("thi,shi->hts", query_block, key_block, precision=highest) * weights
    inner_part = jnp.einsum("hts,shj->thj", scores, value_block, precision=highest)
    carried = (
        jnp.einsum("thi,hij->thj", query_block, state_now, precision=highest)
        * jnp.exp(decay_sums).T[:, :, None]
    )
    tail_decay = jnp.exp(decay_sums[:, -1:] - decay_sums).T
    state_next = jnp.exp(decay_sums[:, -1])[:, None, None] * state_now + jnp.einsum(
        "shi,shj->hij", key_block * tail_decay[:, :, None], value_block, precision=highest
    )
    return (state_next, inner_part + carried)


def attend(pre_query, pre_key, pre_value, decay_sums):
    slot_count, feat_here = pre_query.shape
    block_count, head_count, _ = decay_sums.shape
    head_width = feat_here // head_count
    shape_blocks = (block_count, BLOCK, head_count, head_width)
    queries = jax.nn.silu(pre_query).reshape(shape_blocks)
    key_rows = jax.nn.silu(pre_key).reshape(shape_blocks)
    values = pre_value.reshape(shape_blocks)
    starts = lax.iota(jnp.int32, block_count) * BLOCK

    def step_fn(state_now, inputs):
        query_block, key_block, value_block, block_sums, block_start = inputs
        return block_step(state_now, query_block, key_block, value_block, block_sums)

    start_state = jnp.zeros((head_count, head_width, head_width), jnp.float32)
    _, outputs = lax.scan(
        jax.checkpoint(step_fn), start_state, (queries, key_rows, values, decay_sums, starts)
    )
    return outputs.reshape(slot_count, feat_here)


def on_device(
    tokens,
    cotangent,
    lengths,
    decay,
    query_weight,
    key_weight,
    value_weight,
    outgate_weight,
    output_weight,
    left_weight,
    right_weight,
    down_weight,
):
    micro_count, local_len, feat_width = tokens.shape
    fsdp_size = lax.axis_size("fsdp")
    positions = lax.axis_index("seq") * local_len + lax.iota(jnp.int32, local_len)
    head_count = decay.shape[0]
    slot_count = decay.shape[1]
    decay_sums = jnp.cumsum(
        decay.reshape(head_count, slot_count // BLOCK, BLOCK), axis=-1
    ).transpose(1, 0, 2)
    seq_shape = (1, local_len, feat_width)
    layer_list = []
    input_list = []
    accum = None
    full_query, full_key, full_value, full_outgate, full_output = (
        lax.all_gather(query_weight, "fsdp", axis=0, tiled=True),
        lax.all_gather(key_weight, "fsdp", axis=0, tiled=True),
        lax.all_gather(value_weight, "fsdp", axis=0, tiled=True),
        lax.all_gather(outgate_weight, "fsdp", axis=0, tiled=True),
        lax.all_gather(output_weight, "fsdp", axis=0, tiled=True),
    )
    for micro_item in range(micro_count):
        length_item = lengths[micro_item]
        valid_rows = (positions < length_item).astype(jnp.float32).reshape(local_len, 1)
        tokens_wide = tokens[micro_item].astype(jnp.float32)
        normed, factor_input = scaled(tokens_wide)
        normed_low = normed.astype(jnp.bfloat16)
        pre_query = times_rows(normed_low, full_query).astype(jnp.bfloat16)
        pre_key = times_rows(normed_low, full_key).astype(jnp.bfloat16)
        pre_value = times_rows(normed_low, full_value).astype(jnp.bfloat16)
        outgate = times_rows(normed_low, full_outgate)
        head_query, head_key, head_value = (
            lax.all_to_all(
                pre_query.reshape(seq_shape), "seq", split_axis=2, concat_axis=1, tiled=True
            ),
            lax.all_to_all(
                pre_key.reshape(seq_shape), "seq", split_axis=2, concat_axis=1, tiled=True
            ),
            lax.all_to_all(
                pre_value.reshape(seq_shape), "seq", split_axis=2, concat_axis=1, tiled=True
            ),
        )
        query_wide = head_query[0].astype(jnp.float32)
        key_wide = head_key[0].astype(jnp.float32)
        value_wide = head_value[0].astype(jnp.float32)
        attn_heads = attend(query_wide, key_wide, value_wide, decay_sums)
        attn_heads = attn_heads.astype(jnp.bfloat16)[None]
        attn_back = lax.all_to_all(attn_heads, "seq", split_axis=1, concat_axis=2, tiled=True)
        attn_rows = attn_back.reshape(local_len, feat_width).astype(jnp.float32)
        attn_normed, factor_attn = scaled(attn_rows)
        gated_rows = (attn_normed * outgate).astype(jnp.bfloat16)
        branch = times_rows(gated_rows, full_output)
        residual = tokens_wide + branch
        resid_normed, factor_resid = scaled(residual)
        resid_low = resid_normed.astype(jnp.bfloat16)
        group_rows = lax.all_gather(resid_low, "fsdp", axis=0, tiled=True)
        left_all = times_rows(group_rows, left_weight)
        right_all = times_rows(group_rows, right_weight)
        product_all = (left_all * right_all).astype(jnp.bfloat16)
        ffn_out = lax.psum_scatter(
            jnp.dot(product_all, down_weight, preferred_element_type=jnp.float32).astype(
                jnp.bfloat16
            ),
            "fsdp",
            scatter_dimension=0,
            tiled=True,
        ).astype(jnp.float32)
        final_rows = valid_rows * (residual + ffn_out)
        layer_list.append(final_rows.astype(jnp.bfloat16))
        grad_y = valid_rows * cotangent[micro_item].astype(jnp.float32)
        grad_ffn = grad_y.astype(jnp.bfloat16)
        group_grad = lax.all_gather(grad_ffn, "fsdp", axis=0, tiled=True)
        grad_product = times_rows(group_grad, down_weight)
        grad_left = (grad_product * right_all).astype(jnp.bfloat16)
        grad_right = (grad_product * left_all).astype(jnp.bfloat16)
        grad_hn = lax.psum_scatter(
            (
                jnp.dot(grad_left, left_weight, preferred_element_type=jnp.float32)
                + jnp.dot(grad_right, right_weight, preferred_element_type=jnp.float32)
            ).astype(jnp.bfloat16),
            "fsdp",
            scatter_dimension=0,
            tiled=True,
        ).astype(jnp.float32)
        left_grad = rows_outer(grad_left, group_rows)
        right_grad = rows_outer(grad_right, group_rows)
        down_grad = rows_outer(product_all, group_grad)
        grad_resid = grad_y + scaled_back(residual, factor_resid, grad_hn)
        grad_branch = grad_resid.astype(jnp.bfloat16)
        grad_gated = jnp.dot(grad_branch, full_output, preferred_element_type=jnp.float32)
        grad_outgate = (grad_gated * attn_normed).astype(jnp.bfloat16)
        grad_attn = scaled_back(attn_rows, factor_attn, grad_gated * outgate).astype(jnp.bfloat16)
        head_grad = lax.all_to_all(
            grad_attn.reshape(seq_shape), "seq", split_axis=2, concat_axis=1, tiled=True
        )

        def local_attend(query_in, key_in, value_in):
            return attend(query_in, key_in, value_in, decay_sums)

        _, pullback = jax.vjp(local_attend, query_wide, key_wide, value_wide)
        grad_parts = pullback(head_grad[0].astype(jnp.float32))
        back_query, back_key, back_value = (
            lax.all_to_all(
                grad_parts[0].astype(jnp.bfloat16)[None],
                "seq",
                split_axis=1,
                concat_axis=2,
                tiled=True,
            ),
            lax.all_to_all(
                grad_parts[1].astype(jnp.bfloat16)[None],
                "seq",
                split_axis=1,
                concat_axis=2,
                tiled=True,
            ),
            lax.all_to_all(
                grad_parts[2].astype(jnp.bfloat16)[None],
                "seq",
                split_axis=1,
                concat_axis=2,
                tiled=True,
            ),
        )
        grad_query = back_query.reshape(local_len, feat_width)
        grad_key = back_key.reshape(local_len, feat_width)
        grad_value = back_value.reshape(local_len, feat_width)
        grad_normed = (
            jnp.dot(grad_query, full_query, preferred_element_type=jnp.float32)
            + jnp.dot(grad_key, full_key, preferred_element_type=jnp.float32)
            + jnp.dot(grad_value, full_value, preferred_element_type=jnp.float32)
            + jnp.dot(grad_outgate, full_outgate, preferred_element_type=jnp.float32)
        )
        input_rows = grad_resid + scaled_back(tokens_wide, factor_input, grad_normed)
        input_list.append(input_rows.astype(jnp.bfloat16))
        gathered = (
            lax.all_gather(normed_low, "fsdp", axis=0, tiled=True),
            lax.all_gather(gated_rows, "fsdp", axis=0, tiled=True),
            lax.all_gather(grad_query, "fsdp", axis=0, tiled=True),
            lax.all_gather(grad_key, "fsdp", axis=0, tiled=True),
            lax.all_gather(grad_value, "fsdp", axis=0, tiled=True),
            lax.all_gather(grad_outgate, "fsdp", axis=0, tiled=True),
            lax.all_gather(grad_branch, "fsdp", axis=0, tiled=True),
        )
        width_own = feat_width // fsdp_size
        start_own = lax.axis_index("fsdp") * width_own

        def own_rows(grad_all, inputs_all):
            return rows_outer(
                lax.dynamic_slice_in_dim(grad_all, start_own, width_own, 1), inputs_all
            )

        query_grad = own_rows(gathered[2], gathered[0])
        key_grad = own_rows(gathered[3], gathered[0])
        value_grad = own_rows(gathered[4], gathered[0])
        outgate_grad = own_rows(gathered[5], gathered[0])
        output_grad = own_rows(gathered[6], gathered[1])
        current = (
            query_grad,
            key_grad,
            value_grad,
            outgate_grad,
            output_grad,
            left_grad,
            right_grad,
            down_grad,
        )
        if accum is None:
            accum = current
        else:
            accum = tuple((total_one + grad_one for total_one, grad_one in zip(accum, current)))
    summed = jax.tree.map(lambda part: part.astype(jnp.float32), lax.psum(shortened(accum), "seq"))
    layer_out = jnp.stack(layer_list)
    input_grad = jnp.stack(input_list)
    return (
        layer_out,
        input_grad,
        summed[0],
        summed[1],
        summed[2],
        summed[3],
        summed[4],
        summed[5],
        summed[6],
        summed[7],
    )


def solution(mesh):
    placed = (
        P("fsdp", "seq", None),
        P("fsdp", "seq", None),
        P("fsdp"),
        P("seq", None),
        P("fsdp", None),
        P("fsdp", None),
        P("fsdp", None),
        P("fsdp", None),
        P("fsdp", None),
        P("fsdp", None),
        P("fsdp", None),
        P("fsdp", None),
    )
    return jax.shard_map(
        on_device,
        mesh=mesh,
        in_specs=placed,
        out_specs=(
            P("fsdp", "seq", None),
            P("fsdp", "seq", None),
            P("fsdp", None),
            P("fsdp", None),
            P("fsdp", None),
            P("fsdp", None),
            P("fsdp", None),
            P("fsdp", None),
            P("fsdp", None),
            P("fsdp", None),
        ),
        check_vma=False,
    )
```

profile of v0, /device:TPU:0, one launch (start us, length us, event | category | flops | bytes accessed | tf_op | source)
XLA Modules:
  0.0 2728.5 jit_solution(14296445528328162571)
XLA Ops:
  15.7 78.7 %all-gather.24.cloned.1.call-done = bf16[2048,2048]{1,0:T(8,128)(2,1)} async-done(((bf16[256,2048]{1,0:T(8,128)(2,1)}), bf16[2048,2048]{1,0:T(8,128)(2,1)}) %all-gather.24.cloned.1.call-update) | async-done | bytes 8388624 | tf_op jit(solution)/shard_map/all_gather | solution.py:112
  108.0 12.5 reduce.14
  128.2 48.4 %all-gather.28.cloned.1.call-done = bf16[2048,2048]{1,0:T(8,128)(2,1)} async-done(((bf16[256,2048]{1,0:T(8,128)(2,1)}), bf16[2048,2048]{1,0:T(8,128)(2,1)}) %all-gather.28.cloned.1.call-update) | async-done | bytes 8388624 | tf_op jit(solution)/shard_map/all_gather | solution.py:111
  189.7 12.5 reduce.16
  215.3 43.6 %all-gather.26.cloned.1.call-done = bf16[2048,2048]{1,0:T(8,128)(2,1)} async-done(((bf16[256,2048]{1,0:T(8,128)(2,1)}), bf16[2048,2048]{1,0:T(8,128)(2,1)}) %all-gather.26.cloned.1.call-update) | async-done | bytes 8388624 | tf_op jit(solution)/shard_map/all_gather | solution.py:113
  272.0 12.5 reduce.15
  327.1 75.5 %while.95 = (s32[]{:T(128)}, f32[4,128,128]{2,1,0:T(8,128)}, bf16[4,256,4,128]{1,3,2,0:T(8,128)(2,1)}, f32[4,4,256]{1,2,0:T(8,128)S(1)}, f32[4,256,4,128]{1,3,2,...) while((s32[]{:T(128)}, f32[4,128,128]{2,1,0:T(8,128)}, ...), condition=%wide.region_11.12_spmd.clone, body=%wide.region_10.11_spmd.clone.sunk | while | flops 1209730048 | bytes 20380964 | solution.py:78
  412.2 8.9 reduce.17
  424.9 19.3 all_to_all.184
  454.5 8.4 multiply_convert_fusion.10
  473.8 7.7 fusion.101
  487.5 12.7 reduce.10
  524.5 12.5 reduce.12
  557.8 12.6 reduce.11
  613.0 75.1 %while.94 = (s32[]{:T(128)}, f32[4,128,128]{2,1,0:T(8,128)}, bf16[4,256,4,128]{1,3,2,0:T(8,128)(2,1)}, f32[4,4,256]{1,2,0:T(8,128)S(1)}, f32[4,256,4,128]{1,3,2,...) while((s32[]{:T(128)}, f32[4,128,128]{2,1,0:T(8,128)}, ...), condition=%wide.region_4.5_spmd.clone, body=%wide.region_3.4_spmd.clone.sunk | while | flops 1209730048 | bytes 20380964 | solution.py:78
  697.7 8.9 reduce.13
  710.4 17.8 all_to_all.185
  738.5 8.3 multiply_convert_fusion.13
  756.5 11.8 fusion.193
  768.3 8.0 fusion.194
  776.3 13.1 multiply_convert_fusion
  789.5 10.3 fusion.197
  799.7 23.4 add_convert_fusion
  823.2 11.5 all-gather.34.cloned.1.call-done
  834.7 11.2 fusion.191
  846.0 8.0 fusion.192
  853.9 63.0 %all-gather.38.cloned.1.call-done = bf16[2048,2048]{1,0:T(8,128)(2,1)} async-done(((bf16[256,2048]{1,0:T(8,128)(2,1)}), bf16[2048,2048]{1,0:T(8,128)(2,1)}) %all-gather.38.cloned.1.call-update) | async-done | bytes 8388624 | tf_op jit(solution)/shard_map/all_gather | solution.py:167
  916.9 12.9 multiply_convert_fusion.2
  929.9 10.3 fusion.195
  940.2 13.0 add_convert_fusion.1
  953.3 10.9 convolution_convert_fusion
  964.2 10.9 convolution_convert_fusion.1
  975.8 31.5 %reduce-scatter.11.cloned.1.call-done = bf16[256,2048]{1,0:T(8,128)(2,1)} async-done(((bf16[2048,2048]{1,0:T(8,128)(2,1)}), bf16[256,2048]{1,0:T(8,128)(2,1)}) %reduce-scatter.11.cloned.1.call-update) | async-done | bytes 1048592 | tf_op jit(solution)/shard_map/reduce_scatter | solution.py:171
  1008.9 88.7 %reduce-scatter.9.cloned.1.call-done = bf16[256,2048]{1,0:T(8,128)(2,1)} async-done(((bf16[2048,2048]{1,0:T(8,128)(2,1)}), bf16[256,2048]{1,0:T(8,128)(2,1)}) %reduce-scatter.9.cloned.1.call-update) | async-done | bytes 1048592 | tf_op jit(solution)/shard_map/reduce_scatter | solution.py:171
  1099.7 88.0 %reduce-scatter.7.cloned.1.call-done = bf16[256,2048]{1,0:T(8,128)(2,1)} async-done(((bf16[2048,2048]{1,0:T(8,128)(2,1)}), bf16[256,2048]{1,0:T(8,128)(2,1)}) %reduce-scatter.7.cloned.1.call-update) | async-done | bytes 1048592 | tf_op jit(solution)/shard_map/reduce_scatter | solution.py:155
  1187.7 90.3 %reduce-scatter.5.cloned.1.call-done = bf16[256,2048]{1,0:T(8,128)(2,1)} async-done(((bf16[2048,2048]{1,0:T(8,128)(2,1)}), bf16[256,2048]{1,0:T(8,128)(2,1)}) %reduce-scatter.5.cloned.1.call-update) | async-done | bytes 1048592 | tf_op jit(solution)/shard_map/reduce_scatter | solution.py:155
  1297.6 15.8 while.96
  1316.1 11.5 reduce.22
  1358.4 93.0 %while.97 = (s32[]{:T(128)}, f32[4,128,128]{2,1,0:T(8,128)S(1)}, f32[4,256,4,128]{3,2,1,0:T(4,128)}, f32[4,256,4,128]{3,2,1,0:T(4,128)}, bf16[4,256,4,128]{1,3,2...) while((s32[]{:T(128)}, f32[4,128,128]{2,1,0:T(8,128)S(1)}, ...), condition=%wide.region_22.23_spmd.clone, body=%wide.region_21.22_spmd.clone.sunk | while | flops 2821850112 | bytes 28840304 | solution.py:78
  1461.7 16.0 all_to_all.180
  1499.4 14.7 all_to_all.181
  1520.4 10.5 reduce.18
  1547.7 7.9 reduce.23
  1564.7 18.8 while.98
  1596.7 92.6 %while.99 = (s32[]{:T(128)}, f32[4,128,128]{2,1,0:T(8,128)S(1)}, f32[4,256,4,128]{3,2,1,0:T(4,128)}, f32[4,256,4,128]{3,2,1,0:T(4,128)}, bf16[4,256,4,128]{1,3,2...) while((s32[]{:T(128)}, f32[4,128,128]{2,1,0:T(8,128)S(1)}, ...), condition=%wide.region_30.31_spmd.clone, body=%wide.region_29.30_spmd.clone.sunk | while | flops 2821850112 | bytes 28840304 | solution.py:78
  1699.4 14.5 all_to_all.182
  1735.9 12.5 all_to_all.183
  1774.6 11.8 fusion.200
  1789.1 11.7 add_convert_fusion.3
  1800.9 10.3 fusion.199
  1811.2 9.5 add_convert_fusion.4
  1820.8 7.9 fusion.201
  1828.7 9.5 add_convert_fusion.2
  1859.1 75.6 %all-gather.60.cloned.1.call-done = bf16[2048,2048]{1,0:T(8,128)(2,1)} async-done(((bf16[256,2048]{1,0:T(8,128)(2,1)}), bf16[2048,2048]{1,0:T(8,128)(2,1)}) %all-gather.60.cloned.1.call-update) | async-done | bytes 8388624 | tf_op jit(solution)/shard_map/all_gather | solution.py:237
  1934.7 7.6 fusion.99
  1942.3 75.0 %all-gather.54.cloned.1.call-done = bf16[2048,2048]{0,1:T(8,128)(2,1)} async-done(((bf16[256,2048]{0,1:T(8,128)(2,1)}), bf16[2048,2048]{0,1:T(8,128)(2,1)}) %all-gather.54.cloned.1.call-update) | async-done | bytes 8388624 | tf_op jit(solution)/shard_map/all_gather | solution.py:236
  2024.7 75.0 %all-gather.50.cloned.1.call-done = bf16[2048,2048]{0,1:T(8,128)(2,1)} async-done(((bf16[256,2048]{0,1:T(8,128)(2,1)}), bf16[2048,2048]{0,1:T(8,128)(2,1)}) %all-gather.50.cloned.1.call-update) | async-done | bytes 8388624 | tf_op jit(solution)/shard_map/all_gather | solution.py:235
  2107.0 74.8 %all-gather.42.cloned.1.call-done = bf16[2048,2048]{0,1:T(8,128)(2,1)} async-done(((bf16[256,2048]{0,1:T(8,128)(2,1)}), bf16[2048,2048]{0,1:T(8,128)(2,1)}) %all-gather.42.cloned.1.call-update) | async-done | bytes 8388624 | tf_op jit(solution)/shard_map/all_gather | solution.py:234
  2188.1 76.6 %all-gather.56.cloned.1.call-done = bf16[2048,2048]{0,1:T(8,128)(2,1)} async-done(((bf16[256,2048]{0,1:T(8,128)(2,1)}), bf16[2048,2048]{0,1:T(8,128)(2,1)}) %all-gather.56.cloned.1.call-update) | async-done | bytes 8388624 | tf_op jit(solution)/shard_map/all_gather | solution.py:236
  2264.7 7.6 fusion.98
  2272.3 75.2 %all-gather.52.cloned.1.call-done = bf16[2048,2048]{0,1:T(8,128)(2,1)} async-done(((bf16[256,2048]{0,1:T(8,128)(2,1)}), bf16[2048,2048]{0,1:T(8,128)(2,1)}) %all-gather.52.cloned.1.call-update) | async-done | bytes 8388624 | tf_op jit(solution)/shard_map/all_gather | solution.py:235
  2347.5 7.6 fusion.97
  2355.0 75.2 %all-gather.46.cloned.1.call-done = bf16[2048,2048]{0,1:T(8,128)(2,1)} async-done(((bf16[256,2048]{0,1:T(8,128)(2,1)}), bf16[2048,2048]{0,1:T(8,128)(2,1)}) %all-gather.46.cloned.1.call-update) | async-done | bytes 8388624 | tf_op jit(solution)/shard_map/all_gather | solution.py:234
  2472.1 229.3 %all-reduce.3.cloned.1.call-done = (bf16[256,2048]{1,0:T(8,128)(2,1)}, bf16[256,2048]{1,0:T(8,128)(2,1)}, bf16[256,2048]{1,0:T(8,128)(2,1)}, bf16[256,2048]{1,0:...) async-done(((bf16[256,2048]{1,0:T(8,128)(2,1)}, bf16[256,2048]{1,0:T(8,128)(2,1)}, ...) | async-done | bytes 13893648 | tf_op jit(solution)/shard_map/psum | solution.py:267
  (966 shorter events, 939.4 us)
Async XLA Ops:
  7.2 769.1 %copy-start = (bf16[704,2048]{1,0:T(8,128)(2,1)S(1)}, bf16[704,2048]{1,0:T(8,128)(2,1)}, u32[]{:S(2)}) copy-start(bf16[704,2048]{1,0:T(8,128)(2,1)} %param.35) | copy-start | bytes 8650756
  7.2 87.2 %all-gather.24.cloned.1.call-start = ((), (), s32[]{:S(2)}) async-start(), calls=%async_computation.20 | async-start | bytes 9437184 | tf_op jit(solution)/shard_map/all_gather | solution.py:112
  7.9 168.7 %all-gather.28.cloned.1.call-start = ((), (), s32[]{:S(2)}) async-start(), calls=%async_computation.22 | async-start | bytes 9437184 | tf_op jit(solution)/shard_map/all_gather | solution.py:111
  8.7 250.2 %all-gather.26.cloned.1.call-start = ((), (), s32[]{:S(2)}) async-start(), calls=%async_computation.21 | async-start | bytes 9437184 | tf_op jit(solution)/shard_map/all_gather | solution.py:113
  9.4 445.1 %all-gather.30.cloned.1.call-start = ((), (), s32[]{:S(2)}) async-start(), calls=%async_computation.23 | async-start | bytes 9437184 | tf_op jit(solution)/shard_map/all_gather | solution.py:114
  10.0 453.0 %all-gather.32.cloned.1.call-start = ((), (), s32[]{:S(2)}) async-start(), calls=%async_computation.24 | async-start | bytes 9437184 | tf_op jit(solution)/shard_map/all_gather | solution.py:115
  123.9 81.8 %all-to-all-start.4 = ((bf16[4,2,65536]{2,1,0:T(2,128)(2,1)}), bf16[4,2,65536]{2,1,0:T(2,128)(2,1)}, u32[]{:S(2)}, u32[]{:S(2)}) async-start(bf16[4,2,65536]{2,1,0:T(2,128)(2,1)} %reshape.734), calls=%async_computation.5 | async-start | bytes 2097152 | tf_op jit(solution)/shard_map/all_to_all | solution.py:131
  205.7 82.2 %all-to-all-start.6 = ((bf16[4,2,65536]{2,1,0:T(2,128)(2,1)}), bf16[4,2,65536]{2,1,0:T(2,128)(2,1)}, u32[]{:S(2)}, u32[]{:S(2)}) async-start(bf16[4,2,65536]{2,1,0:T(2,128)(2,1)} %reshape.738), calls=%async_computation.7 | async-start | bytes 2097152 | tf_op jit(solution)/shard_map/all_to_all | solution.py:128
  287.9 24.7 all-to-all-start.5
  292.2 464.3 %all-gather.36.cloned.1.call-start = ((), (), s32[]{:S(2)}) async-start(), calls=%async_computation.27 | async-start | bytes 9437184 | tf_op jit(solution)/shard_map/all_gather | solution.py:151
  473.8 34.2 %copy-start.68 = (f32[256]{0:T(256)}, f32[256]{0:T(256)S(1)}, u32[]{:S(2)}) copy-start(f32[256]{0:T(256)S(1)} %get-tuple-element.1188) | copy-start | bytes 3076
  473.8 34.2 %copy-start.70 = (f32[256]{0:T(256)}, f32[256]{0:T(256)S(1)}, u32[]{:S(2)}) copy-start(f32[256]{0:T(256)S(1)} %get-tuple-element.1189) | copy-start | bytes 3076
  503.7 36.7 %all-to-all-start = ((bf16[4,2,65536]{2,1,0:T(2,128)(2,1)}), bf16[4,2,65536]{2,1,0:T(2,128)(2,1)}, u32[]{:S(2)}, u32[]{:S(2)}) async-start(bf16[4,2,65536]{2,1,0:T(2,128)(2,1)} %reshape.742), calls=%async_computation | async-start | bytes 2097152 | tf_op jit(solution)/shard_map/all_to_all | solution.py:131
  507.9 268.4 %all-gather.40.cloned.1.call-start = ((), (), s32[]{:S(2)}) async-start(), calls=%async_computation.31 | async-start | bytes 9437184 | tf_op jit(solution)/shard_map/all_gather | solution.py:167
  540.4 33.4 %all-to-all-start.2 = ((bf16[4,2,65536]{2,1,0:T(2,128)(2,1)}), bf16[4,2,65536]{2,1,0:T(2,128)(2,1)}, u32[]{:S(2)}, u32[]{:S(2)}) async-start(bf16[4,2,65536]{2,1,0:T(2,128)(2,1)} %reshape.746), calls=%async_computation.2 | async-start | bytes 2097152 | tf_op jit(solution)/shard_map/all_to_all | solution.py:128
  573.8 24.7 all-to-all-start.1
  578.1 256.6 %all-gather.34.cloned.1.call-start = ((), (), s32[]{:S(2)}) async-start(), calls=%async_computation.25 | async-start | bytes 9437184 | tf_op jit(solution)/shard_map/all_gather | solution.py:151
  755.7 161.3 %all-gather.38.cloned.1.call-start = ((), (), s32[]{:S(2)}) async-start(), calls=%async_computation.29 | async-start | bytes 9437184 | tf_op jit(solution)/shard_map/all_gather | solution.py:167
  756.4 250.8 %reduce-scatter.11.cloned.1.call-start = ((), (), s32[]{:S(2)}) async-start(), calls=%async_computation.32 | async-start | bytes 9437184 | tf_op jit(solution)/shard_map/reduce_scatter | solution.py:171
  756.5 11.8 copy-start.87
  756.5 11.8 copy-start.91
  776.3 13.1 copy-start.89
  789.4 10.3 copy-start.98
  823.1 274.4 %reduce-scatter.9.cloned.1.call-start = ((), (), s32[]{:S(2)}) async-start(), calls=%async_computation.30 | async-start | bytes 9437184 | tf_op jit(solution)/shard_map/reduce_scatter | solution.py:171
  834.7 11.3 copy-start.88
  834.7 11.3 copy-start.93
  916.9 12.9 copy-start.90
  953.2 234.5 %reduce-scatter.7.cloned.1.call-start = ((), (), s32[]{:S(2)}) async-start(), calls=%async_computation.28 | async-start | bytes 9437184 | tf_op jit(solution)/shard_map/reduce_scatter | solution.py:155
  964.2 313.8 %reduce-scatter.5.cloned.1.call-start = ((), (), s32[]{:S(2)}) async-start(), calls=%async_computation.26 | async-start | bytes 9437184 | tf_op jit(solution)/shard_map/reduce_scatter | solution.py:155
  975.1 32.2 %copy-start.10 = (f32[256,2048]{1,0:T(8,128)S(1)}, f32[256,2048]{1,0:T(8,128)}, u32[]{:S(2)}) copy-start(f32[256,2048]{1,0:T(8,128)} %copy-done.9) | copy-start | bytes 6291460
  975.1 863.2 %all-gather.64.cloned.1.call-start = ((), (), s32[]{:S(2)}) async-start(), calls=%async_computation.44 | async-start | bytes 9437184 | tf_op jit(solution)/shard_map/all_gather | solution.py:233
  975.7 862.6 %all-gather.62.cloned.1.call-start = ((), (), s32[]{:S(2)}) async-start(), calls=%async_computation.43 | async-start | bytes 9437184 | tf_op jit(solution)/shard_map/all_gather | solution.py:238
  1008.8 269.2 %copy-start.47 = (bf16[256,2048]{1,0:T(8,128)(2,1)S(1)}, bf16[256,2048]{1,0:T(8,128)(2,1)}, u32[]{:S(2)}) copy-start(bf16[256,2048]{1,0:T(8,128)(2,1)} %reduce-scatter.11.cloned.1.call-done) | copy-start | bytes 3145732
  1008.8 269.2 %copy-start.65 = (f32[256]{0:T(256)S(1)}, f32[256]{0:T(256)}, u32[]{:S(2)}) copy-start(f32[256]{0:T(256)} %copy-done.64) | copy-start | bytes 3076
  1008.8 269.2 %copy-start.67 = (f32[256]{0:T(256)S(1)}, f32[256]{0:T(256)}, u32[]{:S(2)}) copy-start(f32[256]{0:T(256)} %copy-done.66) | copy-start | bytes 3076
  1008.8 269.2 %copy-start.69 = (f32[256]{0:T(256)S(1)}, f32[256]{0:T(256)}, u32[]{:S(2)}) copy-start(f32[256]{0:T(256)} %copy-done.68) | copy-start | bytes 3076
  1008.8 269.2 %copy-start.71 = (f32[256]{0:T(256)S(1)}, f32[256]{0:T(256)}, u32[]{:S(2)}) copy-start(f32[256]{0:T(256)} %copy-done.70) | copy-start | bytes 3076
  1008.8 269.2 %copy-start.79 = (f32[256]{0:T(256)S(1)}, f32[256]{0:T(256)}, u32[]{:S(2)}) copy-start(f32[256]{0:T(256)} %get-tuple-element.1169) | copy-start | bytes 3076
  1008.8 269.2 %copy-start.83 = (f32[256]{0:T(256)S(1)}, f32[256]{0:T(256)}, u32[]{:S(2)}) copy-start(f32[256]{0:T(256)} %get-tuple-element.1165) | copy-start | bytes 3076
  1284.4 560.1 %all-gather.44.cloned.1.call-start = ((), (), s32[]{:S(2)}) async-start(), calls=%async_computation.34 | async-start | bytes 9437184 | tf_op jit(solution)/shard_map/all_gather | solution.py:232
  1285.0 559.5 %all-gather.58.cloned.1.call-start = ((), (), s32[]{:S(2)}) async-start(), calls=%async_computation.41 | async-start | bytes 9437184 | tf_op jit(solution)/shard_map/all_gather | solution.py:237
  1295.5 556.5 %all-gather.68.cloned.1.call-start = ((), (), s32[]{:S(2)}) async-start(), calls=%async_computation.46 | async-start | bytes 9437184 | tf_op jit(solution)/shard_map/all_gather | solution.py:233
  1296.1 555.9 %all-gather.66.cloned.1.call-start = ((), (), s32[]{:S(2)}) async-start(), calls=%async_computation.45 | async-start | bytes 9437184 | tf_op jit(solution)/shard_map/all_gather | solution.py:238
  1296.9 562.2 %all-gather.48.cloned.1.call-start = ((), (), s32[]{:S(2)}) async-start(), calls=%async_computation.36 | async-start | bytes 9437184 | tf_op jit(solution)/shard_map/all_gather | solution.py:232
  1331.2 16.6 all-to-all-start.8
  1335.4 599.2 %all-gather.60.cloned.1.call-start = ((), (), s32[]{:S(2)}) async-start(), calls=%async_computation.42 | async-start | bytes 9437184 | tf_op jit(solution)/shard_map/all_gather | solution.py:237
  1344.4 672.9 %all-gather.54.cloned.1.call-start = ((), (), s32[]{:S(2)}) async-start(), calls=%async_computation.39 | async-start | bytes 9437184 | tf_op jit(solution)/shard_map/all_gather | solution.py:236
  1480.4 619.2 %all-gather.50.cloned.1.call-start = ((), (), s32[]{:S(2)}) async-start(), calls=%async_computation.37 | async-start | bytes 9437184 | tf_op jit(solution)/shard_map/all_gather | solution.py:235
  1532.6 26.7 all-to-all-start.12
  1559.3 28.8 %all-to-all-start.9 = ((bf16[4,2,65536]{2,1,0:T(2,128)(2,1)}), bf16[4,2,65536]{2,1,0:T(2,128)(2,1)}, u32[]{:S(2)}, u32[]{:S(2)}) async-start(bf16[4,2,65536]{2,1,0:T(2,128)(2,1)} %reshape.760), calls=%async_computation.12 | async-start | bytes 2097152 | tf_op jit(solution)/shard_map/all_to_all | solution.py:198
  1563.6 618.2 %all-gather.42.cloned.1.call-start = ((), (), s32[]{:S(2)}) async-start(), calls=%async_computation.33 | async-start | bytes 9437184 | tf_op jit(solution)/shard_map/all_gather | solution.py:234
  1592.4 672.3 %all-gather.56.cloned.1.call-start = ((), (), s32[]{:S(2)}) async-start(), calls=%async_computation.40 | async-start | bytes 9437184 | tf_op jit(solution)/shard_map/all_gather | solution.py:236
  1716.5 631.0 %all-gather.52.cloned.1.call-start = ((), (), s32[]{:S(2)}) async-start(), calls=%async_computation.38 | async-start | bytes 9437184 | tf_op jit(solution)/shard_map/all_gather | solution.py:235
  1771.1 15.4 all-to-all-start.13
  1774.6 655.6 %all-gather.46.cloned.1.call-start = ((), (), s32[]{:S(2)}) async-start(), calls=%async_computation.35 | async-start | bytes 9437184 | tf_op jit(solution)/shard_map/all_gather | solution.py:234
  1789.0 11.8 copy-start.101
  1789.0 912.4 %all-reduce.3.cloned.1.call-start = ((), (), s32[]{:S(2)}) async-start(), calls=%async_computation.47 | async-start | bytes 27787264 | tf_op jit(solution)/shard_map/psum | solution.py:267
  1789.1 22.1 slice-start.6
  1789.1 31.6 %slice-start.10 = ((s8[8388608]{0:T(1024)(128)(4,1)}), s8[4194304]{0:T(1024)(128)(4,1)S(1)}, s32[]{:S(2)}) async-start(s8[8388608]{0:T(1024)(128)(4,1)} %bitcast.869), calls=%async_computation.58 | async-start | bytes 8388608
  1800.8 10.3 slice-start.7
  1800.8 10.3 copy-start.97
  1800.8 19.9 slice-start.11
  1811.2 17.5 slice-start.8
  2440.3 13.3 slice-start
  (125 other events, 411.9 us)
Sparse Core Ops, SparseCore 0:
  9.6 84.7 all-gather.23
  96.0 80.5 all-gather.27
  178.2 80.5 all-gather.25
  260.3 80.5 all-gather.29
  342.4 80.5 all-gather.31
  472.0 79.0 all-gather.35
  552.8 80.5 all-gather.39
  755.8 78.8 all-gather.33
  836.3 80.5 all-gather.37
  919.1 88.1 reduce-scatter.10
  1009.6 87.9 reduce-scatter.8
  1099.7 87.9 reduce-scatter.6
  1190.0 87.9 reduce-scatter.4
  1279.4 80.3 all-gather.63
  1361.3 80.5 all-gather.61
  1443.4 80.5 all-gather.43
  1525.5 80.5 all-gather.57
  1607.5 80.5 all-gather.67
  1689.8 80.5 all-gather.65
  1771.8 80.5 all-gather.47
  1854.0 80.5 all-gather.59
  1936.3 81.0 all-gather.53
  2018.9 80.6 all-gather.49
  2101.1 80.6 all-gather.41
  2184.0 80.6 all-gather.55
  2266.7 80.6 all-gather.51
  2349.5 80.6 all-gather.45
  2437.4 264.0 all-reduce.2
where the time goes:
time: 2750 us; the launch traced here: 2730 us
  waiting for transfers between devices  1310 us (48%)
  matrix products  572 us (21%)
  local copies, waits for them, and re-layouts  410 us (15%)
  other arithmetic  278 us (10%)
  blocking collectives  94.9 us (3%)
  starting transfers between devices  43 us (2%)
    psum x1, waiting for transfers between devices, on_device(): lax.psum(shortened(accum), 'seq')  229 us
    reduce_scatter x2, waiting for transfers between devices, on_device(): lax.psum_scatter(jnp.dot(product_all, down_weight, preferred_element_type...  178 us
    unnamed x28, other arithmetic  158 us
    all_gather x2, waiting for transfers between devices, on_device(): lax.all_gather(grad_value, 'fsdp', axis=0, tiled=True)  152 us
    all_gather x2, waiting for transfers between devices, on_device(): lax.all_gather(grad_key, 'fsdp', axis=0, tiled=True)  150 us
    all_gather x2, waiting for transfers between devices, on_device(): lax.all_gather(grad_query, 'fsdp', axis=0, tiled=True)  150 us
    dot_general x16, matrix products, times_rows(): lax.dot_general(left_side, weight, (((1,), (1,)), ((), ())), preferred_el...  138 us
    dot_general x16, matrix products, rows_outer(): lax.dot_general(left_side, right_side, (((0,), (0,)), ((), ())), preferre...  132 us
  transfers between devices with their start and end apart: 38, of which 18 were waited for; matrix products, arithmetic and copies ran while one was open for 44% of the time, Pallas kernels for 0%

commit v1 on v0

v1 whole, which is shorter than its diff:
```python
import functools

import jax
import jax.numpy as jnp
from jax import lax
from jax.experimental import pallas as pl
from jax.experimental.pallas import tpu as pltpu
from jax.sharding import PartitionSpec as P

HEAD = 128
EPS = 1e-06
F32 = jnp.float32
LOW = jnp.bfloat16


def swap_seq(x, bit):
    size = lax.axis_size("seq")
    return lax.ppermute(x, "seq", [(i, i ^ bit) for i in range(size)])


def swap_core(x):
    size = lax.axis_size("fsdp")
    return lax.ppermute(x, "fsdp", [(i, i ^ 1) for i in range(size)])


def spread(units):
    size = lax.axis_size("seq")
    if size != 4:
        return [units] + [[swap_seq(u, i) for u in units] for i in range(1, size)]
    by_x = [swap_seq(u, 1) for u in units]
    by_y = [swap_seq(u, 2) for u in units]
    half = (len(units) + 1) // 2
    both = [swap_seq(u, 2) for u in by_x[:half]] + [swap_seq(u, 1) for u in by_y[half:]]
    return [units, by_x, by_y, both]


def collect(parts):
    size = lax.axis_size("seq")
    wide = lambda x: x.astype(F32)
    count = len(parts[0])
    if size != 4:
        out = []
        for b in range(count):
            total = wide(parts[0][b])
            for i in range(1, size):
                total = total + wide(swap_seq(parts[i][b].astype(LOW), i))
            out.append(total)
        return out
    half = (count + 1) // 2
    out = []
    for b in range(count):
        first, second = (1, 2) if b < half else (2, 1)
        passed = swap_seq(parts[3][b].astype(LOW), first)
        direct = swap_seq(parts[first][b].astype(LOW), first)
        joined = swap_seq((wide(parts[second][b]) + wide(passed)).astype(LOW), second)
        out.append(wide(parts[0][b]) + wide(direct) + wide(joined))
    return out


def times_rows(left_side, weight):
    return lax.dot_general(
        left_side, weight, (((1,), (1,)), ((), ())), preferred_element_type=F32
    )


def times(left_side, weight):
    return lax.dot_general(
        left_side, weight, (((1,), (0,)), ((), ())), preferred_element_type=F32
    )


def rows_outer(left_side, right_side):
    return lax.dot_general(
        left_side, right_side, (((0,), (0,)), ((), ())), preferred_element_type=F32
    )


def norm_factor(values):
    return lax.rsqrt(jnp.mean(values * values, axis=-1, keepdims=True) + EPS)


def norm_back(values, factor, grad_in):
    inner_mean = jnp.mean(grad_in * values, axis=-1, keepdims=True)
    return factor * grad_in - values * (factor * factor * factor) * inner_mean


def sigmoid(x):
    return 1.0 / (1.0 + jnp.exp(-x))


def dot_nt(a, b):
    return lax.dot_general(a, b, (((1,), (1,)), ((), ())), preferred_element_type=F32)


def dot_nn(a, b):
    return lax.dot_general(a, b, (((1,), (0,)), ((), ())), preferred_element_type=F32)


def dot_tn(a, b):
    return lax.dot_general(a, b, (((0,), (0,)), ((), ())), preferred_element_type=F32)


def decay_weights(down, across):
    count = down.shape[0]
    rows = lax.broadcasted_iota(jnp.int32, (count, count), 0)
    cols = lax.broadcasted_iota(jnp.int32, (count, count), 1)
    apart = down[:, :1] - across
    return jnp.where(rows >= cols, jnp.exp(jnp.minimum(apart, 0.0)), 0.0)


def attend_kernel(s_ref, pre_ref, down_ref, across_ref, out_ref, attn_ref, square_ref, state_ref):
    me = s_ref[0]
    head = pl.program_id(1)
    blocks = pre_ref.shape[0]
    state_ref[...] = jnp.zeros_like(state_ref)

    def step(c, carry):
        i = lax.bitwise_xor(jnp.int32(c), me)
        pre_q = pre_ref[i, 0, :, 0:HEAD].astype(F32)
        pre_k = pre_ref[i, 0, :, HEAD : 2 * HEAD].astype(F32)
        value = pre_ref[i, 0, :, 2 * HEAD : 3 * HEAD]
        gate = pre_ref[i, 0, :, 3 * HEAD : 4 * HEAD].astype(F32)
        query = (pre_q * sigmoid(pre_q)).astype(LOW)
        key = pre_k * sigmoid(pre_k)
        down = down_ref[0, c]
        across = across_ref[0, pl.ds(c, 1), :]
        weights = decay_weights(down, across)
        scores = (dot_nt(query, key.astype(LOW)) * weights).astype(LOW)
        state = state_ref[...]
        out = dot_nn(scores, value) + dot_nn(query, state.astype(LOW)) * jnp.exp(down)
        last = down[down.shape[0] - 1 :, :]
        tail = (key * jnp.exp(last - down)).astype(LOW)
        state_ref[...] = jnp.exp(last) * state + dot_tn(tail, value)
        low = out.astype(LOW)
        attn_ref[i, 0] = low
        rounded = low.astype(F32)
        out_ref[i, 0] = (rounded * gate).astype(LOW)
        before = jnp.where(head == 0, 0.0, square_ref[i, 0])
        square_ref[i, 0] = before + rounded * rounded
        return carry

    lax.fori_loop(0, blocks, step, 0)


def attend_back_kernel(
    s_ref,
    pre_ref,
    attn_ref,
    grad_ref,
    factor_ref,
    inner_ref,
    down_ref,
    across_ref,
    out_ref,
    gated_ref,
    states_ref,
    state_ref,
):
    me = s_ref[0]
    blocks = pre_ref.shape[0]
    state_ref[...] = jnp.zeros_like(state_ref)

    def forward(c, carry):
        i = lax.bitwise_xor(jnp.int32(c), me)
        pre_k = pre_ref[i, 0, :, HEAD : 2 * HEAD].astype(F32)
        value = pre_ref[i, 0, :, 2 * HEAD : 3 * HEAD]
        key = pre_k * sigmoid(pre_k)
        down = down_ref[0, c]
        last = down[down.shape[0] - 1 :, :]
        tail = (key * jnp.exp(last - down)).astype(LOW)
        state = state_ref[...]
        states_ref[c] = state.astype(LOW)
        state_ref[...] = jnp.exp(last) * state + dot_tn(tail, value)
        return carry

    lax.fori_loop(0, blocks, forward, 0)
    state_ref[...] = jnp.zeros_like(state_ref)

    def backward(n, carry):
        c = blocks - 1 - n
        i = lax.bitwise_xor(jnp.int32(c), me)
        pre_q = pre_ref[i, 0, :, 0:HEAD].astype(F32)
        pre_k = pre_ref[i, 0, :, HEAD : 2 * HEAD].astype(F32)
        value = pre_ref[i, 0, :, 2 * HEAD : 3 * HEAD]
        gate = pre_ref[i, 0, :, 3 * HEAD : 4 * HEAD].astype(F32)
        attn = attn_ref[i, 0].astype(F32)
        grad = grad_ref[i, 0].astype(F32)
        factor = factor_ref[i, 0]
        scaled = attn * factor
        gated_ref[i, 0] = (scaled * gate).astype(LOW)
        grad_gate = grad * scaled
        grad_attn = (factor * (grad * gate) - attn * inner_ref[i, 0]).astype(LOW)
        sig_q = sigmoid(pre_q)
        sig_k = sigmoid(pre_k)
        query = pre_q * sig_q
        key = pre_k * sig_k
        query_low = query.astype(LOW)
        key_low = key.astype(LOW)
        down = down_ref[0, c]
        across = across_ref[0, pl.ds(c, 1), :]
        last = down[down.shape[0] - 1 :, :]
        weights = decay_weights(down, across)
        scores = (dot_nt(query_low, key_low) * weights).astype(LOW)
        paired = (dot_nt(grad_attn, value) * weights).astype(LOW)
        tail = jnp.exp(last - down)
        later = state_ref[...]
        later_low = later.astype(LOW)
        grown = jnp.exp(down)
        grad_q = dot_nn(paired, key_low) + grown * dot_nt(grad_attn, states_ref[c])
        grad_k = dot_tn(paired, query_low) + tail * dot_nt(value, later_low)
        grad_v = dot_tn(scores, grad_attn) + tail * dot_nn(key_low, later_low)
        state_ref[...] = jnp.exp(last) * later + dot_tn((query * grown).astype(LOW), grad_attn)
        out_ref[i, 0, :, 0:HEAD] = (grad_q * (sig_q * (1.0 + pre_q * (1.0 - sig_q)))).astype(LOW)
        out_ref[i, 0, :, HEAD : 2 * HEAD] = (
            grad_k * (sig_k * (1.0 + pre_k * (1.0 - sig_k)))
        ).astype(LOW)
        out_ref[i, 0, :, 2 * HEAD : 3 * HEAD] = grad_v.astype(LOW)
        out_ref[i, 0, :, 3 * HEAD : 4 * HEAD] = grad_gate.astype(LOW)
        return carry

    lax.fori_loop(0, blocks, backward, 0)


def attend(me, pre, down, across):
    blocks, seqs, slots, width = pre.shape
    heads = width // (4 * HEAD)
    one = pl.BlockSpec((blocks, 1, slots, HEAD), lambda b, h, s: (0, b, 0, h))
    return pl.pallas_call(
        attend_kernel,
        grid_spec=pltpu.PrefetchScalarGridSpec(
            num_scalar_prefetch=1,
            grid=(seqs, heads),
            in_specs=[
                pl.BlockSpec((blocks, 1, slots, 4 * HEAD), lambda b, h, s: (0, b, 0, h)),
                pl.BlockSpec((1, blocks, slots, HEAD), lambda b, h, s: (h, 0, 0, 0)),
                pl.BlockSpec((1, blocks, slots), lambda b, h, s: (h, 0, 0)),
            ],
            out_specs=[
                one,
                one,
                pl.BlockSpec((blocks, 1, slots, HEAD), lambda b, h, s: (0, b, 0, 0)),
            ],
            scratch_shapes=[pltpu.VMEM((HEAD, HEAD), F32)],
        ),
        out_shape=[
            jax.ShapeDtypeStruct((blocks, seqs, slots, heads * HEAD), LOW),
            jax.ShapeDtypeStruct((blocks, seqs, slots, heads * HEAD), LOW),
            jax.ShapeDtypeStruct((blocks, seqs, slots, HEAD), F32),
        ],
        compiler_params=pltpu.CompilerParams(
            dimension_semantics=("arbitrary", "arbitrary"), vmem_limit_bytes=32 << 20
        ),
        cost_estimate=pl.CostEstimate(
            flops=2_500_000_000, bytes_accessed=16 << 20, transcendentals=4_000_000
        ),
        name="attend",
    )(me, pre, down, across)


def attend_back(me, pre, attn, grad, factor, inner, down, across):
    blocks, seqs, slots, width = pre.shape
    heads = width // (4 * HEAD)
    one = pl.BlockSpec((blocks, 1, slots, HEAD), lambda b, h, s: (0, b, 0, h))
    four = pl.BlockSpec((blocks, 1, slots, 4 * HEAD), lambda b, h, s: (0, b, 0, h))
    same = pl.BlockSpec((blocks, 1, slots, HEAD), lambda b, h, s: (0, b, 0, 0))
    return pl.pallas_call(
        attend_back_kernel,
        grid_spec=pltpu.PrefetchScalarGridSpec(
            num_scalar_prefetch=1,
            grid=(seqs, heads),
            in_specs=[
                four,
                one,
                one,
                same,
                same,
                pl.BlockSpec((1, blocks, slots, HEAD), lambda b, h, s: (h, 0, 0, 0)),
                pl.BlockSpec((1, blocks, slots), lambda b, h, s: (h, 0, 0)),
            ],
            out_specs=[four, one],
            scratch_shapes=[
                pltpu.VMEM((blocks, HEAD, HEAD), LOW),
                pltpu.VMEM((HEAD, HEAD), F32),
            ],
        ),
        out_shape=[
            jax.ShapeDtypeStruct((blocks, seqs, slots, width), LOW),
            jax.ShapeDtypeStruct((blocks, seqs, slots, heads * HEAD), LOW),
        ],
        compiler_params=pltpu.CompilerParams(
            dimension_semantics=("arbitrary", "arbitrary"), vmem_limit_bytes=40 << 20
        ),
        cost_estimate=pl.CostEstimate(
            flops=8_000_000_000, bytes_accessed=32 << 20, transcendentals=8_000_000
        ),
        name="attend_back",
    )(me, pre, attn, grad, factor, inner, down, across)


def paired_heads(rows):
    return rows % HEAD == 0 and 2 * rows // HEAD == lax.axis_size("seq") == 4


def gather_projections(weights, me_seq, me_fsdp):
    rows, feat = weights[0].shape
    size = lax.axis_size("seq")
    if not paired_heads(rows):
        picked = []
        for weight in weights:
            full = lax.all_gather(weight, "fsdp", axis=0, tiled=True)
            full = full.reshape(-1, size, HEAD, feat)
            picked.append(lax.dynamic_index_in_dim(full, me_seq, 1, keepdims=False))
        return jnp.stack(picked, 1).reshape(-1, feat)
    core = me_fsdp % 2
    own = [
        lax.dynamic_slice_in_dim(weight, (me_seq % 2) * HEAD, HEAD, 0) for weight in weights
    ]
    first = jnp.concatenate(own[:2], 0)
    second = jnp.concatenate(own[2:], 0)
    keep = jnp.where(core == 0, first, second)
    give = jnp.where(core == 0, second, first)
    got = swap_core(give)
    return lax.all_gather(
        jnp.where(core == me_seq // 2, keep, got), "fsdp", axis=0, tiled=True
    )


def scatter_projections(grad, rows, me_seq, me_fsdp):
    feat = grad.shape[1]
    size = lax.axis_size("seq")
    if not paired_heads(rows):
        parts = grad.reshape(-1, 1, 4, HEAD, feat)
        result = []
        for which in range(4):
            full = jnp.zeros((parts.shape[0], size, HEAD, feat), grad.dtype)
            full = lax.dynamic_update_slice_in_dim(full, parts[:, :, which], me_seq, 1)
            part = lax.psum_scatter(
                full.reshape(-1, feat), "fsdp", scatter_dimension=0, tiled=True
            )
            result.append(lax.psum(part, "seq").astype(F32))
        return result
    core = me_fsdp % 2
    mine = lax.psum_scatter(grad, "fsdp", scatter_dimension=0, tiled=True)
    pieces = spread([mine[:HEAD], mine[HEAD:]])
    pieces = [jnp.concatenate(p, 0) for p in pieces]
    straight = (core ^ (me_seq // 2)) == 0
    keep = [jnp.where(straight, pieces[j], pieces[2 + j]) for j in range(2)]
    give = [jnp.where(straight, pieces[2 + j], pieces[j]) for j in range(2)]
    got = [swap_core(g) for g in give]
    even = me_seq % 2 == 0
    keep = [jnp.where(even, keep[0], keep[1]), jnp.where(even, keep[1], keep[0])]
    got = [jnp.where(even, got[0], got[1]), jnp.where(even, got[1], got[0])]
    first = [jnp.where(core == 0, k, g) for k, g in zip(keep, got)]
    second = [jnp.where(core == 0, g, k) for k, g in zip(keep, got)]
    result = []
    for pair in (first, second):
        for part in range(2):
            span = slice(part * HEAD, (part + 1) * HEAD)
            result.append(jnp.concatenate([p[span] for p in pair], 0).astype(F32))
    return result


def in_order(pieces, me_seq):
    size = len(pieces)
    stack = jnp.stack(pieces)
    bit = 1
    index = lax.iota(jnp.int32, size)
    while bit < size:
        turned = jnp.stack([stack[i ^ bit] for i in range(size)])
        stack = jnp.where((me_seq & bit) != 0, turned, stack)
        bit *= 2
    return [stack[i] for i in range(size)]


def place_rows(units_by_piece, me_seq):
    rows = sum(u.shape[0] for u in units_by_piece[0])
    feat = units_by_piece[0][0].shape[1]
    out = jnp.zeros((rows * len(units_by_piece), feat), F32)
    for i, units in enumerate(units_by_piece):
        start = (me_seq ^ i) * rows
        for unit in units:
            out = lax.dynamic_update_slice_in_dim(out, unit.astype(F32), start, 0)
            start = start + unit.shape[0]
    return out


def halves(x):
    cut = max(16, x.shape[0] // 32 * 16)
    return [x[:cut], x[cut:]]


def on_device(
    tokens,
    cotangent,
    lengths,
    decay,
    query_weight,
    key_weight,
    value_weight,
    outgate_weight,
    output_weight,
    left_weight,
    right_weight,
    down_weight,
):
    seqs, slots, feat = tokens.shape
    size = lax.axis_size("seq")
    me_seq = lax.axis_index("seq")
    me_fsdp = lax.axis_index("fsdp")
    rows_all = size * seqs * slots
    span = range(seqs)

    def whole(pieces):
        return jnp.concatenate([u for units in pieces for u in units], 0)

    def cut(rows):
        return [rows[b * slots : (b + 1) * slots] for b in span]

    wide = [tokens[b].astype(F32) for b in span]
    factor_in = [norm_factor(w) for w in wide]
    normed = [(w * r).astype(LOW) for w, r in zip(wide, factor_in)]

    project = gather_projections(
        (query_weight, key_weight, value_weight, outgate_weight), me_seq, me_fsdp
    )
    out_rows = output_weight.shape[0]
    out_own = lax.dynamic_index_in_dim(
        output_weight.reshape(out_rows, -1, size, HEAD), me_seq, 2, keepdims=False
    ).reshape(out_rows, -1)
    out_slice = lax.all_gather(out_own, "fsdp", axis=0, tiled=True)
    own_units = left_weight.shape[0] // size
    hidden = lambda weight: lax.dynamic_slice_in_dim(weight, me_seq * own_units, own_units, 0)
    sides = lax.all_gather(
        jnp.concatenate([hidden(left_weight), hidden(right_weight)], 1), "fsdp", axis=0, tiled=True
    )
    left_slice, right_slice = sides[:, :feat], sides[:, feat:]
    down_slice = lax.all_gather(hidden(down_weight), "fsdp", axis=0, tiled=True)

    normed_all = whole(spread(normed))

    positions = me_seq * slots + lax.iota(jnp.int32, slots)
    valid = [(positions < lengths[b]).astype(F32)[:, None] for b in span]
    grad_y = [v * cotangent[b].astype(F32) for b, v in zip(span, valid)]
    grad_all = whole(spread([g.astype(LOW) for g in grad_y]))

    heads = decay.shape[0]
    all_decay = lax.all_gather(decay, "seq", axis=0, tiled=True).reshape(heads, size, -1)
    own_decay = lax.dynamic_index_in_dim(all_decay, me_seq, 1, keepdims=False)
    across = jnp.cumsum(own_decay.reshape(heads, size, slots), axis=-1)
    down = jnp.broadcast_to(across[..., None], (heads, size, slots, HEAD))
    me = me_seq.astype(jnp.int32).reshape(1)

    pre = times_rows(normed_all, project).astype(LOW).reshape(size, seqs, slots, -1)
    ungated, attn, squares = attend(me, pre, down, across)

    branch_parts = [
        cut(times_rows(ungated[i].reshape(seqs * slots, -1), out_slice).astype(LOW))
        for i in range(size)
    ]
    branch_raw = collect(branch_parts)
    square = jnp.sum(squares, axis=-1)
    square_own = square[0]
    for i in range(1, size):
        square_own = square_own + swap_seq(square[i], i)
    factor_attn = lax.rsqrt(square_own / feat + EPS)
    residual = [w + b * factor_attn[n][:, None] for n, (w, b) in enumerate(zip(wide, branch_raw))]
    factor_resid = [norm_factor(r) for r in residual]
    resid_low = [(r * f).astype(LOW) for r, f in zip(residual, factor_resid)]
    resid_all = whole(spread(resid_low))

    grad_product = times_rows(grad_all, down_slice)
    left = times_rows(resid_all, left_slice)
    right = times_rows(resid_all, right_slice)
    product = (left * right).astype(LOW)
    grad_left = (grad_product * right).astype(LOW)
    grad_right = (grad_product * left).astype(LOW)
    count = seqs * slots
    piece = lambda rows, i: rows[i * count : (i + 1) * count]
    grad_hn = collect(
        [
            cut(
                (
                    times(piece(grad_left, i), left_slice)
                    + times(piece(grad_right, i), right_slice)
                ).astype(LOW)
            )
            for i in range(size)
        ]
    )
    ffn = collect(
        [cut(times(piece(product, i), down_slice).astype(LOW)) for i in range(size)]
    )
    layer_out = jnp.stack(
        [(v * (r + f)).astype(LOW) for v, r, f in zip(valid, residual, ffn)]
    )

    down_grad = rows_outer(product, grad_all).astype(LOW)
    left_grad = rows_outer(grad_left, resid_all).astype(LOW)
    right_grad = rows_outer(grad_right, resid_all).astype(LOW)

    def share(grad):
        own = lax.psum_scatter(grad, "fsdp", scatter_dimension=0, tiled=True)
        return place_rows(spread(halves(own)), me_seq)

    down_out = share(down_grad)
    left_out = share(left_grad)
    right_out = share(right_grad)

    grad_resid = [
        g + norm_back(r, f, h) for g, r, f, h in zip(grad_y, residual, factor_resid, grad_hn)
    ]
    grad_branch = [g.astype(LOW) for g in grad_resid]
    branch_all = whole(spread(grad_branch))
    inner = jnp.stack(
        [jnp.mean(g.astype(F32) * b, axis=-1) for g, b in zip(grad_branch, branch_raw)]
    )
    scalars = jnp.stack([factor_attn, (factor_attn * inner) * factor_attn * factor_attn])
    scalars = jnp.stack([scalars] + [swap_seq(scalars, i) for i in range(1, size)])
    shape_scalars = (size, seqs, slots, HEAD)
    factor_cols = jnp.broadcast_to(scalars[:, 0, :, :, None], shape_scalars)
    inner_cols = jnp.broadcast_to(scalars[:, 1, :, :, None], shape_scalars)
    grad_gated = times(branch_all, out_slice).reshape(size, seqs, slots, -1)
    grad_pre, gated = attend_back(
        me, pre, attn, grad_gated, factor_cols, inner_cols, down, across
    )
    grad_pre_rows = grad_pre.reshape(rows_all, -1)
    grad_normed = collect(
        [cut(times(piece(grad_pre_rows, i), project).astype(LOW)) for i in range(size)]
    )
    input_grad = jnp.stack(
        [
            (g + norm_back(w, r, n)).astype(LOW)
            for g, w, r, n in zip(grad_resid, wide, factor_in, grad_normed)
        ]
    )
    project_grad = rows_outer(grad_pre_rows, normed_all).astype(LOW)
    out_grad = rows_outer(branch_all, gated.reshape(rows_all, -1)).astype(LOW)
    query_out, key_out, value_out, outgate_out = scatter_projections(
        project_grad, query_weight.shape[0], me_seq, me_fsdp
    )
    out_mine = lax.psum_scatter(out_grad, "fsdp", scatter_dimension=0, tiled=True)
    out_pieces = [jnp.concatenate(u, 0) for u in spread(halves(out_mine))]
    out_cols = in_order(out_pieces, me_seq)
    out_out = jnp.concatenate(
        [
            part[:, h * HEAD : (h + 1) * HEAD]
            for h in range(out_own.shape[1] // HEAD)
            for part in out_cols
        ],
        1,
    ).astype(F32)
    return (
        layer_out,
        input_grad,
        query_out,
        key_out,
        value_out,
        outgate_out,
        out_out,
        left_out,
        right_out,
        down_out,
    )


def solution(mesh):
    placed = (
        P("fsdp", "seq", None),
        P("fsdp", "seq", None),
        P("fsdp"),
        P("seq", None),
    ) + (P("fsdp", None),) * 8
    return jax.shard_map(
        on_device,
        mesh=mesh,
        in_specs=placed,
        out_specs=(P("fsdp", "seq", None),) * 2 + (P("fsdp", None),) * 8,
        check_vma=False,
    )
```

time: 2750 us -> 1120 us (0.41)
  waiting for transfers between devices: 1310 us -> 437 us
  local copies, waits for them, and re-layouts: 410 us -> 82.6 us
  matrix products: 572 us -> 284 us
  other arithmetic: 278 us -> 103 us
  starting transfers between devices: 43 us -> 87.1 us
  Pallas kernels: 0 us -> 43.5 us
  blocking collectives: 94.9 us -> 62.3 us
    all_gather x23 -> x4, waiting for transfers between devices: 773 us -> 0.01 us  [the longest x1 0.01 us: gather_projections(): lax.all_gather(jnp.where(core == me_seq // 2, keep, got), 'fsdp', axis=0,...]
    ppermute x0 -> x87, waiting for transfers between devices: none -> 370 us  [the longest x84 367 us: swap_seq(): return lax.ppermute(x, 'seq', [(i, i ^ bit) for i in range(size)])]
    reduce_scatter x4 -> x5, waiting for transfers between devices: 298 us -> 66.4 us  [the longest x3 42.2 us: share(): own = lax.psum_scatter(grad, 'fsdp', scatter_dimension=0, tiled=True)]
    psum x1 -> x0, waiting for transfers between devices: 229 us -> none  [on_device(): lax.psum(shortened(accum), 'seq')]
    dot_general x128 -> x17, matrix products: 302 us -> 111 us  [times(): lax.dot_general(left_side, weight, (((1,), (0,)), ((), ())), preferred_el...]
    unnamed x28 -> x11, other arithmetic: 158 us -> 11.8 us
    all_to_all x6 -> x0, blocking collectives: 94.9 us -> none  [the longest x2 37.1 us: on_device(): lax.all_to_all(attn_heads, 'seq', split_axis=1, concat_axis=2, tiled=True)]
    unnamed x255 -> x189, local copies, waits for them, and re-layouts: 124 us -> 34.4 us
  transfers between devices with their start and end apart: 38 -> 96, of which waited for: 18 -> 41; matrix products, arithmetic and copies ran while one was open for 44% -> 36% of each run, Pallas kernels for 0% -> 1%
where the time goes in v1:
time: 1120 us
  waiting for transfers between devices  437 us (39%)
  matrix products  284 us (25%)
  other arithmetic  103 us (9%)
  starting transfers between devices  87.1 us (8%)
  local copies, waits for them, and re-layouts  82.6 us (7%)
  blocking collectives  62.3 us (6%)
  Pallas kernels  43.5 us (4%)
  between operations  15.8 us (1%)
    ppermute x84, waiting for transfers between devices, swap_seq(): return lax.ppermute(x, 'seq', [(i, i ^ bit) for i in range(size)])  367 us
    dot_general x17, matrix products, times(): lax.dot_general(left_side, weight, (((1,), (0,)), ((), ())), preferred_el...  111 us
    dot_general x8, matrix products, times_rows(): lax.dot_general(left_side, weight, (((1,), (1,)), ((), ())), preferred_el...  91.6 us
    ppermute x84, starting transfers between devices, swap_seq(): return lax.ppermute(x, 'seq', [(i, i ^ bit) for i in range(size)])  85.7 us
    dot_general x5, matrix products, rows_outer(): lax.dot_general(left_side, right_side, (((0,), (0,)), ((), ())), preferre...  81.1 us
    all_gather x1, blocking collectives, on_device(): lax.all_gather(decay, 'seq', axis=0, tiled=True).reshape(heads, size, -1)  62.3 us
    reduce_scatter x3, waiting for transfers between devices, share(): own = lax.psum_scatter(grad, 'fsdp', scatter_dimension=0, tiled=True)  42.2 us
    unnamed x189, local copies, waits for them, and re-layouts  34.4 us
  transfers between devices with their start and end apart: 96, of which 41 were waited for; matrix products, arithmetic and copies ran while one was open for 36% of the time, Pallas kernels for 1%

profile of v1, /device:TPU:0, one launch (start us, length us, event | category | flops | bytes accessed | tf_op | source)
XLA Modules:
  0.0 1115.1 jit_solution(9593000027938850867)
XLA Ops:
  43.3 62.3 %all-gather = f32[4,4,1024]{2,1,0:T(4,128)S(1)} all-gather(f32[1,4,1024]{2,1,0:T(4,128)S(1)} %bitcast.178), channel_id=1, replica_groups=mesh['seq'=4,'fsdp'=8] {'seq'}, dimensions={0}, use_global_device_ids=true | all-gather | bytes 81920 | tf_op jit(solution)/shard_map/all_gather | solution.py:447
  105.6 5.0 reduce-window.6
  122.6 12.7 %collective-permute-done.4 = bf16[256,2048]{1,0:T(8,128)(2,1)} collective-permute-done((bf16[256,2048]{1,0:T(8,128)(2,1)}, bf16[256,2048]{1,0:T(8,128)(2,1)}, u32[]{:S(2)}, u32[]{:S(2)}) %collective-permute-start.4) | collective-permute-done | bytes 1048608 | tf_op jit(solution)/shard_map/ppermute | solution.py:18
  138.7 22.3 %convolution_convert_fusion.1 = bf16[2048,2048]{1,0:T(8,128)(2,1)S(1)} fusion(bf16[2048,2048]{1,0:T(8,128)(2,1)} %constant_dynamic-update-slice_fusion, bf16[2048,2048]{1,0:T(8,128)(2,1)} %all-gather.6.cloned.1.call-done), kind=kOutput, calls=%fused_computation.4 | convolution fusion | flops 17184063488 | bytes 25165824 | tf_op jit(solution)/shard_map/dot_general | solution.py:61
  161.7 14.2 %attend.1 = (bf16[4,2,256,512]{3,2,1,0:T(8,128)(2,1)S(1)}, bf16[4,2,256,512]{3,2,1,0:T(8,128)(2,1)S(1)}, f32[4,2,256,128]{3,2,1,0:T(8,128)S(1)}) custom-call(s32[1]{0:T(128)} %bitcast.2.s_ref, bf16[4,2,256,2048]{3,2,1,0:T(8,128)(2,1)S(1)} %bitcast.153, f32[4,4,256,128]{3,2,1,0:T(8,128)S(1)} %broadcast_in_dim.10.down_ref, ...), custom_call_target="tpu_custom_call" | custom-call | flops 2500000000 | bytes 16777216 | tf_op jit(solution)/shard_map/attend/pallas_call | solution.py:228
  196.5 13.8 %collective-permute-done.14 = bf16[256,2048]{1,0:T(8,128)(2,1)} collective-permute-done((bf16[256,2048]{1,0:T(8,128)(2,1)}, bf16[256,2048]{1,0:T(8,128)(2,1)}, u32[]{:S(2)}, u32[]{:S(2)}) %collective-permute-start.14) | collective-permute-done | bytes 1048608 | tf_op jit(solution)/shard_map/ppermute | solution.py:18
  220.1 12.6 %collective-permute-done.11 = f32[2,256]{1,0:T(2,128)S(1)} collective-permute-done((f32[2,256]{1,0:T(2,128)S(1)}, f32[2,256]{1,0:T(2,128)S(1)}, u32[]{:S(2)}, u32[]{:S(2)}) %collective-permute-start.11) | collective-permute-done | bytes 2080 | tf_op jit(solution)/shard_map/ppermute | solution.py:18
  242.2 13.1 %collective-permute-done.13 = bf16[256,2048]{1,0:T(8,128)(2,1)} collective-permute-done((bf16[256,2048]{1,0:T(8,128)(2,1)}, bf16[256,2048]{1,0:T(8,128)(2,1)}, u32[]{:S(2)}, u32[]{:S(2)}) %collective-permute-start.13) | collective-permute-done | bytes 1048608 | tf_op jit(solution)/shard_map/ppermute | solution.py:18
  257.3 11.1 collective-permute-done.15
  269.0 8.7 collective-permute-done.9
  285.7 5.1 collective-permute-done.29
  292.3 7.8 collective-permute-done.30
  301.6 21.0 %collective-permute-done.32 = bf16[256,2048]{1,0:T(8,128)(2,1)S(1)} collective-permute-done((bf16[256,2048]{1,0:T(8,128)(2,1)}, bf16[256,2048]{1,0:T(8,128)(2,1)S(1)}, u32[]{:S(2)}, u32[]{:S(2)}) %collective-permute-start.32) | collective-permute-done | bytes 1048608 | tf_op jit(solution)/shard_map/ppermute | solution.py:18
  326.5 9.3 collective-permute-done.16
  337.3 7.8 collective-permute-done.19
  346.6 11.6 %collective-permute-done.17 = bf16[256,2048]{1,0:T(8,128)(2,1)S(1)} collective-permute-done((bf16[256,2048]{1,0:T(8,128)(2,1)S(1)}, bf16[256,2048]{1,0:T(8,128)(2,1)S(1)}, u32[]{:S(2)}, u32[]{:S(2)}) %collective-permute-start.17) | collective-permute-done | bytes 1048608 | tf_op jit(solution)/shard_map/ppermute | solution.py:18
  359.3 8.3 collective-permute-done.18
  369.7 17.3 %collective-permute-done.20 = bf16[256,2048]{1,0:T(8,128)(2,1)S(1)} collective-permute-done((bf16[256,2048]{1,0:T(8,128)(2,1)S(1)}, bf16[256,2048]{1,0:T(8,128)(2,1)S(1)}, u32[]{:S(2)}, u32[]{:S(2)}) %collective-permute-start.20) | collective-permute-done | bytes 1048608 | tf_op jit(solution)/shard_map/ppermute | solution.py:18
  389.1 18.9 %fusion.18 = f32[2048,1408]{1,0:T(8,128)} fusion(bf16[2048,2048]{1,0:T(8,128)(2,1)} %constant_dynamic-update-slice_fusion.8, bf16[1408,4096]{1,0:T(8,128)(2,1)} %all-gather.10.cloned.1.call-done), kind=kOutput, calls=%fused_computation.40 | convolution fusion | flops 11811160064 | bytes 25690112 | tf_op jit(solution)/shard_map/dot_general | solution.py:61
  408.0 17.0 %fusion.8 = f32[2048,1408]{1,0:T(8,128)} fusion(bf16[2048,2048]{1,0:T(8,128)(2,1)} %constant_dynamic-update-slice_fusion.8, bf16[1408,4096]{1,0:T(8,128)(2,1)S(1)} %copy-done.61), kind=kOutput, calls=%fused_computation.30 | convolution fusion | flops 11811160064 | bytes 25690112 | tf_op jit(solution)/shard_map/dot_general | solution.py:61
  425.0 24.8 %multiply_convert_fusion.1 = (bf16[2048,1408]{1,0:T(8,128)(2,1)}, bf16[2048,1408]{1,0:T(8,128)(2,1)}, bf16[2048,1408]{1,0:T(8,128)(2,1)}) fusion(f32[2048,1408]{1,0:T(8,128)} %fusion.8, f32[2048,1408]{1,0:T(8,128)} %fusion.18, bf16[2048,2048]{1,0:T(8,128)(2,1)} %constant_dynamic-update-slice_fusion.16, bf16[1408,2048]{1,0:T(8,128)(2,1)} %all-gather.12.cloned.1.call-done), kind=kOutput, calls=%fused_computation.1 | convolution fusion | flops 11828461568 | bytes 54525952 | tf_op jit(solution)/shard_map/dot_general | solution.py:61
  449.8 6.5 convolution_convert_fusion.14
  458.6 5.9 fusion
  464.5 6.6 add_convert_fusion
  471.7 6.4 fusion.4
  478.0 6.6 add_convert_fusion.2
  486.8 5.1 convolution_convert_fusion.15
  491.9 5.9 fusion.2
  497.8 6.6 add_convert_fusion.1
  504.3 5.5 convolution_convert_fusion.16
  510.1 8.5 fusion.6
  523.4 10.0 collective-permute-done.35
  535.8 8.8 collective-permute-done.37
  546.1 9.7 collective-permute-done.22
  557.3 5.1 convolution_convert_fusion.17
  562.4 7.8 add_convert_fusion.3
  570.3 19.3 %collective-permute-done.24 = bf16[256,2048]{1,0:T(8,128)(2,1)S(1)} collective-permute-done((bf16[256,2048]{1,0:T(8,128)(2,1)S(1)}, bf16[256,2048]{1,0:T(8,128)(2,1)S(1)}, u32[]{:S(2)}, u32[]{:S(2)}) %collective-permute-start.24) | collective-permute-done | bytes 1048608 | tf_op jit(solution)/shard_map/ppermute | solution.py:18
  589.6 6.3 collective-permute-done.39
  595.9 10.7 collective-permute-done.36
  610.4 6.0 multiply_reduce_fusion.1
  622.3 20.4 %collective-permute-done.46 = f32[2,2,256]{2,1,0:T(2,128)S(1)} collective-permute-done((f32[2,2,256]{2,1,0:T(2,128)S(1)}, f32[2,2,256]{2,1,0:T(2,128)S(1)}, u32[]{:S(2)}, u32[]{:S(2)}) %collective-permute-start.46) | collective-permute-done | bytes 4128 | tf_op jit(solution)/shard_map/ppermute | solution.py:18
  645.8 16.7 %collective-permute-done.48 = f32[2,2,256]{2,1,0:T(2,128)S(1)} collective-permute-done((f32[2,2,256]{2,1,0:T(2,128)S(1)}, f32[2,2,256]{2,1,0:T(2,128)S(1)}, u32[]{:S(2)}, u32[]{:S(2)}) %collective-permute-start.48) | collective-permute-done | bytes 4128 | tf_op jit(solution)/shard_map/ppermute | solution.py:18
  665.0 17.7 %collective-permute-done.44 = bf16[256,2048]{1,0:T(8,128)(2,1)S(1)} collective-permute-done((bf16[256,2048]{1,0:T(8,128)(2,1)S(1)}, bf16[256,2048]{1,0:T(8,128)(2,1)S(1)}, u32[]{:S(2)}, u32[]{:S(2)}) %collective-permute-start.44) | collective-permute-done | bytes 1048608 | tf_op jit(solution)/shard_map/ppermute | solution.py:18
  682.9 4.8 fusion.91
  688.5 29.3 %attend_back.1 = (bf16[4,2,256,2048]{3,2,1,0:T(8,128)(2,1)}, bf16[4,2,256,512]{3,2,1,0:T(8,128)(2,1)S(1)}) custom-call(s32[1]{0:T(128)} %bitcast.2.s_ref, bf16[4,2,256,2048]{3,2,1,0:T(8,128)(2,1)} %bitcast.154, bf16[4,2,256,512]{3,2,1,0:T(8,128)(2,1)S(1)} %copy-done.7, f32[4,2,256,512]{3,2,1,0:T(8,128)S(1)} %bitcast.155, ...), custom_call_target="tpu_custom_call" | custom-call | flops 8000000000 | bytes 33554432 | tf_op jit(solution)/shard_map/attend_back/pallas_call | solution.py:266
  717.8 5.7 convolution_convert_fusion.5
  723.6 18.1 %convolution_convert_fusion.2 = bf16[1408,2048]{1,0:T(8,128)(2,1)} fusion(bf16[2048,1408]{1,0:T(8,128)(2,1)} %get-tuple-element.52, bf16[2048,2048]{1,0:T(8,128)(2,1)} %constant_dynamic-update-slice_fusion.16), kind=kOutput, calls=%fused_computation.5 | convolution fusion | flops 11814043648 | bytes 19922944 | tf_op jit(solution)/shard_map/dot_general | solution.py:73
  741.8 18.0 %convolution_convert_fusion.3 = bf16[1408,2048]{1,0:T(8,128)(2,1)} fusion(bf16[2048,1408]{1,0:T(8,128)(2,1)} %get-tuple-element.53, bf16[2048,2048]{1,0:T(8,128)(2,1)} %constant_dynamic-update-slice_fusion.8), kind=kOutput, calls=%fused_computation.6 | convolution fusion | flops 11814043648 | bytes 19922944 | tf_op jit(solution)/shard_map/dot_general | solution.py:73
  759.9 18.3 %convolution_convert_fusion.4 = bf16[1408,2048]{1,0:T(8,128)(2,1)} fusion(bf16[2048,1408]{1,0:T(8,128)(2,1)} %get-tuple-element.51, bf16[2048,2048]{1,0:T(8,128)(2,1)} %constant_dynamic-update-slice_fusion.8), kind=kOutput, calls=%fused_computation.7 | convolution fusion | flops 11814043648 | bytes 19922944 | tf_op jit(solution)/shard_map/dot_general | solution.py:73
  781.3 5.4 fusion.76
  786.7 8.4 convolution_convert_fusion.6
  805.3 20.9 %convolution_convert_fusion = bf16[2048,2048]{1,0:T(8,128)(2,1)} fusion(bf16[2048,2048]{1,0:T(8,128)(2,1)S(1)} %bitcast.159, bf16[2048,2048]{1,0:T(8,128)(2,1)S(1)} %bitcast.175), kind=kOutput, calls=%fused_computation.3 | convolution fusion | flops 17184063488 | bytes 25165824 | tf_op jit(solution)/shard_map/dot_general | solution.py:73
  826.1 8.5 convolution_convert_fusion.7
  840.8 11.3 %collective-permute-done.50 = bf16[256,2048]{1,0:T(8,128)(2,1)} collective-permute-done((bf16[256,2048]{1,0:T(8,128)(2,1)}, bf16[256,2048]{1,0:T(8,128)(2,1)}, u32[]{:S(2)}, u32[]{:S(2)}) %collective-permute-start.50) | collective-permute-done | bytes 1048608 | tf_op jit(solution)/shard_map/ppermute | solution.py:18
  855.6 8.4 convolution_convert_fusion.9
  867.5 10.9 collective-permute-done.51
  915.2 42.2 %reduce-scatter.10.cloned.1.call-done = bf16[176,2048]{1,0:T(8,128)(2,1)} async-done(((bf16[1408,2048]{1,0:T(8,128)(2,1)}), bf16[176,2048]{1,0:T(8,128)(2,1)}) %reduce-scatter.10.cloned.1.call-update) | async-done | bytes 720912 | tf_op jit(solution)/shard_map/reduce_scatter | solution.py:502
  1008.5 7.2 collective-permute-done.72
  1016.7 6.0 collective-permute-done.85
  1023.6 24.1 %reduce-scatter.6.cloned.1.call-done = bf16[256,2048]{1,0:T(8,128)(2,1)} async-done(((bf16[2048,2048]{1,0:T(8,128)(2,1)}), bf16[256,2048]{1,0:T(8,128)(2,1)}) %reduce-scatter.6.cloned.1.call-update) | async-done | bytes 1048592 | tf_op jit(solution)/shard_map/reduce_scatter | solution.py:343
  1057.0 7.1 collective-permute-done.57
  1065.5 8.5 collective-permute-done.56
  1076.4 7.4 collective-permute-done.58
  1085.4 9.6 collective-permute-done.60
  (502 shorter events, 292.5 us)
Async XLA Ops:
  7.2 131.5 %all-gather.6.cloned.1.call-start = ((), (), s32[]{:S(2)}) async-start(), calls=%async_computation.5 | async-start | bytes 9437184 | tf_op jit(solution)/shard_map/all_gather | solution.py:323
  17.5 161.8 %all-gather.8.cloned.1.call-start = ((), (), s32[]{:S(2)}) async-start(), calls=%async_computation.6 | async-start | bytes 2359296 | tf_op jit(solution)/shard_map/all_gather | solution.py:430
  21.5 367.5 %all-gather.10.cloned.1.call-start = ((), (), s32[]{:S(2)}) async-start(), calls=%async_computation.7 | async-start | bytes 12976128 | tf_op jit(solution)/shard_map/all_gather | solution.py:433
  24.3 400.7 %all-gather.12.cloned.1.call-start = ((), (), s32[]{:S(2)}) async-start(), calls=%async_computation.8 | async-start | bytes 6488064 | tf_op jit(solution)/shard_map/all_gather | solution.py:437
  30.0 81.0 %collective-permute-start = (bf16[256,2048]{1,0:T(8,128)(2,1)}, bf16[256,2048]{1,0:T(8,128)(2,1)}, u32[]{:S(2)}, u32[]{:S(2)}) collective-permute-start(bf16[256,2048]{1,0:T(8,128)(2,1)} %get-tuple-element.50), channel_id=1, source_target_pairs={{0,8},{8,0},{16,24},{24,16},{1,9},{9,1},{17,25},{25,17},{2,10},{10... | collective-permute-start | bytes 3145736 | tf_op jit(solution)/shard_map/ppermute | solution.py:18
  32.9 85.0 %collective-permute-start.2 = (bf16[256,2048]{1,0:T(8,128)(2,1)}, bf16[256,2048]{1,0:T(8,128)(2,1)}, u32[]{:S(2)}, u32[]{:S(2)}) collective-permute-start(bf16[256,2048]{1,0:T(8,128)(2,1)} %get-tuple-element.50), channel_id=1, source_target_pairs={{0,16},{8,24},{16,0},{24,8},{1,17},{9,25},{17,1},{25,9},{2,18},{10... | collective-permute-start | bytes 3145736 | tf_op jit(solution)/shard_map/ppermute | solution.py:18
  36.5 79.1 %collective-permute-start.1 = (bf16[256,2048]{1,0:T(8,128)(2,1)}, bf16[256,2048]{1,0:T(8,128)(2,1)}, u32[]{:S(2)}, u32[]{:S(2)}) collective-permute-start(bf16[256,2048]{1,0:T(8,128)(2,1)} %get-tuple-element.48), channel_id=1, source_target_pairs={{0,8},{8,0},{16,24},{24,16},{1,9},{9,1},{17,25},{25,17},{2,10},{10... | collective-permute-start | bytes 3145736 | tf_op jit(solution)/shard_map/ppermute | solution.py:18
  37.0 75.3 %collective-permute-start.3 = (bf16[256,2048]{1,0:T(8,128)(2,1)}, bf16[256,2048]{1,0:T(8,128)(2,1)}, u32[]{:S(2)}, u32[]{:S(2)}) collective-permute-start(bf16[256,2048]{1,0:T(8,128)(2,1)} %get-tuple-element.48), channel_id=1, source_target_pairs={{0,16},{8,24},{16,0},{24,8},{1,17},{9,25},{17,1},{25,9},{2,18},{10... | collective-permute-start | bytes 3145736 | tf_op jit(solution)/shard_map/ppermute | solution.py:18
  41.7 176.3 %collective-permute-start.28 = (bf16[256,2048]{1,0:T(8,128)(2,1)}, bf16[256,2048]{1,0:T(8,128)(2,1)}, u32[]{:S(2)}, u32[]{:S(2)}) collective-permute-start(bf16[256,2048]{1,0:T(8,128)(2,1)} %get-tuple-element.38), channel_id=1, source_target_pairs={{0,8},{8,0},{16,24},{24,16},{1,9},{9,1},{17,25},{25,17},{2,10},{10... | collective-permute-start | bytes 3145736 | tf_op jit(solution)/shard_map/ppermute | solution.py:18
  112.3 25.3 %collective-permute-start.5 = (bf16[256,2048]{1,0:T(8,128)(2,1)}, bf16[256,2048]{1,0:T(8,128)(2,1)S(1)}, u32[]{:S(2)}, u32[]{:S(2)}) collective-permute-start(bf16[256,2048]{1,0:T(8,128)(2,1)} %collective-permute-done.3), channel_id=1, source_target_pairs={{0,8},{8,0},{16,24},{24,16},{1,9},{9,1},{17,25},{25,17},{2,10},{10... | collective-permute-start | bytes 3145736 | tf_op jit(solution)/shard_map/ppermute | solution.py:18
  183.9 26.4 %collective-permute-start.14 = (bf16[256,2048]{1,0:T(8,128)(2,1)}, bf16[256,2048]{1,0:T(8,128)(2,1)}, u32[]{:S(2)}, u32[]{:S(2)}) collective-permute-start(bf16[256,2048]{1,0:T(8,128)(2,1)} %get-tuple-element.74), channel_id=1, source_target_pairs={{0,16},{8,24},{16,0},{24,8},{1,17},{9,25},{17,1},{25,9},{2,18},{10... | collective-permute-start | bytes 3145736 | tf_op jit(solution)/shard_map/ppermute | solution.py:18
  186.4 55.3 %collective-permute-start.31 = (bf16[256,2048]{1,0:T(8,128)(2,1)}, bf16[256,2048]{1,0:T(8,128)(2,1)}, u32[]{:S(2)}, u32[]{:S(2)}) collective-permute-start(bf16[256,2048]{1,0:T(8,128)(2,1)} %get-tuple-element.36), channel_id=1, source_target_pairs={{0,16},{8,24},{16,0},{24,8},{1,17},{9,25},{17,1},{25,9},{2,18},{10... | collective-permute-start | bytes 3145736 | tf_op jit(solution)/shard_map/ppermute | solution.py:18
  187.5 26.2 %collective-permute-start.8 = (bf16[256,2048]{1,0:T(8,128)(2,1)}, bf16[256,2048]{1,0:T(8,128)(2,1)}, u32[]{:S(2)}, u32[]{:S(2)}) collective-permute-start(bf16[256,2048]{1,0:T(8,128)(2,1)} %get-tuple-element.73), channel_id=1, source_target_pairs={{0,8},{8,0},{16,24},{24,16},{1,9},{9,1},{17,25},{25,17},{2,10},{10... | collective-permute-start | bytes 3145736 | tf_op jit(solution)/shard_map/ppermute | solution.py:18
  218.0 37.3 %collective-permute-start.13 = (bf16[256,2048]{1,0:T(8,128)(2,1)}, bf16[256,2048]{1,0:T(8,128)(2,1)}, u32[]{:S(2)}, u32[]{:S(2)}) collective-permute-start(bf16[256,2048]{1,0:T(8,128)(2,1)} %slice.474), channel_id=1, source_target_pairs={{0,16},{8,24},{16,0},{24,8},{1,17},{9,25},{17,1},{25,9},{2,18},{10... | collective-permute-start | bytes 3145736 | tf_op jit(solution)/shard_map/ppermute | solution.py:18
  219.6 36.2 %collective-permute-start.7 = (bf16[256,2048]{1,0:T(8,128)(2,1)}, bf16[256,2048]{1,0:T(8,128)(2,1)}, u32[]{:S(2)}, u32[]{:S(2)}) collective-permute-start(bf16[256,2048]{1,0:T(8,128)(2,1)} %slice.465), channel_id=1, source_target_pairs={{0,8},{8,0},{16,24},{24,16},{1,9},{9,1},{17,25},{25,17},{2,10},{10... | collective-permute-start | bytes 3145736 | tf_op jit(solution)/shard_map/ppermute | solution.py:18
  232.8 35.7 %collective-permute-start.15 = (bf16[256,2048]{1,0:T(8,128)(2,1)}, bf16[256,2048]{1,0:T(8,128)(2,1)}, u32[]{:S(2)}, u32[]{:S(2)}) collective-permute-start(bf16[256,2048]{1,0:T(8,128)(2,1)} %add_convert_fusion.10), channel_id=1, source_target_pairs={{0,8},{8,0},{16,24},{24,16},{1,9},{9,1},{17,25},{25,17},{2,10},{10... | collective-permute-start | bytes 3145736 | tf_op jit(solution)/shard_map/ppermute | solution.py:18
  233.3 44.5 %collective-permute-start.9 = (bf16[256,2048]{1,0:T(8,128)(2,1)}, bf16[256,2048]{1,0:T(8,128)(2,1)}, u32[]{:S(2)}, u32[]{:S(2)}) collective-permute-start(bf16[256,2048]{1,0:T(8,128)(2,1)} %add_convert_fusion.11), channel_id=1, source_target_pairs={{0,16},{8,24},{16,0},{24,8},{1,17},{9,25},{17,1},{25,9},{2,18},{10... | collective-permute-start | bytes 3145736 | tf_op jit(solution)/shard_map/ppermute | solution.py:18
  235.8 649.8 %reduce-scatter.8.cloned.1.call-start = ((), (), s32[]{:S(2)}) async-start(), calls=%async_computation.10 | async-start | bytes 2359296 | tf_op jit(solution)/shard_map/reduce_scatter | solution.py:541
  241.7 49.2 %collective-permute-start.29 = (bf16[256,2048]{1,0:T(8,128)(2,1)}, bf16[256,2048]{1,0:T(8,128)(2,1)S(1)}, u32[]{:S(2)}, u32[]{:S(2)}) collective-permute-start(bf16[256,2048]{1,0:T(8,128)(2,1)} %get-tuple-element.36), channel_id=1, source_target_pairs={{0,8},{8,0},{16,24},{24,16},{1,9},{9,1},{17,25},{25,17},{2,10},{10... | collective-permute-start | bytes 3145736 | tf_op jit(solution)/shard_map/ppermute | solution.py:18
  255.3 44.8 %collective-permute-start.30 = (bf16[256,2048]{1,0:T(8,128)(2,1)}, bf16[256,2048]{1,0:T(8,128)(2,1)S(1)}, u32[]{:S(2)}, u32[]{:S(2)}) collective-permute-start(bf16[256,2048]{1,0:T(8,128)(2,1)} %get-tuple-element.38), channel_id=1, source_target_pairs={{0,16},{8,24},{16,0},{24,8},{1,17},{9,25},{17,1},{25,9},{2,18},{10... | collective-permute-start | bytes 3145736 | tf_op jit(solution)/shard_map/ppermute | solution.py:18
  255.8 66.8 %collective-permute-start.32 = (bf16[256,2048]{1,0:T(8,128)(2,1)}, bf16[256,2048]{1,0:T(8,128)(2,1)S(1)}, u32[]{:S(2)}, u32[]{:S(2)}) collective-permute-start(bf16[256,2048]{1,0:T(8,128)(2,1)} %collective-permute-done.28), channel_id=1, source_target_pairs={{0,16},{8,24},{16,0},{24,8},{1,17},{9,25},{17,1},{25,9},{2,18},{10... | collective-permute-start | bytes 3145736 | tf_op jit(solution)/shard_map/ppermute | solution.py:18
  268.5 67.8 %collective-permute-start.33 = (bf16[256,2048]{1,0:T(8,128)(2,1)}, bf16[256,2048]{1,0:T(8,128)(2,1)S(1)}, u32[]{:S(2)}, u32[]{:S(2)}) collective-permute-start(bf16[256,2048]{1,0:T(8,128)(2,1)} %collective-permute-done.31), channel_id=1, source_target_pairs={{0,8},{8,0},{16,24},{24,16},{1,9},{9,1},{17,25},{25,17},{2,10},{10... | collective-permute-start | bytes 3145736 | tf_op jit(solution)/shard_map/ppermute | solution.py:18
  283.4 52.4 %collective-permute-start.16 = (bf16[256,2048]{1,0:T(8,128)(2,1)S(1)}, bf16[256,2048]{1,0:T(8,128)(2,1)S(1)}, u32[]{:S(2)}, u32[]{:S(2)}) collective-permute-start(bf16[256,2048]{1,0:T(8,128)(2,1)S(1)} %get-tuple-element.44), channel_id=1, source_target_pairs={{0,8},{8,0},{16,24},{24,16},{1,9},{9,1},{17,25},{25,17},{2,10},{10... | collective-permute-start | bytes 3145736 | tf_op jit(solution)/shard_map/ppermute | solution.py:18
  290.8 54.2 %collective-permute-start.19 = (bf16[256,2048]{1,0:T(8,128)(2,1)S(1)}, bf16[256,2048]{1,0:T(8,128)(2,1)S(1)}, u32[]{:S(2)}, u32[]{:S(2)}) collective-permute-start(bf16[256,2048]{1,0:T(8,128)(2,1)S(1)} %get-tuple-element.40), channel_id=1, source_target_pairs={{0,16},{8,24},{16,0},{24,8},{1,17},{9,25},{17,1},{25,9},{2,18},{10... | collective-permute-start | bytes 3145736 | tf_op jit(solution)/shard_map/ppermute | solution.py:18
  300.1 58.1 %collective-permute-start.17 = (bf16[256,2048]{1,0:T(8,128)(2,1)S(1)}, bf16[256,2048]{1,0:T(8,128)(2,1)S(1)}, u32[]{:S(2)}, u32[]{:S(2)}) collective-permute-start(bf16[256,2048]{1,0:T(8,128)(2,1)S(1)} %get-tuple-element.40), channel_id=1, source_target_pairs={{0,8},{8,0},{16,24},{24,16},{1,9},{9,1},{17,25},{25,17},{2,10},{10... | collective-permute-start | bytes 3145736 | tf_op jit(solution)/shard_map/ppermute | solution.py:18
  322.6 44.9 %collective-permute-start.18 = (bf16[256,2048]{1,0:T(8,128)(2,1)S(1)}, bf16[256,2048]{1,0:T(8,128)(2,1)S(1)}, u32[]{:S(2)}, u32[]{:S(2)}) collective-permute-start(bf16[256,2048]{1,0:T(8,128)(2,1)S(1)} %get-tuple-element.44), channel_id=1, source_target_pairs={{0,16},{8,24},{16,0},{24,8},{1,17},{9,25},{17,1},{25,9},{2,18},{10... | collective-permute-start | bytes 3145736 | tf_op jit(solution)/shard_map/ppermute | solution.py:18
  335.8 51.2 %collective-permute-start.20 = (bf16[256,2048]{1,0:T(8,128)(2,1)S(1)}, bf16[256,2048]{1,0:T(8,128)(2,1)S(1)}, u32[]{:S(2)}, u32[]{:S(2)}) collective-permute-start(bf16[256,2048]{1,0:T(8,128)(2,1)S(1)} %collective-permute-done.16), channel_id=1, source_target_pairs={{0,16},{8,24},{16,0},{24,8},{1,17},{9,25},{17,1},{25,9},{2,18},{10... | collective-permute-start | bytes 3145736 | tf_op jit(solution)/shard_map/ppermute | solution.py:18
  345.1 42.9 %collective-permute-start.21 = (bf16[256,2048]{1,0:T(8,128)(2,1)S(1)}, bf16[256,2048]{1,0:T(8,128)(2,1)S(1)}, u32[]{:S(2)}, u32[]{:S(2)}) collective-permute-start(bf16[256,2048]{1,0:T(8,128)(2,1)S(1)} %collective-permute-done.19), channel_id=1, source_target_pairs={{0,8},{8,0},{16,24},{24,16},{1,9},{9,1},{17,25},{25,17},{2,10},{10... | collective-permute-start | bytes 3145736 | tf_op jit(solution)/shard_map/ppermute | solution.py:18
  456.5 62.0 %collective-permute-start.23 = (bf16[256,2048]{1,0:T(8,128)(2,1)S(1)}, bf16[256,2048]{1,0:T(8,128)(2,1)S(1)}, u32[]{:S(2)}, u32[]{:S(2)}) collective-permute-start(bf16[256,2048]{1,0:T(8,128)(2,1)S(1)} %get-tuple-element.71), channel_id=1, source_target_pairs={{0,8},{8,0},{16,24},{24,16},{1,9},{9,1},{17,25},{25,17},{2,10},{10... | collective-permute-start | bytes 3145736 | tf_op jit(solution)/shard_map/ppermute | solution.py:18
  456.9 63.5 %collective-permute-start.26 = (bf16[256,2048]{1,0:T(8,128)(2,1)S(1)}, bf16[256,2048]{1,0:T(8,128)(2,1)S(1)}, u32[]{:S(2)}, u32[]{:S(2)}) collective-permute-start(bf16[256,2048]{1,0:T(8,128)(2,1)S(1)} %get-tuple-element.72), channel_id=1, source_target_pairs={{0,16},{8,24},{16,0},{24,8},{1,17},{9,25},{17,1},{25,9},{2,18},{10... | collective-permute-start | bytes 3145736 | tf_op jit(solution)/shard_map/ppermute | solution.py:18
  471.3 50.1 %collective-permute-start.38 = (bf16[256,2048]{1,0:T(8,128)(2,1)S(1)}, bf16[256,2048]{1,0:T(8,128)(2,1)S(1)}, u32[]{:S(2)}, u32[]{:S(2)}) collective-permute-start(bf16[256,2048]{1,0:T(8,128)(2,1)S(1)} %get-tuple-element.69), channel_id=1, source_target_pairs={{0,16},{8,24},{16,0},{24,8},{1,17},{9,25},{17,1},{25,9},{2,18},{10... | collective-permute-start | bytes 3145736 | tf_op jit(solution)/shard_map/ppermute | solution.py:18
  484.7 50.5 %collective-permute-start.34 = (bf16[256,2048]{1,0:T(8,128)(2,1)S(1)}, bf16[256,2048]{1,0:T(8,128)(2,1)S(1)}, u32[]{:S(2)}, u32[]{:S(2)}) collective-permute-start(bf16[256,2048]{1,0:T(8,128)(2,1)S(1)} %slice.497), channel_id=1, source_target_pairs={{0,8},{8,0},{16,24},{24,16},{1,9},{9,1},{17,25},{25,17},{2,10},{10... | collective-permute-start | bytes 3145736 | tf_op jit(solution)/shard_map/ppermute | solution.py:18
  486.2 47.1 %collective-permute-start.35 = (bf16[256,2048]{1,0:T(8,128)(2,1)S(1)}, bf16[256,2048]{1,0:T(8,128)(2,1)S(1)}, u32[]{:S(2)}, u32[]{:S(2)}) collective-permute-start(bf16[256,2048]{1,0:T(8,128)(2,1)S(1)} %get-tuple-element.70), channel_id=1, source_target_pairs={{0,8},{8,0},{16,24},{24,16},{1,9},{9,1},{17,25},{25,17},{2,10},{10... | collective-permute-start | bytes 3145736 | tf_op jit(solution)/shard_map/ppermute | solution.py:18
  518.5 26.1 %collective-permute-start.37 = (bf16[256,2048]{1,0:T(8,128)(2,1)S(1)}, bf16[256,2048]{1,0:T(8,128)(2,1)S(1)}, u32[]{:S(2)}, u32[]{:S(2)}) collective-permute-start(bf16[256,2048]{1,0:T(8,128)(2,1)S(1)} %slice.505), channel_id=1, source_target_pairs={{0,16},{8,24},{16,0},{24,8},{1,17},{9,25},{17,1},{25,9},{2,18},{10... | collective-permute-start | bytes 3145736 | tf_op jit(solution)/shard_map/ppermute | solution.py:18
  520.4 35.4 %collective-permute-start.22 = (bf16[256,2048]{1,0:T(8,128)(2,1)S(1)}, bf16[256,2048]{1,0:T(8,128)(2,1)S(1)}, u32[]{:S(2)}, u32[]{:S(2)}) collective-permute-start(bf16[256,2048]{1,0:T(8,128)(2,1)S(1)} %slice.483), channel_id=1, source_target_pairs={{0,8},{8,0},{16,24},{24,16},{1,9},{9,1},{17,25},{25,17},{2,10},{10... | collective-permute-start | bytes 3145736 | tf_op jit(solution)/shard_map/ppermute | solution.py:18
  521.5 48.9 %collective-permute-start.25 = (bf16[256,2048]{1,0:T(8,128)(2,1)S(1)}, bf16[256,2048]{1,0:T(8,128)(2,1)S(1)}, u32[]{:S(2)}, u32[]{:S(2)}) collective-permute-start(bf16[256,2048]{1,0:T(8,128)(2,1)S(1)} %slice.489), channel_id=1, source_target_pairs={{0,16},{8,24},{16,0},{24,8},{1,17},{9,25},{17,1},{25,9},{2,18},{10... | collective-permute-start | bytes 3145736 | tf_op jit(solution)/shard_map/ppermute | solution.py:18
  533.3 56.2 %collective-permute-start.24 = (bf16[256,2048]{1,0:T(8,128)(2,1)S(1)}, bf16[256,2048]{1,0:T(8,128)(2,1)S(1)}, u32[]{:S(2)}, u32[]{:S(2)}) collective-permute-start(bf16[256,2048]{1,0:T(8,128)(2,1)S(1)} %add_convert_fusion.9), channel_id=1, source_target_pairs={{0,16},{8,24},{16,0},{24,8},{1,17},{9,25},{17,1},{25,9},{2,18},{10... | collective-permute-start | bytes 3145736 | tf_op jit(solution)/shard_map/ppermute | solution.py:18
  535.2 54.4 %collective-permute-start.27 = (bf16[256,2048]{1,0:T(8,128)(2,1)S(1)}, bf16[256,2048]{1,0:T(8,128)(2,1)S(1)}, u32[]{:S(2)}, u32[]{:S(2)}) collective-permute-start(bf16[256,2048]{1,0:T(8,128)(2,1)S(1)} %add_convert_fusion.8), channel_id=1, source_target_pairs={{0,8},{8,0},{16,24},{24,16},{1,9},{9,1},{17,25},{25,17},{2,10},{10... | collective-permute-start | bytes 3145736 | tf_op jit(solution)/shard_map/ppermute | solution.py:18
  544.6 51.2 %collective-permute-start.39 = (bf16[256,2048]{1,0:T(8,128)(2,1)S(1)}, bf16[256,2048]{1,0:T(8,128)(2,1)S(1)}, u32[]{:S(2)}, u32[]{:S(2)}) collective-permute-start(bf16[256,2048]{1,0:T(8,128)(2,1)S(1)} %add_convert_fusion.6), channel_id=1, source_target_pairs={{0,8},{8,0},{16,24},{24,16},{1,9},{9,1},{17,25},{25,17},{2,10},{10... | collective-permute-start | bytes 3145736 | tf_op jit(solution)/shard_map/ppermute | solution.py:18
  555.8 50.8 %collective-permute-start.36 = (bf16[256,2048]{1,0:T(8,128)(2,1)S(1)}, bf16[256,2048]{1,0:T(8,128)(2,1)S(1)}, u32[]{:S(2)}, u32[]{:S(2)}) collective-permute-start(bf16[256,2048]{1,0:T(8,128)(2,1)S(1)} %add_convert_fusion.7), channel_id=1, source_target_pairs={{0,16},{8,24},{16,0},{24,8},{1,17},{9,25},{17,1},{25,9},{2,18},{10... | collective-permute-start | bytes 3145736 | tf_op jit(solution)/shard_map/ppermute | solution.py:18
  616.4 46.0 %collective-permute-start.40 = (bf16[256,2048]{1,0:T(8,128)(2,1)S(1)}, bf16[256,2048]{1,0:T(8,128)(2,1)S(1)}, u32[]{:S(2)}, u32[]{:S(2)}) collective-permute-start(bf16[256,2048]{1,0:T(8,128)(2,1)S(1)} %get-tuple-element.32), channel_id=1, source_target_pairs={{0,8},{8,0},{16,24},{24,16},{1,9},{9,1},{17,25},{25,17},{2,10},{10... | collective-permute-start | bytes 3145736 | tf_op jit(solution)/shard_map/ppermute | solution.py:18
  618.0 45.0 %collective-permute-start.43 = (bf16[256,2048]{1,0:T(8,128)(2,1)S(1)}, bf16[256,2048]{1,0:T(8,128)(2,1)S(1)}, u32[]{:S(2)}, u32[]{:S(2)}) collective-permute-start(bf16[256,2048]{1,0:T(8,128)(2,1)S(1)} %get-tuple-element.31), channel_id=1, source_target_pairs={{0,16},{8,24},{16,0},{24,8},{1,17},{9,25},{17,1},{25,9},{2,18},{10... | collective-permute-start | bytes 3145736 | tf_op jit(solution)/shard_map/ppermute | solution.py:18
  620.7 44.0 %collective-permute-start.41 = (bf16[256,2048]{1,0:T(8,128)(2,1)S(1)}, bf16[256,2048]{1,0:T(8,128)(2,1)S(1)}, u32[]{:S(2)}, u32[]{:S(2)}) collective-permute-start(bf16[256,2048]{1,0:T(8,128)(2,1)S(1)} %get-tuple-element.31), channel_id=1, source_target_pairs={{0,8},{8,0},{16,24},{24,16},{1,9},{9,1},{17,25},{25,17},{2,10},{10... | collective-permute-start | bytes 3145736 | tf_op jit(solution)/shard_map/ppermute | solution.py:18
  723.5 180.8 %reduce-scatter.14.cloned.1.call-start = ((), (), s32[]{:S(2)}) async-start(), calls=%async_computation.13 | async-start | bytes 6488064 | tf_op jit(solution)/shard_map/reduce_scatter | solution.py:502
  741.7 170.2 %reduce-scatter.12.cloned.1.call-start = ((), (), s32[]{:S(2)}) async-start(), calls=%async_computation.12 | async-start | bytes 6488064 | tf_op jit(solution)/shard_map/reduce_scatter | solution.py:502
  759.8 197.6 %reduce-scatter.10.cloned.1.call-start = ((), (), s32[]{:S(2)}) async-start(), calls=%async_computation.11 | async-start | bytes 6488064 | tf_op jit(solution)/shard_map/reduce_scatter | solution.py:502
  778.2 269.5 %reduce-scatter.6.cloned.1.call-start = ((), (), s32[]{:S(2)}) async-start(), calls=%async_computation.9 | async-start | bytes 9437184 | tf_op jit(solution)/shard_map/reduce_scatter | solution.py:343
  796.7 41.8 %collective-permute-start.53 = (bf16[256,2048]{1,0:T(8,128)(2,1)}, bf16[256,2048]{1,0:T(8,128)(2,1)}, u32[]{:S(2)}, u32[]{:S(2)}) collective-permute-start(bf16[256,2048]{1,0:T(8,128)(2,1)} %get-tuple-element.66), channel_id=1, source_target_pairs={{0,16},{8,24},{16,0},{24,8},{1,17},{9,25},{17,1},{25,9},{2,18},{10... | collective-permute-start | bytes 3145736 | tf_op jit(solution)/shard_map/ppermute | solution.py:18
  803.2 60.9 %collective-permute-start.49 = (bf16[256,2048]{1,0:T(8,128)(2,1)}, bf16[256,2048]{1,0:T(8,128)(2,1)}, u32[]{:S(2)}, u32[]{:S(2)}) collective-permute-start(bf16[256,2048]{1,0:T(8,128)(2,1)} %slice.511), channel_id=1, source_target_pairs={{0,8},{8,0},{16,24},{24,16},{1,9},{9,1},{17,25},{25,17},{2,10},{10... | collective-permute-start | bytes 3145736 | tf_op jit(solution)/shard_map/ppermute | solution.py:18
  804.7 47.4 %collective-permute-start.50 = (bf16[256,2048]{1,0:T(8,128)(2,1)}, bf16[256,2048]{1,0:T(8,128)(2,1)}, u32[]{:S(2)}, u32[]{:S(2)}) collective-permute-start(bf16[256,2048]{1,0:T(8,128)(2,1)} %get-tuple-element.65), channel_id=1, source_target_pairs={{0,8},{8,0},{16,24},{24,16},{1,9},{9,1},{17,25},{25,17},{2,10},{10... | collective-permute-start | bytes 3145736 | tf_op jit(solution)/shard_map/ppermute | solution.py:18
  837.0 27.0 %collective-permute-start.52 = (bf16[256,2048]{1,0:T(8,128)(2,1)}, bf16[256,2048]{1,0:T(8,128)(2,1)}, u32[]{:S(2)}, u32[]{:S(2)}) collective-permute-start(bf16[256,2048]{1,0:T(8,128)(2,1)} %slice.515), channel_id=1, source_target_pairs={{0,16},{8,24},{16,0},{24,8},{1,17},{9,25},{17,1},{25,9},{2,18},{10... | collective-permute-start | bytes 3145736 | tf_op jit(solution)/shard_map/ppermute | solution.py:18
  840.3 27.2 %collective-permute-start.54 = (bf16[256,2048]{1,0:T(8,128)(2,1)S(1)}, bf16[256,2048]{1,0:T(8,128)(2,1)S(1)}, u32[]{:S(2)}, u32[]{:S(2)}) collective-permute-start(bf16[256,2048]{1,0:T(8,128)(2,1)S(1)} %add_convert_fusion.4), channel_id=1, source_target_pairs={{0,8},{8,0},{16,24},{24,16},{1,9},{9,1},{17,25},{25,17},{2,10},{10... | collective-permute-start | bytes 3145736 | tf_op jit(solution)/shard_map/ppermute | solution.py:18
  854.1 24.3 %collective-permute-start.51 = (bf16[256,2048]{1,0:T(8,128)(2,1)S(1)}, bf16[256,2048]{1,0:T(8,128)(2,1)S(1)}, u32[]{:S(2)}, u32[]{:S(2)}) collective-permute-start(bf16[256,2048]{1,0:T(8,128)(2,1)S(1)} %add_convert_fusion.5), channel_id=1, source_target_pairs={{0,16},{8,24},{16,0},{24,8},{1,17},{9,25},{17,1},{25,9},{2,18},{10... | collective-permute-start | bytes 3145736 | tf_op jit(solution)/shard_map/ppermute | solution.py:18
  906.1 68.7 %collective-permute-start.81 = (bf16[80,2048]{1,0:T(8,128)(2,1)}, bf16[80,2048]{1,0:T(8,128)(2,1)S(1)}, u32[]{:S(2)}, u32[]{:S(2)}) collective-permute-start(bf16[80,2048]{1,0:T(8,128)(2,1)} %slice.556), channel_id=1, source_target_pairs={{0,8},{8,0},{16,24},{24,16},{1,9},{9,1},{17,25},{25,17},{2,10},{10... | collective-permute-start | bytes 983048 | tf_op jit(solution)/shard_map/ppermute | solution.py:18
  906.6 87.6 %collective-permute-start.83 = (bf16[80,2048]{1,0:T(8,128)(2,1)}, bf16[80,2048]{1,0:T(8,128)(2,1)}, u32[]{:S(2)}, u32[]{:S(2)}) collective-permute-start(bf16[80,2048]{1,0:T(8,128)(2,1)} %slice.556), channel_id=1, source_target_pairs={{0,16},{8,24},{16,0},{24,8},{1,17},{9,25},{17,1},{25,9},{2,18},{10... | collective-permute-start | bytes 983048 | tf_op jit(solution)/shard_map/ppermute | solution.py:18
  909.9 78.4 %collective-permute-start.82 = (bf16[96,2048]{1,0:T(8,128)(2,1)}, bf16[96,2048]{1,0:T(8,128)(2,1)}, u32[]{:S(2)}, u32[]{:S(2)}) collective-permute-start(bf16[96,2048]{1,0:T(8,128)(2,1)} %slice.557), channel_id=1, source_target_pairs={{0,8},{8,0},{16,24},{24,16},{1,9},{9,1},{17,25},{25,17},{2,10},{10... | collective-permute-start | bytes 1179656 | tf_op jit(solution)/shard_map/ppermute | solution.py:18
  910.6 87.1 %collective-permute-start.84 = (bf16[96,2048]{1,0:T(8,128)(2,1)}, bf16[96,2048]{1,0:T(8,128)(2,1)}, u32[]{:S(2)}, u32[]{:S(2)}) collective-permute-start(bf16[96,2048]{1,0:T(8,128)(2,1)} %slice.557), channel_id=1, source_target_pairs={{0,16},{8,24},{16,0},{24,8},{1,17},{9,25},{17,1},{25,9},{2,18},{10... | collective-permute-start | bytes 1179656 | tf_op jit(solution)/shard_map/ppermute | solution.py:18
  913.6 63.5 %collective-permute-start.75 = (bf16[80,2048]{1,0:T(8,128)(2,1)}, bf16[80,2048]{1,0:T(8,128)(2,1)}, u32[]{:S(2)}, u32[]{:S(2)}) collective-permute-start(bf16[80,2048]{1,0:T(8,128)(2,1)} %slice.554), channel_id=1, source_target_pairs={{0,8},{8,0},{16,24},{24,16},{1,9},{9,1},{17,25},{25,17},{2,10},{10... | collective-permute-start | bytes 983048 | tf_op jit(solution)/shard_map/ppermute | solution.py:18
  974.8 26.5 %collective-permute-start.77 = (bf16[80,2048]{1,0:T(8,128)(2,1)}, bf16[80,2048]{1,0:T(8,128)(2,1)S(1)}, u32[]{:S(2)}, u32[]{:S(2)}) collective-permute-start(bf16[80,2048]{1,0:T(8,128)(2,1)} %slice.554), channel_id=1, source_target_pairs={{0,16},{8,24},{16,0},{24,8},{1,17},{9,25},{17,1},{25,9},{2,18},{10... | collective-permute-start | bytes 983048 | tf_op jit(solution)/shard_map/ppermute | solution.py:18
  1002.5 49.7 %collective-permute-start.79 = (bf16[80,2048]{1,0:T(8,128)(2,1)}, bf16[80,2048]{1,0:T(8,128)(2,1)}, u32[]{:S(2)}, u32[]{:S(2)}) collective-permute-start(bf16[80,2048]{1,0:T(8,128)(2,1)} %collective-permute-done.75), channel_id=1, source_target_pairs={{0,16},{8,24},{16,0},{24,8},{1,17},{9,25},{17,1},{25,9},{2,18},{10... | collective-permute-start | bytes 983048 | tf_op jit(solution)/shard_map/ppermute | solution.py:18
  1005.1 49.4 %collective-permute-start.73 = (bf16[80,2048]{1,0:T(8,128)(2,1)}, bf16[80,2048]{1,0:T(8,128)(2,1)}, u32[]{:S(2)}, u32[]{:S(2)}) collective-permute-start(bf16[80,2048]{1,0:T(8,128)(2,1)} %collective-permute-done.69), channel_id=1, source_target_pairs={{0,16},{8,24},{16,0},{24,8},{1,17},{9,25},{17,1},{25,9},{2,18},{10... | collective-permute-start | bytes 983048 | tf_op jit(solution)/shard_map/ppermute | solution.py:18
  1007.3 88.0 %collective-permute-start.86 = (bf16[96,2048]{1,0:T(8,128)(2,1)}, bf16[96,2048]{1,0:T(8,128)(2,1)S(1)}, u32[]{:S(2)}, u32[]{:S(2)}) collective-permute-start(bf16[96,2048]{1,0:T(8,128)(2,1)} %collective-permute-done.84), channel_id=1, source_target_pairs={{0,8},{8,0},{16,24},{24,16},{1,9},{9,1},{17,25},{25,17},{2,10},{10... | collective-permute-start | bytes 1179656 | tf_op jit(solution)/shard_map/ppermute | solution.py:18
  1050.7 24.8 %collective-permute-start.55 = (bf16[128,2048]{1,0:T(8,128)(2,1)S(1)}, bf16[128,2048]{1,0:T(8,128)(2,1)S(1)}, u32[]{:S(2)}, u32[]{:S(2)}) collective-permute-start(bf16[128,2048]{1,0:T(8,128)(2,1)S(1)} %get-tuple-element.94), channel_id=1, source_target_pairs={{0,16},{8,24},{16,0},{24,8},{1,17},{9,25},{17,1},{25,9},{2,18},{10... | collective-permute-start | bytes 1572872 | tf_op jit(solution)/shard_map/ppermute | solution.py:18
  1054.6 41.6 %collective-permute-start.80 = (bf16[96,2048]{1,0:T(8,128)(2,1)}, bf16[96,2048]{1,0:T(8,128)(2,1)S(1)}, u32[]{:S(2)}, u32[]{:S(2)}) collective-permute-start(bf16[96,2048]{1,0:T(8,128)(2,1)} %copy-done.37), channel_id=1, source_target_pairs={{0,8},{8,0},{16,24},{24,16},{1,9},{9,1},{17,25},{25,17},{2,10},{10... | collective-permute-start | bytes 1179656 | tf_op jit(solution)/shard_map/ppermute | solution.py:18
  (106 other events, 2146.0 us)
Sparse Core Ops, SparseCore 0:
  17.7 84.9 all-gather.5
  104.8 29.4 all-gather.7
  136.5 108.1 all-gather.9
  246.8 58.7 all-gather.11
  723.6 36.4 reduce-scatter.7
  762.3 63.4 reduce-scatter.13
  828.1 63.2 reduce-scatter.11
  894.2 63.2 reduce-scatter.9
  959.8 87.9 reduce-scatter.5

commit v2 on v1

--- a/solution.py
+++ b/solution.py
@@ -23,38 +23,56 @@
     return lax.ppermute(x, "fsdp", [(i, i ^ 1) for i in range(size)])
 
 
-def spread(units):
+def halfway(rows):
+    return max(16, rows // 32 * 16)
+
+
+def spread_near(x):
     size = lax.axis_size("seq")
     if size != 4:
-        return [units] + [[swap_seq(u, i) for u in units] for i in range(1, size)]
-    by_x = [swap_seq(u, 1) for u in units]
-    by_y = [swap_seq(u, 2) for u in units]
-    half = (len(units) + 1) // 2
-    both = [swap_seq(u, 2) for u in by_x[:half]] + [swap_seq(u, 1) for u in by_y[half:]]
-    return [units, by_x, by_y, both]
-
-
-def collect(parts):
-    size = lax.axis_size("seq")
+        return [x] + [swap_seq(x, i) for i in range(1, size)]
+    return [x, swap_seq(x, 1), swap_seq(x, 2)]
+
+
+def spread_far(near):
+    if len(near) != 3:
+        return [[x] for x in near]
+    _, by_x, by_y = near
+    cut = halfway(by_x.shape[0])
+    return [[x] for x in near] + [[swap_seq(by_x[:cut], 2), swap_seq(by_y[cut:], 1)]]
+
+
+def spread(x):
+    return spread_far(spread_near(x))
+
+
+def collect_far(part):
+    if lax.axis_size("seq") != 4:
+        return ()
+    cut = halfway(part.shape[0])
+    return swap_seq(part[:cut], 1), swap_seq(part[cut:], 2)
+
+
+def collect_near(parts, passed):
     wide = lambda x: x.astype(F32)
-    count = len(parts[0])
-    if size != 4:
-        out = []
-        for b in range(count):
-            total = wide(parts[0][b])
-            for i in range(1, size):
-                total = total + wide(swap_seq(parts[i][b].astype(LOW), i))
-            out.append(total)
-        return out
-    half = (count + 1) // 2
-    out = []
-    for b in range(count):
-        first, second = (1, 2) if b < half else (2, 1)
-        passed = swap_seq(parts[3][b].astype(LOW), first)
-        direct = swap_seq(parts[first][b].astype(LOW), first)
-        joined = swap_seq((wide(parts[second][b]) + wide(passed)).astype(LOW), second)
-        out.append(wide(parts[0][b]) + wide(direct) + wide(joined))
-    return out
+    if not passed:
+        total = wide(parts[0])
+        for i in range(1, len(parts)):
+            total = total + wide(swap_seq(parts[i], i))
+        return total
+    by_x, by_y = passed
+    cut = by_x.shape[0]
+    to_x = lax.dynamic_update_slice_in_dim(
+        parts[1], (wide(parts[1][cut:]) + wide(by_y)).astype(LOW), cut, 0
+    )
+    to_y = lax.dynamic_update_slice_in_dim(
+        parts[2], (wide(parts[2][:cut]) + wide(by_x)).astype(LOW), 0, 0
+    )
+    return wide(parts[0]) + wide(swap_seq(to_x, 1)) + wide(swap_seq(to_y, 2))
+
+
+def after(value, *others):
+    return lax.optimization_barrier((value, others))[0]
 
 
 def times_rows(left_side, weight):
@@ -147,12 +165,10 @@
     pre_ref,
     attn_ref,
     grad_ref,
-    factor_ref,
     inner_ref,
     down_ref,
     across_ref,
     out_ref,
-    gated_ref,
     states_ref,
     state_ref,
 ):
@@ -185,11 +201,8 @@
         gate = pre_ref[i, 0, :, 3 * HEAD : 4 * HEAD].astype(F32)
         attn = attn_ref[i, 0].astype(F32)
         grad = grad_ref[i, 0].astype(F32)
-        factor = factor_ref[i, 0]
-        scaled = attn * factor
-        gated_ref[i, 0] = (scaled * gate).astype(LOW)
-        grad_gate = grad * scaled
-        grad_attn = (factor * (grad * gate) - attn * inner_ref[i, 0]).astype(LOW)
+        grad_gate = grad * attn
+        grad_attn = (grad * gate - attn * inner_ref[i, 0]).astype(LOW)
         sig_q = sigmoid(pre_q)
         sig_k = sigmoid(pre_k)
         query = pre_q * sig_q
@@ -257,7 +270,7 @@
     )(me, pre, down, across)
 
 
-def attend_back(me, pre, attn, grad, factor, inner, down, across):
+def attend_back(me, pre, attn, grad, inner, down, across):
     blocks, seqs, slots, width = pre.shape
     heads = width // (4 * HEAD)
     one = pl.BlockSpec((blocks, 1, slots, HEAD), lambda b, h, s: (0, b, 0, h))
@@ -273,20 +286,16 @@
                 one,
                 one,
                 same,
-                same,
                 pl.BlockSpec((1, blocks, slots, HEAD), lambda b, h, s: (h, 0, 0, 0)),
                 pl.BlockSpec((1, blocks, slots), lambda b, h, s: (h, 0, 0)),
             ],
-            out_specs=[four, one],
+            out_specs=four,
             scratch_shapes=[
                 pltpu.VMEM((blocks, HEAD, HEAD), LOW),
                 pltpu.VMEM((HEAD, HEAD), F32),
             ],
         ),
-        out_shape=[
-            jax.ShapeDtypeStruct((blocks, seqs, slots, width), LOW),
-            jax.ShapeDtypeStruct((blocks, seqs, slots, heads * HEAD), LOW),
-        ],
+        out_shape=jax.ShapeDtypeStruct((blocks, seqs, slots, width), LOW),
         compiler_params=pltpu.CompilerParams(
             dimension_semantics=("arbitrary", "arbitrary"), vmem_limit_bytes=40 << 20
         ),
@@ -294,14 +303,280 @@
             flops=8_000_000_000, bytes_accessed=32 << 20, transcendentals=8_000_000
         ),
         name="attend_back",
-    )(me, pre, attn, grad, factor, inner, down, across)
+    )(me, pre, attn, grad, inner, down, across)
+
+
+CHUNK = 512
+
+
+def chunks(hidden):
+    full = hidden // CHUNK
+    return [(c * CHUNK, CHUNK) for c in range(full)] + (
+        [(full * CHUNK, hidden % CHUNK)] if hidden % CHUNK else []
+    )
+
+
+def each_chunk(hidden, step):
+    full = hidden // CHUNK
+
+    def body(c, carry):
+        step(c, pl.multiple_of(c * CHUNK, CHUNK), CHUNK)
+        return carry
+
+    lax.fori_loop(0, full, body, 0)
+    if hidden % CHUNK:
+        step(full, full * CHUNK, hidden % CHUNK)
+
+
+def row_copies(sources, to, sem, first):
+    copies, start = [], 0
+    for n, source in enumerate(sources):
+        count = source.shape[0]
+        copies.append(
+            pltpu.make_async_copy(source, to.at[pl.ds(start, count)], sem.at[first + n])
+        )
+        start += count
+    return copies
+
+
+def unit_forward_kernel(piece, inputs, refs_in, *refs):
+    rows = refs[:inputs]
+    sides = refs[inputs]
+    kept = refs[refs_in : refs_in + 3]
+    xs, left, right, low_left, low_right, prod, row_sem, side_sem, out_sem = refs[refs_in + 3 :]
+    hidden, feat = left.shape
+
+    def fetch(c, start, length):
+        here = pl.ds(start, length)
+        return [
+            pltpu.make_async_copy(sides.at[here, pl.ds(0, feat)], left.at[here], side_sem.at[0, c]),
+            pltpu.make_async_copy(
+                sides.at[here, pl.ds(feat, feat)], right.at[here], side_sem.at[1, c]
+            ),
+        ]
+
+    def store(c, start, length):
+        here = pl.ds(start, length)
+        return [
+            pltpu.make_async_copy(source.at[:, here], to.at[piece, :, here], out_sem.at[k, c])
+            for k, (source, to) in enumerate(zip((low_left, low_right, prod), kept))
+        ]
+
+    loads = row_copies(rows, xs, row_sem, 0)
+    for copy in loads:
+        copy.start()
+    for c, (start, length) in enumerate(chunks(hidden)):
+        for copy in fetch(c, start, length):
+            copy.start()
+    for copy in loads:
+        copy.wait()
+
+    def step(c, start, length):
+        for copy in fetch(c, start, length):
+            copy.wait()
+        here = pl.ds(start, length)
+        lefts = dot_nt(xs[...], left[here])
+        rights = dot_nt(xs[...], right[here])
+        low_left[:, here] = lefts.astype(LOW)
+        low_right[:, here] = rights.astype(LOW)
+        prod[:, here] = (lefts * rights).astype(LOW)
+        for copy in store(c, start, length):
+            copy.start()
+
+    each_chunk(hidden, step)
+    for c, (start, length) in enumerate(chunks(hidden)):
+        for copy in store(c, start, length):
+            copy.wait()
+
+
+WIDE = 2048
+
+
+def unit_backward_kernel(piece, inputs, refs_in, *refs):
+    rows = refs[:inputs]
+    sides, down_ref = refs[inputs : inputs + 2]
+    saved = refs[inputs + 2 : inputs + 5]
+    kept = refs[refs_in : refs_in + 2]
+    head_ref, out_ref = refs[refs_in + 2 : refs_in + 4]
+    gs, left, right, down, low_left, low_right, prod, gl, gr, hs, fs = refs[refs_in + 4 : -5]
+    row_sem, down_sem, side_sem, prod_sem, out_sem = refs[-5:]
+    hidden, feat = left.shape
+    spans = [(n, n * WIDE) for n in range(feat // WIDE)]
+
+    def fetch(c, start, length):
+        here = pl.ds(start, length)
+        return [pltpu.make_async_copy(down_ref.at[here], down.at[here], down_sem.at[0, c])] + [
+            pltpu.make_async_copy(source.at[piece, :, here], to.at[:, here], down_sem.at[1 + k, c])
+            for k, (source, to) in enumerate(zip(saved[:2], (low_left, low_right)))
+        ]
+
+    def fetch_sides(n, start):
+        return [
+            pltpu.make_async_copy(
+                sides.at[:, pl.ds(k * feat + start, WIDE)],
+                to.at[:, pl.ds(start, WIDE)],
+                side_sem.at[k, n],
+            )
+            for k, to in enumerate((left, right))
+        ]
+
+    def store(c, start, length):
+        here = pl.ds(start, length)
+        return [
+            pltpu.make_async_copy(source.at[:, here], to.at[piece, :, here], out_sem.at[k, c])
+            for k, (source, to) in enumerate(zip((gl, gr), kept))
+        ]
+
+    def store_wide(k, n, start):
+        source, to = ((hs, head_ref), (fs, out_ref))[k]
+        here = pl.ds(start, WIDE)
+        return pltpu.make_async_copy(source.at[:, here], to.at[:, here], out_sem.at[2 + k, n])
+
+    loads = row_copies(rows, gs, row_sem, 0)
+    load_prod = pltpu.make_async_copy(saved[2].at[piece], prod, prod_sem)
+    for copy in loads:
+        copy.start()
+    for c, (start, length) in enumerate(chunks(hidden)):
+        for copy in fetch(c, start, length):
+            copy.start()
+    load_prod.start()
+    for n, start in spans:
+        for copy in fetch_sides(n, start):
+            copy.start()
+    for copy in loads:
+        copy.wait()
+
+    def step(c, start, length):
+        for copy in fetch(c, start, length):
+            copy.wait()
+        here = pl.ds(start, length)
+        grad = dot_nt(gs[...], down[here])
+        gl[:, here] = (grad * low_right[:, here].astype(F32)).astype(LOW)
+        gr[:, here] = (grad * low_left[:, here].astype(F32)).astype(LOW)
+        for copy in store(c, start, length):
+            copy.start()
+
+    each_chunk(hidden, step)
+    load_prod.wait()
+
+    def outs(n, carry):
+        start = pl.multiple_of(n * WIDE, WIDE)
+        here = pl.ds(start, WIDE)
+        fs[:, here] = dot_nn(prod[...], down[:, here]).astype(LOW)
+        store_wide(1, n, start).start()
+        return carry
+
+    lax.fori_loop(0, len(spans), outs, 0)
+
+    def heads(n, carry):
+        start = pl.multiple_of(n * WIDE, WIDE)
+        here = pl.ds(start, WIDE)
+        for copy in fetch_sides(n, start):
+            copy.wait()
+        hs[:, here] = (dot_nn(gl[...], left[:, here]) + dot_nn(gr[...], right[:, here])).astype(LOW)
+        store_wide(0, n, start).start()
+        return carry
+
+    lax.fori_loop(0, len(spans), heads, 0)
+    for c, (start, length) in enumerate(chunks(hidden)):
+        for copy in store(c, start, length):
+            copy.wait()
+    for n, start in spans:
+        store_wide(1, n, start).wait()
+        store_wide(0, n, start).wait()
+
+
+def unit_forward(piece, size, rows, sides, kept):
+    count = sum(r.shape[0] for r in rows)
+    hidden, feat = sides.shape[0], sides.shape[1] // 2
+    parts = len(chunks(hidden))
+    anywhere = pl.BlockSpec(memory_space=pl.ANY)
+    inputs = [*rows, sides]
+    aliases = {}
+    if kept is not None:
+        aliases = {len(inputs) + k: k for k in range(3)}
+        inputs += kept
+    return pl.pallas_call(
+        functools.partial(unit_forward_kernel, piece, len(rows), len(inputs)),
+        in_specs=[anywhere] * len(inputs),
+        out_specs=[anywhere] * 3,
+        out_shape=[jax.ShapeDtypeStruct((size, count, hidden), LOW)] * 3,
+        input_output_aliases=aliases,
+        scratch_shapes=[
+            pltpu.VMEM((count, feat), LOW),
+            pltpu.VMEM((hidden, feat), LOW),
+            pltpu.VMEM((hidden, feat), LOW),
+            pltpu.VMEM((count, hidden), LOW),
+            pltpu.VMEM((count, hidden), LOW),
+            pltpu.VMEM((count, hidden), LOW),
+            pltpu.SemaphoreType.DMA((len(rows),)),
+            pltpu.SemaphoreType.DMA((2, parts)),
+            pltpu.SemaphoreType.DMA((3, parts)),
+        ],
+        compiler_params=pltpu.CompilerParams(vmem_limit_bytes=40 << 20),
+        cost_estimate=pl.CostEstimate(
+            flops=4 * count * feat * hidden,
+            bytes_accessed=2 * (2 * feat * hidden + count * (feat + 3 * hidden)),
+            transcendentals=0,
+        ),
+        name="unit_forward",
+    )(*inputs)
+
+
+def unit_backward(piece, size, rows, sides, down, saved, kept):
+    count = sum(r.shape[0] for r in rows)
+    hidden, feat = down.shape
+    parts = len(chunks(hidden))
+    anywhere = pl.BlockSpec(memory_space=pl.ANY)
+    inputs = [*rows, sides, down, *saved]
+    aliases = {}
+    if kept is not None:
+        aliases = {len(inputs) + k: k for k in range(2)}
+        inputs += kept
+    wide = pltpu.VMEM((count, feat), LOW)
+    side = pltpu.VMEM((hidden, feat), LOW)
+    inner = pltpu.VMEM((count, hidden), LOW)
+    outs = pl.pallas_call(
+        functools.partial(unit_backward_kernel, piece, len(rows), len(inputs)),
+        in_specs=[anywhere] * len(inputs),
+        out_specs=[anywhere] * 4,
+        out_shape=[jax.ShapeDtypeStruct((size, count, hidden), LOW)] * 2
+        + [jax.ShapeDtypeStruct((count, feat), LOW)] * 2,
+        input_output_aliases=aliases,
+        scratch_shapes=[
+            wide,
+            side,
+            side,
+            side,
+            inner,
+            inner,
+            inner,
+            inner,
+            inner,
+            wide,
+            wide,
+            pltpu.SemaphoreType.DMA((len(rows),)),
+            pltpu.SemaphoreType.DMA((3, parts)),
+            pltpu.SemaphoreType.DMA((2, feat // WIDE)),
+            pltpu.SemaphoreType.DMA,
+            pltpu.SemaphoreType.DMA((4, max(parts, feat // WIDE))),
+        ],
+        compiler_params=pltpu.CompilerParams(vmem_limit_bytes=50 << 20),
+        cost_estimate=pl.CostEstimate(
+            flops=8 * count * feat * hidden,
+            bytes_accessed=2 * (3 * feat * hidden + count * (3 * feat + 5 * hidden)),
+            transcendentals=0,
+        ),
+        name="unit_backward",
+    )(*inputs)
+    return outs[:2], outs[2], outs[3]
 
 
 def paired_heads(rows):
     return rows % HEAD == 0 and 2 * rows // HEAD == lax.axis_size("seq") == 4
 
 
-def gather_projections(weights, me_seq, me_fsdp):
+def gather_projections(weights, me_seq, me_fsdp, meanwhile):
     rows, feat = weights[0].shape
     size = lax.axis_size("seq")
     if not paired_heads(rows):
@@ -319,7 +594,7 @@
     second = jnp.concatenate(own[2:], 0)
     keep = jnp.where(core == 0, first, second)
     give = jnp.where(core == 0, second, first)
-    got = swap_core(give)
+    got = after(swap_core(give), meanwhile)
     return lax.all_gather(
         jnp.where(core == me_seq // 2, keep, got), "fsdp", axis=0, tiled=True
     )
@@ -340,9 +615,7 @@
             result.append(lax.psum(part, "seq").astype(F32))
         return result
     core = me_fsdp % 2
-    mine = lax.psum_scatter(grad, "fsdp", scatter_dimension=0, tiled=True)
-    pieces = spread([mine[:HEAD], mine[HEAD:]])
-    pieces = [jnp.concatenate(p, 0) for p in pieces]
+    pieces = [jnp.concatenate(p, 0) for p in spread(grad)]
     straight = (core ^ (me_seq // 2)) == 0
     keep = [jnp.where(straight, pieces[j], pieces[2 + j]) for j in range(2)]
     give = [jnp.where(straight, pieces[2 + j], pieces[j]) for j in range(2)]
@@ -372,21 +645,19 @@
     return [stack[i] for i in range(size)]
 
 
-def place_rows(units_by_piece, me_seq):
-    rows = sum(u.shape[0] for u in units_by_piece[0])
-    feat = units_by_piece[0][0].shape[1]
-    out = jnp.zeros((rows * len(units_by_piece), feat), F32)
-    for i, units in enumerate(units_by_piece):
-        start = (me_seq ^ i) * rows
-        for unit in units:
-            out = lax.dynamic_update_slice_in_dim(out, unit.astype(F32), start, 0)
-            start = start + unit.shape[0]
-    return out
-
-
-def halves(x):
-    cut = max(16, x.shape[0] // 32 * 16)
-    return [x[:cut], x[cut:]]
+def place_rows(pieces, me_seq, count):
+    pieces = [jnp.concatenate(p, 0) if len(p) > 1 else p[0] for p in pieces]
+    rows, feat = pieces[0].shape
+    rows //= count
+    result = []
+    for n in range(count):
+        out = jnp.zeros((rows * len(pieces), feat), F32)
+        for i, piece in enumerate(pieces):
+            out = lax.dynamic_update_slice_in_dim(
+                out, piece[n * rows : (n + 1) * rows].astype(F32), (me_seq ^ i) * rows, 0
+            )
+        result.append(out)
+    return result
 
 
 def on_device(
@@ -407,21 +678,24 @@
     size = lax.axis_size("seq")
     me_seq = lax.axis_index("seq")
     me_fsdp = lax.axis_index("fsdp")
-    rows_all = size * seqs * slots
-    span = range(seqs)
+    count = seqs * slots
+    rows_all = size * count
 
     def whole(pieces):
-        return jnp.concatenate([u for units in pieces for u in units], 0)
-
-    def cut(rows):
-        return [rows[b * slots : (b + 1) * slots] for b in span]
-
-    wide = [tokens[b].astype(F32) for b in span]
-    factor_in = [norm_factor(w) for w in wide]
-    normed = [(w * r).astype(LOW) for w, r in zip(wide, factor_in)]
+        return jnp.concatenate([part for parts in pieces for part in parts], 0)
+
+    def cut(rows, i):
+        return rows[i * count : (i + 1) * count]
+
+
+    wide = tokens.reshape(count, feat).astype(F32)
+    factor_in = norm_factor(wide)
+    normed = (wide * factor_in).astype(LOW)
+    normed_pieces = spread(normed)
+    normed_all = whole(normed_pieces)
 
     project = gather_projections(
-        (query_weight, key_weight, value_weight, outgate_weight), me_seq, me_fsdp
+        (query_weight, key_weight, value_weight, outgate_weight), me_seq, me_fsdp, normed
     )
     out_rows = output_weight.shape[0]
     out_own = lax.dynamic_index_in_dim(
@@ -433,113 +707,117 @@
     sides = lax.all_gather(
         jnp.concatenate([hidden(left_weight), hidden(right_weight)], 1), "fsdp", axis=0, tiled=True
     )
-    left_slice, right_slice = sides[:, :feat], sides[:, feat:]
     down_slice = lax.all_gather(hidden(down_weight), "fsdp", axis=0, tiled=True)
 
-    normed_all = whole(spread(normed))
-
     positions = me_seq * slots + lax.iota(jnp.int32, slots)
-    valid = [(positions < lengths[b]).astype(F32)[:, None] for b in span]
-    grad_y = [v * cotangent[b].astype(F32) for b, v in zip(span, valid)]
-    grad_all = whole(spread([g.astype(LOW) for g in grad_y]))
-
-    heads = decay.shape[0]
-    all_decay = lax.all_gather(decay, "seq", axis=0, tiled=True).reshape(heads, size, -1)
-    own_decay = lax.dynamic_index_in_dim(all_decay, me_seq, 1, keepdims=False)
+    valid = (positions[None, :] < lengths[:, None]).astype(F32).reshape(count, 1)
+    grad_y = valid * cotangent.reshape(count, feat).astype(F32)
+    grad_near = spread_near(after(grad_y.astype(LOW), normed_pieces[-1]))
+
+    heads, slot_count = decay.shape
+    if heads == size:
+        send = lambda i: lax.dynamic_slice_in_dim(decay, me_seq ^ i, 1, 0)
+        own_decay = jnp.concatenate(
+            in_order([send(0)] + [swap_seq(send(i), i) for i in range(1, size)], me_seq), 0
+        )
+    else:
+        all_decay = lax.all_gather(decay, "seq", axis=0, tiled=True).reshape(heads, size, -1)
+        own_decay = lax.dynamic_index_in_dim(all_decay, me_seq, 1, keepdims=False)
     across = jnp.cumsum(own_decay.reshape(heads, size, slots), axis=-1)
     down = jnp.broadcast_to(across[..., None], (heads, size, slots, HEAD))
     me = me_seq.astype(jnp.int32).reshape(1)
 
     pre = times_rows(normed_all, project).astype(LOW).reshape(size, seqs, slots, -1)
     ungated, attn, squares = attend(me, pre, down, across)
-
-    branch_parts = [
-        cut(times_rows(ungated[i].reshape(seqs * slots, -1), out_slice).astype(LOW))
-        for i in range(size)
-    ]
-    branch_raw = collect(branch_parts)
-    square = jnp.sum(squares, axis=-1)
+    ungated = after(ungated.reshape(rows_all, -1), grad_near[1:])
+    branch = lambda i: times_rows(cut(ungated, i), out_slice).astype(LOW)
+    branch_parts = [None] * (size - 1) + [branch(size - 1)]
+    branch_far = collect_far(branch_parts[-1])
+    for i in reversed(range(size - 1)):
+        branch_parts[i] = branch(i)
+    branch_raw = collect_near(branch_parts, branch_far)
+    square = jnp.sum(squares, axis=-1).reshape(size, count)
     square_own = square[0]
     for i in range(1, size):
         square_own = square_own + swap_seq(square[i], i)
-    factor_attn = lax.rsqrt(square_own / feat + EPS)
-    residual = [w + b * factor_attn[n][:, None] for n, (w, b) in enumerate(zip(wide, branch_raw))]
-    factor_resid = [norm_factor(r) for r in residual]
-    resid_low = [(r * f).astype(LOW) for r, f in zip(residual, factor_resid)]
-    resid_all = whole(spread(resid_low))
-
-    grad_product = times_rows(grad_all, down_slice)
-    left = times_rows(resid_all, left_slice)
-    right = times_rows(resid_all, right_slice)
-    product = (left * right).astype(LOW)
-    grad_left = (grad_product * right).astype(LOW)
-    grad_right = (grad_product * left).astype(LOW)
-    count = seqs * slots
-    piece = lambda rows, i: rows[i * count : (i + 1) * count]
-    grad_hn = collect(
-        [
-            cut(
-                (
-                    times(piece(grad_left, i), left_slice)
-                    + times(piece(grad_right, i), right_slice)
-                ).astype(LOW)
-            )
-            for i in range(size)
-        ]
-    )
-    ffn = collect(
-        [cut(times(piece(product, i), down_slice).astype(LOW)) for i in range(size)]
-    )
-    layer_out = jnp.stack(
-        [(v * (r + f)).astype(LOW) for v, r, f in zip(valid, residual, ffn)]
-    )
-
-    down_grad = rows_outer(product, grad_all).astype(LOW)
+    factor_attn = lax.rsqrt(square_own / feat + EPS)[:, None]
+    residual = wide + branch_raw * factor_attn
+    factor_resid = norm_factor(residual)
+    resid_pieces = spread((residual * factor_resid).astype(LOW))
+    resid_all = whole(resid_pieces)
+    grad_pieces = spread_far(after(grad_near, resid_pieces[-1]))
+    grad_all = whole(grad_pieces)
+
+    def own_rows(grad):
+        return lax.psum_scatter(grad, "fsdp", scatter_dimension=0, tiled=True)
+
+    saved = None
+    for i in range(size):
+        saved = unit_forward(i, size, resid_pieces[i], sides, saved)
+    down_grad = rows_outer(saved[2].reshape(rows_all, -1), grad_all).astype(LOW)
+    down_mine = own_rows(down_grad)
+    head_parts, ffn_parts = [None] * size, [None] * size
+
+    def back(i, rows, kept):
+        kept, head_parts[i], ffn_parts[i] = unit_backward(
+            i, size, rows, sides, down_slice, saved, kept
+        )
+        return kept
+
+    kept = back(size - 1, after(grad_pieces[-1], down_grad), None)
+    head_far = collect_far(head_parts[-1])
+    ffn_far = collect_far(ffn_parts[-1])
+    for i in range(1, size - 1):
+        kept = back(i, grad_pieces[i], kept)
+    kept = back(0, after(grad_pieces[0], head_far, ffn_far), kept)
+    grad_hn = collect_near(head_parts, head_far)
+    grad_left, grad_right = [k.reshape(rows_all, -1) for k in kept]
     left_grad = rows_outer(grad_left, resid_all).astype(LOW)
-    right_grad = rows_outer(grad_right, resid_all).astype(LOW)
-
-    def share(grad):
-        own = lax.psum_scatter(grad, "fsdp", scatter_dimension=0, tiled=True)
-        return place_rows(spread(halves(own)), me_seq)
-
-    down_out = share(down_grad)
-    left_out = share(left_grad)
-    right_out = share(right_grad)
-
-    grad_resid = [
-        g + norm_back(r, f, h) for g, r, f, h in zip(grad_y, residual, factor_resid, grad_hn)
-    ]
-    grad_branch = [g.astype(LOW) for g in grad_resid]
-    branch_all = whole(spread(grad_branch))
-    inner = jnp.stack(
-        [jnp.mean(g.astype(F32) * b, axis=-1) for g, b in zip(grad_branch, branch_raw)]
-    )
-    scalars = jnp.stack([factor_attn, (factor_attn * inner) * factor_attn * factor_attn])
-    scalars = jnp.stack([scalars] + [swap_seq(scalars, i) for i in range(1, size)])
-    shape_scalars = (size, seqs, slots, HEAD)
-    factor_cols = jnp.broadcast_to(scalars[:, 0, :, :, None], shape_scalars)
-    inner_cols = jnp.broadcast_to(scalars[:, 1, :, :, None], shape_scalars)
+    left_mine = own_rows(left_grad)
+    grad_hn = after(grad_hn, left_grad)
+
+    grad_resid = grad_y + norm_back(residual, factor_resid, grad_hn)
+    grad_branch = (grad_resid * factor_attn).astype(LOW)
+    branch_near = spread_near(grad_branch)
+    right_grad = rows_outer(after(grad_right, grad_branch), resid_all).astype(LOW)
+    right_mine = own_rows(right_grad)
+    inner = jnp.mean(grad_branch.astype(F32) * branch_raw, axis=-1, keepdims=True)
+    inner = (inner * factor_attn * factor_attn)[:, 0]
+    inner = jnp.stack([inner] + [swap_seq(inner, i) for i in range(1, size)])
+    inner = jnp.broadcast_to(inner.reshape(size, seqs, slots, 1), (size, seqs, slots, HEAD))
+    branch_near = after(branch_near, right_grad)
+    branch_pieces = spread_far(branch_near)
+    branch_all = whole(branch_pieces)
     grad_gated = times(branch_all, out_slice).reshape(size, seqs, slots, -1)
-    grad_pre, gated = attend_back(
-        me, pre, attn, grad_gated, factor_cols, inner_cols, down, across
-    )
-    grad_pre_rows = grad_pre.reshape(rows_all, -1)
-    grad_normed = collect(
-        [cut(times(piece(grad_pre_rows, i), project).astype(LOW)) for i in range(size)]
-    )
-    input_grad = jnp.stack(
-        [
-            (g + norm_back(w, r, n)).astype(LOW)
-            for g, w, r, n in zip(grad_resid, wide, factor_in, grad_normed)
-        ]
-    )
-    project_grad = rows_outer(grad_pre_rows, normed_all).astype(LOW)
-    out_grad = rows_outer(branch_all, gated.reshape(rows_all, -1)).astype(LOW)
+
+    grad_pre = attend_back(me, pre, attn, grad_gated, inner, down, across)
+    ffn = collect_near([ffn_parts[0]] + after(ffn_parts[1:], branch_pieces[-1]), ffn_far)
+    grad_pre = after(grad_pre.reshape(rows_all, -1), ffn, down_mine)
+    out_grad = rows_outer(branch_all, after(ungated, grad_pre)).astype(LOW)
+    out_mine = own_rows(after(out_grad, right_mine))
+    project_grad = rows_outer(after(grad_pre, out_grad), normed_all).astype(LOW)
+    project_mine = own_rows(project_grad) if paired_heads(query_weight.shape[0]) else project_grad
+    layer_out = (valid * (residual + ffn)).astype(LOW).reshape(tokens.shape)
+
+    down_near = spread_near(after(down_mine, ffn))
+    normed_part = lambda i, rows: times(cut(rows, i), project).astype(LOW)
+    normed_parts = [None] * (size - 1) + [normed_part(size - 1, after(grad_pre, project_grad, down_near))]
+    normed_far = collect_far(after(normed_parts[-1], left_mine))
+    for i in reversed(range(size - 1)):
+        normed_parts[i] = normed_part(i, after(grad_pre, normed_parts[-1]))
+    grad_normed = collect_near(normed_parts, normed_far)
+    sides_near = spread_near(after(jnp.concatenate([left_mine, right_mine], 0), ffn))
+    grad_normed = after(grad_normed, sides_near, out_mine, project_mine)
+    input_grad = grad_resid + norm_back(wide, factor_in, grad_normed)
+    input_grad = input_grad.astype(LOW).reshape(tokens.shape)
+
+    (down_out,) = place_rows(spread_far(down_near), me_seq, 1)
+    left_out, right_out = place_rows(spread_far(sides_near), me_seq, 2)
+
     query_out, key_out, value_out, outgate_out = scatter_projections(
-        project_grad, query_weight.shape[0], me_seq, me_fsdp
-    )
-    out_mine = lax.psum_scatter(out_grad, "fsdp", scatter_dimension=0, tiled=True)
-    out_pieces = [jnp.concatenate(u, 0) for u in spread(halves(out_mine))]
+        project_mine, query_weight.shape[0], me_seq, me_fsdp
+    )
+    out_pieces = [jnp.concatenate(p, 0) for p in spread(out_mine)]
     out_cols = in_order(out_pieces, me_seq)
     out_out = jnp.concatenate(
         [

time: 1120 us -> 890 us (0.79)
  waiting for transfers between devices: 437 us -> 306 us
  matrix products: 284 us -> 154 us
  Pallas kernels: 43.5 us -> 172 us
  blocking collectives: 62.3 us -> 0 us
  other arithmetic: 103 us -> 83.6 us
  starting transfers between devices: 87.1 us -> 68.1 us
    pallas_call x0 -> x8, Pallas kernels: none -> 130 us  [the longest x4 83.2 us: unit_backward(): pl.pallas_call(functools.partial(unit_backward_kernel, piece, len(rows),...]
    dot_general x17 -> x5, matrix products: 111 us -> 34.4 us  [times(): lax.dot_general(left_side, weight, (((1,), (0,)), ((), ())), preferred_el...]
    reduce_scatter x5, waiting for transfers between devices: 66.4 us -> 0.05 us  [own_rows(): return lax.psum_scatter(grad, 'fsdp', scatter_dimension=0, tiled=True)]
    ppermute x84 -> x57, waiting for transfers between devices: 367 us -> 305 us  [swap_seq(): return lax.ppermute(x, 'seq', [(i, i ^ bit) for i in range(size)])]
    all_gather x1 -> x0, blocking collectives: 62.3 us -> none  [on_device(): lax.all_gather(decay, 'seq', axis=0, tiled=True).reshape(heads, size, -1)]
    dot_general x8 -> x5, matrix products: 91.6 us -> 37.5 us  [times_rows(): lax.dot_general(left_side, weight, (((1,), (1,)), ((), ())), preferred_el...]
    ppermute x84 -> x57, starting transfers between devices: 85.7 us -> 67.1 us  [swap_seq(): return lax.ppermute(x, 'seq', [(i, i ^ bit) for i in range(size)])]
    slice x26 -> x23, local copies, waits for them, and re-layouts: 26.2 us -> 16.3 us  [the longest x7 6.86 us: spread_far(): by_x[:cut]]
  transfers between devices with their start and end apart: 96 -> 69, of which waited for: 41 -> 28; matrix products, arithmetic and copies ran while one was open for 36% -> 33% of each run, Pallas kernels for 1% -> 19%
where the time goes in v2:
time: 890 us; the launch traced here: 885 us
  waiting for transfers between devices  306 us (34%)
  Pallas kernels  172 us (19%)
  matrix products  154 us (17%)
  local copies, waits for them, and re-layouts  85.4 us (10%)
  other arithmetic  83.6 us (9%)
  starting transfers between devices  68.1 us (8%)
  between operations  15.5 us (2%)
    ppermute x57, waiting for transfers between devices, swap_seq(): return lax.ppermute(x, 'seq', [(i, i ^ bit) for i in range(size)])  305 us
    pallas_call x4, Pallas kernels, unit_backward(): pl.pallas_call(functools.partial(unit_backward_kernel, piece, len(rows),...  83.2 us
    dot_general x5, matrix products, rows_outer(): lax.dot_general(left_side, right_side, (((0,), (0,)), ((), ())), preferre...  82.5 us
    ppermute x57, starting transfers between devices, swap_seq(): return lax.ppermute(x, 'seq', [(i, i ^ bit) for i in range(size)])  67.1 us
    pallas_call x4, Pallas kernels, unit_forward(): pl.pallas_call(functools.partial(unit_forward_kernel, piece, len(rows), l...  46.9 us
    unnamed x172, local copies, waits for them, and re-layouts  44.3 us
    dot_general x5, matrix products, times_rows(): lax.dot_general(left_side, weight, (((1,), (1,)), ((), ())), preferred_el...  37.5 us
    dot_general x5, matrix products, times(): lax.dot_general(left_side, weight, (((1,), (0,)), ((), ())), preferred_el...  34.4 us
  transfers between devices with their start and end apart: 69, of which 28 were waited for; matrix products, arithmetic and copies ran while one was open for 33% of the time, Pallas kernels for 19%

profile of v2, /device:TPU:0, one launch (start us, length us, event | category | flops | bytes accessed | tf_op | source)
XLA Modules:
  0.0 885.5 jit_solution(907762877504765454)
XLA Ops:
  14.2 4.2 constant_dynamic-update-slice_fusion.4
  26.7 2.6 collective-permute-start
  29.2 2.7 collective-permute-start.1
  36.2 3.3 fusion.1.refs_0_
  39.6 35.5 %collective-permute-done.5 = f32[1,1024]{1,0:T(1,128)S(1)} collective-permute-done((f32[1,1024]{1,0:T(1,128)S(1)}, f32[1,1024]{1,0:T(1,128)S(1)}, u32[]{:S(2)}, u32[]{:S(2)}) %collective-permute-start.5) | collective-permute-done | bytes 4128 | tf_op jit(solution)/shard_map/ppermute | solution.py:18
  84.2 5.3 reduce-window.6
  90.0 3.2 constant_dynamic-update-slice_fusion.3
  93.1 3.2 constant_dynamic-update-slice_fusion.2
  96.3 10.0 %collective-permute-done.2 = bf16[256,2048]{1,0:T(8,128)(2,1)} collective-permute-done((bf16[256,2048]{1,0:T(8,128)(2,1)}, bf16[256,2048]{1,0:T(8,128)(2,1)}, u32[]{:S(2)}, u32[]{:S(2)}) %collective-permute-start.2) | collective-permute-done | bytes 1048608 | tf_op jit(solution)/shard_map/ppermute | solution.py:18
  115.3 22.3 %convolution_convert_fusion.1 = bf16[2048,2048]{1,0:T(8,128)(2,1)S(1)} fusion(bf16[2048,2048]{1,0:T(8,128)(2,1)} %constant_dynamic-update-slice_fusion, bf16[2048,2048]{1,0:T(8,128)(2,1)} %all-gather.5.cloned.1.call-done), kind=kOutput, calls=%fused_computation.1 | convolution fusion | flops 17184063488 | bytes 25165824 | tf_op jit(solution)/shard_map/dot_general | solution.py:79
  138.3 14.2 %attend.1 = (bf16[4,2,256,512]{3,2,1,0:T(8,128)(2,1)S(1)}, bf16[4,2,256,512]{3,2,1,0:T(8,128)(2,1)S(1)}, f32[4,2,256,128]{3,2,1,0:T(8,128)S(1)}) custom-call(s32[1]{0:T(128)} %bitcast.1.s_ref, bf16[4,2,256,2048]{3,2,1,0:T(8,128)(2,1)S(1)} %bitcast.102, f32[4,4,256,128]{3,2,1,0:T(8,128)S(1)} %broadcast_in_dim.6.down_ref, ...), custom_call_target="tpu_custom_call" | custom-call | flops 2500000000 | bytes 16777216 | tf_op jit(solution)/shard_map/attend/pallas_call | solution.py:241
  156.5 3.0 convolution_convert_fusion.11
  162.0 2.6 convolution_convert_fusion.12
  164.6 2.6 convolution_convert_fusion.10
  167.2 15.7 %collective-permute-done.10 = bf16[256,2048]{1,0:T(8,128)(2,1)S(1)} collective-permute-done((bf16[256,2048]{1,0:T(8,128)(2,1)S(1)}, bf16[256,2048]{1,0:T(8,128)(2,1)S(1)}, u32[]{:S(2)}, u32[]{:S(2)}) %collective-permute-start.10) | collective-permute-done | bytes 1048608 | tf_op jit(solution)/shard_map/ppermute | solution.py:18
  182.9 2.6 fusion.13
  187.2 2.6 fusion.14
  196.4 34.4 %collective-permute-done.14 = f32[512]{0:T(512)S(1)} collective-permute-done((f32[512]{0:T(512)S(1)}, f32[512]{0:T(512)S(1)}, u32[]{:S(2)}, u32[]{:S(2)}) %collective-permute-start.14) | collective-permute-done | bytes 2080 | tf_op jit(solution)/shard_map/ppermute | solution.py:18
  230.8 4.1 collective-permute-done.15
  234.9 7.0 multiply_reduce_fusion.2
  247.5 12.8 %unit_forward.4 = (bf16[4,512,1408]{2,1,0:T(8,128)(2,1)S(1)}, bf16[4,512,1408]{2,1,0:T(8,128)(2,1)S(1)}, bf16[4,512,1408]{2,1,0:T(8,128)(2,1)}) custom-call(bf16[512,2048]{1,0:T(8,128)(2,1)} %get-tuple-element.133.refs_0_, bf16[1408,4096]{1,0:T(8,128)(2,1)} %all-gather.9.cloned.1.call-done.refs_1_.refs_2_), custom_call_target="tpu_custom_call" | custom-call | flops 5905580032 | bytes 17956864 | tf_op jit(solution)/shard_map/unit_forward/pallas_call | solution.py:499
  260.4 28.9 %collective-permute-done.17.refs_0_ = bf16[512,2048]{1,0:T(8,128)(2,1)} collective-permute-done((bf16[512,2048]{1,0:T(8,128)(2,1)}, bf16[512,2048]{1,0:T(8,128)(2,1)}, u32[]{:S(2)}, u32[]{:S(2)}) %collective-permute-start.17) | collective-permute-done | bytes 2097184 | tf_op jit(solution)/shard_map/ppermute | solution.py:18
  293.8 3.2 constant_dynamic-update-slice_fusion.13
  298.6 12.7 %unit_forward.5 = (bf16[4,512,1408]{2,1,0:T(8,128)(2,1)S(1)}, bf16[4,512,1408]{2,1,0:T(8,128)(2,1)S(1)}, bf16[4,512,1408]{2,1,0:T(8,128)(2,1)}) custom-call(bf16[512,2048]{1,0:T(8,128)(2,1)} %collective-permute-done.17.refs_0_, ...), custom_call_target="tpu_custom_call", output_to_operand_aliasing={{0}: (2, {}), {1}: (3, {}), {2}: (4, {})} | custom-call | flops 5905580032 | bytes 17956864 | tf_op jit(solution)/shard_map/unit_forward/pallas_call | solution.py:499
  311.4 10.8 %unit_forward.6 = (bf16[4,512,1408]{2,1,0:T(8,128)(2,1)S(1)}, bf16[4,512,1408]{2,1,0:T(8,128)(2,1)S(1)}, bf16[4,512,1408]{2,1,0:T(8,128)(2,1)}) custom-call(bf16[512,2048]{1,0:T(8,128)(2,1)S(1)} %collective-permute-done.19.refs_0_, ...), custom_call_target="tpu_custom_call", output_to_operand_aliasing={{0}: (2, {}), {1}: (3, {}), {2}: (4, {})} | custom-call | flops 5905580032 | bytes 17956864 | tf_op jit(solution)/shard_map/unit_forward/pallas_call | solution.py:499
  335.8 10.6 %unit_forward.7 = (bf16[4,512,1408]{2,1,0:T(8,128)(2,1)S(1)}, bf16[4,512,1408]{2,1,0:T(8,128)(2,1)S(1)}, bf16[4,512,1408]{2,1,0:T(8,128)(2,1)}) custom-call(bf16[256,2048]{1,0:T(8,128)(2,1)S(1)} %collective-permute-done.18.refs_0_, bf16[256,2048]{1,0:T(8,128)(2,1)S(1)} %collective-permute-done.20.refs_1_, ...), custom_call_target="tpu_custom_call", output_to_operand_aliasing={{0}: (3, {}), {1}: (4, {}), {2}: (5, {})} | custom-call | flops 5905580032 | bytes 17956864 | tf_op jit(solution)/shard_map/unit_forward/pallas_call | solution.py:499
  353.7 18.0 %convolution_convert_fusion.4 = bf16[1408,2048]{1,0:T(8,128)(2,1)} fusion(bf16[2048,1408]{1,0:T(8,128)(2,1)} %bitcast.110, bf16[2048,2048]{1,0:T(8,128)(2,1)} %constant_dynamic-update-slice_fusion.5), kind=kOutput, calls=%fused_computation.4 | convolution fusion | flops 11814043648 | bytes 19922944 | tf_op jit(solution)/shard_map/dot_general | solution.py:91
  371.7 19.1 %unit_backward.4 = (bf16[4,512,1408]{2,1,0:T(8,128)(2,1)}, bf16[4,512,1408]{2,1,0:T(8,128)(2,1)}, bf16[512,2048]{1,0:T(8,128)(2,1)}, bf16[512,2048]{1,0:T(8,128)(2,1)}) custom-call(bf16[256,2048]{1,0:T(8,128)(2,1)S(1)} %collective-permute-done.21.refs_0_, bf16[256,2048]{1,0:T(8,128)(2,1)S(1)} %collective-permute-done.22.refs_1_, ...), custom_call_target="tpu_custom_call" | custom-call | flops 11811160064 | bytes 30801920 | tf_op jit(solution)/shard_map/unit_backward/pallas_call | solution.py:539
  397.2 21.6 %unit_backward.5 = (bf16[4,512,1408]{2,1,0:T(8,128)(2,1)}, bf16[4,512,1408]{2,1,0:T(8,128)(2,1)}, bf16[512,2048]{1,0:T(8,128)(2,1)}, bf16[512,2048]{1,0:T(8,128)(2,1)}) custom-call(bf16[512,2048]{1,0:T(8,128)(2,1)} %collective-permute-done.8.refs_0_, ...), custom_call_target="tpu_custom_call", output_to_operand_aliasing={{0}: (6, {}), {1}: (7, {})} | custom-call | flops 11811160064 | bytes 30801920 | tf_op jit(solution)/shard_map/unit_backward/pallas_call | solution.py:539
  418.8 21.7 %unit_backward.6 = (bf16[4,512,1408]{2,1,0:T(8,128)(2,1)}, bf16[4,512,1408]{2,1,0:T(8,128)(2,1)}, bf16[512,2048]{1,0:T(8,128)(2,1)}, bf16[512,2048]{1,0:T(8,128)(2,1)}) custom-call(bf16[512,2048]{1,0:T(8,128)(2,1)} %collective-permute-done.9.refs_0_, ...), custom_call_target="tpu_custom_call", output_to_operand_aliasing={{0}: (6, {}), {1}: (7, {})} | custom-call | flops 11811160064 | bytes 30801920 | tf_op jit(solution)/shard_map/unit_backward/pallas_call | solution.py:539
  440.6 3.3 fusion.15
  444.4 2.7 fusion.16
  449.1 20.7 %unit_backward.7 = (bf16[4,512,1408]{2,1,0:T(8,128)(2,1)}, bf16[4,512,1408]{2,1,0:T(8,128)(2,1)}, bf16[512,2048]{1,0:T(8,128)(2,1)S(1)}, bf16[512,2048]{1,0:T(8,128)(2,1)}) custom-call(bf16[512,2048]{1,0:T(8,128)(2,1)} %fusion.1.refs_0_, ...), custom_call_target="tpu_custom_call", output_to_operand_aliasing={{0}: (6, {}), {1}: (7, {})} | custom-call | flops 11811160064 | bytes 30801920 | tf_op jit(solution)/shard_map/unit_backward/pallas_call | solution.py:539
  469.9 16.6 %convolution_convert_fusion.3 = bf16[1408,2048]{1,0:T(8,128)(2,1)} fusion(bf16[2048,1408]{1,0:T(8,128)(2,1)} %bitcast.111, bf16[2048,2048]{1,0:T(8,128)(2,1)S(1)} %bitcast.126), kind=kOutput, calls=%fused_computation.3 | convolution fusion | flops 11814043648 | bytes 19922944 | tf_op jit(solution)/shard_map/dot_general | solution.py:91
  488.7 3.6 convert_add_fusion.2
  494.5 6.6 multiply_reduce_fusion
  501.2 14.1 %convolution_convert_fusion.2 = bf16[1408,2048]{1,0:T(8,128)(2,1)} fusion(bf16[2048,1408]{1,0:T(8,128)(2,1)S(1)} %bitcast.114, bf16[2048,2048]{1,0:T(8,128)(2,1)S(1)} %bitcast.128), kind=kOutput, calls=%fused_computation.2 | convolution fusion | flops 11814043648 | bytes 19922944 | tf_op jit(solution)/shard_map/dot_general | solution.py:91
  518.3 39.2 %collective-permute-done.29 = bf16[512,2048]{1,0:T(8,128)(2,1)S(1)} collective-permute-done((bf16[512,2048]{1,0:T(8,128)(2,1)S(1)}, bf16[512,2048]{1,0:T(8,128)(2,1)S(1)}, u32[]{:S(2)}, u32[]{:S(2)}) %collective-permute-start.29) | collective-permute-done | bytes 2097184 | tf_op jit(solution)/shard_map/ppermute | solution.py:18
  563.4 2.7 collective-permute-start.32
  566.8 2.7 collective-permute-start.37
  569.6 11.3 %collective-permute-done.35 = f32[512]{0:T(512)S(1)} collective-permute-done((f32[512]{0:T(512)S(1)}, f32[512]{0:T(512)S(1)}, u32[]{:S(2)}, u32[]{:S(2)}) %collective-permute-start.35) | collective-permute-done | bytes 2080 | tf_op jit(solution)/shard_map/ppermute | solution.py:18
  587.6 2.7 fusion.18
  594.5 4.8 fusion.41
  599.7 28.2 %attend_back.1 = bf16[4,2,256,2048]{3,2,1,0:T(8,128)(2,1)} custom-call(s32[1]{0:T(128)} %bitcast.1.s_ref, bf16[4,2,256,2048]{3,2,1,0:T(8,128)(2,1)} %bitcast.103, bf16[4,2,256,512]{3,2,1,0:T(8,128)(2,1)S(1)} %copy-done.12, f32[4,2,256,512]{3,2,1,0:T(8,128)S(1)} %bitcast.109, f32[4,2,256,128]{3,2,1,0:T(8,128)S(1)} %broadcast_in_dim.8.inner_ref, ...), custom_call_target="tpu_custom_call" | custom-call | flops 8000000000 | bytes 33554432 | tf_op jit(solution)/shard_map/attend_back/pallas_call | solution.py:279
  628.0 3.1 multiply_convert_fusion
  631.1 9.5 %convolution_convert_fusion.9 = bf16[2048,512]{1,0:T(8,128)(2,1)} fusion(bf16[2048,2048]{1,0:T(8,128)(2,1)} %copy-done.49, bf16[2048,512]{1,0:T(8,128)(2,1)S(1)} %bitcast.108), kind=kOutput, calls=%fused_computation.34 | convolution fusion | flops 4296015872 | bytes 12582912 | tf_op jit(solution)/shard_map/dot_general | solution.py:91
  640.7 24.3 %convolution_convert_fusion = bf16[2048,2048]{1,0:T(8,128)(2,1)} fusion(bf16[2048,2048]{1,0:T(8,128)(2,1)} %bitcast.151, bf16[2048,2048]{1,0:T(8,128)(2,1)} %constant_dynamic-update-slice_fusion), kind=kOutput, calls=%fused_computation | convolution fusion | flops 17184063488 | bytes 25165824 | tf_op jit(solution)/shard_map/dot_general | solution.py:91
  667.2 3.2 broadcast.110.clone.2
  671.7 9.3 %collective-permute-done.39 = bf16[176,2048]{1,0:T(8,128)(2,1)S(1)} collective-permute-done((bf16[176,2048]{1,0:T(8,128)(2,1)S(1)}, bf16[176,2048]{1,0:T(8,128)(2,1)S(1)}, u32[]{:S(2)}, u32[]{:S(2)}) %collective-permute-start.39) | collective-permute-done | bytes 720928 | tf_op jit(solution)/shard_map/ppermute | solution.py:18
  685.2 9.3 %convolution_convert_fusion.8 = bf16[512,2048]{1,0:T(8,128)(2,1)S(1)} fusion(bf16[2048,2048]{1,0:T(8,128)(2,1)} %all-gather.5.cloned.1.call-done, bf16[2048,2048]{1,0:T(8,128)(2,1)} %bitcast.152), kind=kOutput, calls=%fused_computation.33 | convolution fusion | flops 4296015872 | bytes 12582912 | tf_op jit(solution)/shard_map/dot_general | solution.py:85
  694.5 5.7 convolution_convert_fusion.7
  700.2 5.9 convolution_convert_fusion.6
  708.1 8.7 convolution_convert_fusion.5
  716.8 15.7 %collective-permute-done.40 = bf16[256,2048]{1,0:T(8,128)(2,1)S(1)} collective-permute-done((bf16[256,2048]{1,0:T(8,128)(2,1)S(1)}, bf16[256,2048]{1,0:T(8,128)(2,1)S(1)}, u32[]{:S(2)}, u32[]{:S(2)}) %collective-permute-start.40) | collective-permute-done | bytes 1048608 | tf_op jit(solution)/shard_map/ppermute | solution.py:18
  742.6 3.2 broadcast.110.clone.1
  747.1 3.2 broadcast.110.clone
  751.6 26.8 %collective-permute-done.41 = bf16[512,2048]{1,0:T(8,128)(2,1)S(1)} collective-permute-done((bf16[512,2048]{1,0:T(8,128)(2,1)S(1)}, bf16[512,2048]{1,0:T(8,128)(2,1)S(1)}, u32[]{:S(2)}, u32[]{:S(2)}) %collective-permute-start.41) | collective-permute-done | bytes 2097184 | tf_op jit(solution)/shard_map/ppermute | solution.py:18
  780.4 3.2 convert_add_fusion
  783.6 23.6 %collective-permute-done.45 = bf16[352,2048]{1,0:T(8,128)(2,1)S(1)} collective-permute-done((bf16[352,2048]{1,0:T(8,128)(2,1)S(1)}, bf16[352,2048]{1,0:T(8,128)(2,1)S(1)}, u32[]{:S(2)}, u32[]{:S(2)}) %collective-permute-start.45) | collective-permute-done | bytes 1441824 | tf_op jit(solution)/shard_map/ppermute | solution.py:18
  816.2 11.2 %collective-permute-done.57 = bf16[176,2048]{1,0:T(8,128)(2,1)} collective-permute-done((bf16[176,2048]{1,0:T(8,128)(2,1)}, bf16[176,2048]{1,0:T(8,128)(2,1)}, u32[]{:S(2)}, u32[]{:S(2)}) %collective-permute-start.57) | collective-permute-done | bytes 720928 | tf_op jit(solution)/shard_map/ppermute | solution.py:18
  829.7 3.1 collective-permute-done.52
  836.3 3.0 collective-permute-done.53
  845.2 11.1 %collective-permute-done.47 = bf16[256,2048]{1,0:T(8,128)(2,1)S(1)} collective-permute-done((bf16[256,2048]{1,0:T(8,128)(2,1)}, bf16[256,2048]{1,0:T(8,128)(2,1)S(1)}, u32[]{:S(2)}, u32[]{:S(2)}) %collective-permute-start.47) | collective-permute-done | bytes 1048608 | tf_op jit(solution)/shard_map/ppermute | solution.py:18
  858.9 6.7 collective-permute-done.48
  (401 shorter events, 180.2 us)
Async XLA Ops:
  7.2 108.1 %all-gather.5.cloned.1.call-start = ((), (), s32[]{:S(2)}) async-start(), calls=%async_computation.5 | async-start | bytes 9437184 | tf_op jit(solution)/shard_map/all_gather | solution.py:598
  19.9 136.6 %all-gather.7.cloned.1.call-start = ((), (), s32[]{:S(2)}) async-start(), calls=%async_computation.6 | async-start | bytes 2359296 | tf_op jit(solution)/shard_map/all_gather | solution.py:704
  23.9 223.6 %all-gather.9.cloned.1.call-start = ((), (), s32[]{:S(2)}) async-start(), calls=%async_computation.7 | async-start | bytes 12976128 | tf_op jit(solution)/shard_map/all_gather | solution.py:707
  26.6 345.1 %all-gather.11.cloned.1.call-start = ((), (), s32[]{:S(2)}) async-start(), calls=%async_computation.8 | async-start | bytes 6488064 | tf_op jit(solution)/shard_map/all_gather | solution.py:710
  26.7 52.1 %collective-permute-start = (bf16[512,2048]{1,0:T(8,128)(2,1)}, bf16[512,2048]{1,0:T(8,128)(2,1)}, u32[]{:S(2)}, u32[]{:S(2)}) collective-permute-start(bf16[512,2048]{1,0:T(8,128)(2,1)} %get-tuple-element.182), channel_id=1, source_target_pairs={{0,8},{8,0},{16,24},{24,16},{1,9},{9,1},{17,25},{25,17},{2,10},{10... | collective-permute-start | bytes 6291464 | tf_op jit(solution)/shard_map/ppermute | solution.py:18
  29.2 52.2 %collective-permute-start.1 = (bf16[512,2048]{1,0:T(8,128)(2,1)}, bf16[512,2048]{1,0:T(8,128)(2,1)}, u32[]{:S(2)}, u32[]{:S(2)}) collective-permute-start(bf16[512,2048]{1,0:T(8,128)(2,1)} %get-tuple-element.182), channel_id=1, source_target_pairs={{0,16},{8,24},{16,0},{24,8},{1,17},{9,25},{17,1},{25,9},{2,18},{10... | collective-permute-start | bytes 6291464 | tf_op jit(solution)/shard_map/ppermute | solution.py:18
  32.0 43.0 %collective-permute-start.5 = (f32[1,1024]{1,0:T(1,128)S(1)}, f32[1,1024]{1,0:T(1,128)S(1)}, u32[]{:S(2)}, u32[]{:S(2)}) collective-permute-start(f32[1,1024]{1,0:T(1,128)S(1)} %get-tuple-element.171), channel_id=1, source_target_pairs={{0,8},{8,0},{16,24},{24,16},{1,9},{9,1},{17,25},{25,17},{2,10},{10... | collective-permute-start | bytes 12296 | tf_op jit(solution)/shard_map/ppermute | solution.py:18
  32.6 44.6 %collective-permute-start.6 = (f32[1,1024]{1,0:T(1,128)S(1)}, f32[1,1024]{1,0:T(1,128)S(1)}, u32[]{:S(2)}, u32[]{:S(2)}) collective-permute-start(f32[1,1024]{1,0:T(1,128)S(1)} %get-tuple-element.174), channel_id=1, source_target_pairs={{0,24},{8,16},{16,8},{24,0},{1,25},{9,17},{17,9},{25,1},{2,26},{10... | collective-permute-start | bytes 12296 | tf_op jit(solution)/shard_map/ppermute | solution.py:18
  33.5 45.1 %collective-permute-start.7 = (f32[1,1024]{1,0:T(1,128)S(1)}, f32[1,1024]{1,0:T(1,128)S(1)}, u32[]{:S(2)}, u32[]{:S(2)}) collective-permute-start(f32[1,1024]{1,0:T(1,128)S(1)} %get-tuple-element.173), channel_id=1, source_target_pairs={{0,16},{8,24},{16,0},{24,8},{1,17},{9,25},{17,1},{25,9},{2,18},{10... | collective-permute-start | bytes 12296 | tf_op jit(solution)/shard_map/ppermute | solution.py:18
  81.1 25.2 %collective-permute-start.2 = (bf16[256,2048]{1,0:T(8,128)(2,1)}, bf16[256,2048]{1,0:T(8,128)(2,1)}, u32[]{:S(2)}, u32[]{:S(2)}) collective-permute-start(bf16[256,2048]{1,0:T(8,128)(2,1)} %slice.358), channel_id=1, source_target_pairs={{0,16},{8,24},{16,0},{24,8},{1,17},{9,25},{17,1},{25,9},{2,18},{10... | collective-permute-start | bytes 3145736 | tf_op jit(solution)/shard_map/ppermute | solution.py:18
  83.8 24.9 %collective-permute-start.3 = (bf16[256,2048]{1,0:T(8,128)(2,1)}, bf16[256,2048]{1,0:T(8,128)(2,1)}, u32[]{:S(2)}, u32[]{:S(2)}) collective-permute-start(bf16[256,2048]{1,0:T(8,128)(2,1)} %slice.359), channel_id=1, source_target_pairs={{0,8},{8,0},{16,24},{24,16},{1,9},{9,1},{17,25},{25,17},{2,10},{10... | collective-permute-start | bytes 3145736 | tf_op jit(solution)/shard_map/ppermute | solution.py:18
  108.6 47.4 %collective-permute-start.8 = (bf16[512,2048]{1,0:T(8,128)(2,1)}, bf16[512,2048]{1,0:T(8,128)(2,1)}, u32[]{:S(2)}, u32[]{:S(2)}) collective-permute-start(bf16[512,2048]{1,0:T(8,128)(2,1)} %fusion.1.refs_0_), channel_id=1, source_target_pairs={{0,8},{8,0},{16,24},{24,16},{1,9},{9,1},{17,25},{25,17},{2,10},{10... | collective-permute-start | bytes 6291464 | tf_op jit(solution)/shard_map/ppermute | solution.py:18
  109.7 46.8 %collective-permute-start.9 = (bf16[512,2048]{1,0:T(8,128)(2,1)}, bf16[512,2048]{1,0:T(8,128)(2,1)}, u32[]{:S(2)}, u32[]{:S(2)}) collective-permute-start(bf16[512,2048]{1,0:T(8,128)(2,1)} %fusion.1.refs_0_), channel_id=1, source_target_pairs={{0,16},{8,24},{16,0},{24,8},{1,17},{9,25},{17,1},{25,9},{2,18},{10... | collective-permute-start | bytes 6291464 | tf_op jit(solution)/shard_map/ppermute | solution.py:18
  159.8 23.2 %collective-permute-start.10 = (bf16[256,2048]{1,0:T(8,128)(2,1)S(1)}, bf16[256,2048]{1,0:T(8,128)(2,1)S(1)}, u32[]{:S(2)}, u32[]{:S(2)}) collective-permute-start(bf16[256,2048]{1,0:T(8,128)(2,1)S(1)} %get-tuple-element.145), channel_id=1, source_target_pairs={{0,16},{8,24},{16,0},{24,8},{1,17},{9,25},{17,1},{25,9},{2,18},{10... | collective-permute-start | bytes 3145736 | tf_op jit(solution)/shard_map/ppermute | solution.py:18
  160.5 26.7 %collective-permute-start.12 = (bf16[256,2048]{1,0:T(8,128)(2,1)S(1)}, bf16[256,2048]{1,0:T(8,128)(2,1)S(1)}, u32[]{:S(2)}, u32[]{:S(2)}) collective-permute-start(bf16[256,2048]{1,0:T(8,128)(2,1)S(1)} %get-tuple-element.146), channel_id=1, source_target_pairs={{0,8},{8,0},{16,24},{24,16},{1,9},{9,1},{17,25},{25,17},{2,10},{10... | collective-permute-start | bytes 3145736 | tf_op jit(solution)/shard_map/ppermute | solution.py:18
  185.5 49.4 %collective-permute-start.11 = (bf16[512,2048]{1,0:T(8,128)(2,1)}, bf16[512,2048]{1,0:T(8,128)(2,1)}, u32[]{:S(2)}, u32[]{:S(2)}) collective-permute-start(bf16[512,2048]{1,0:T(8,128)(2,1)} %fusion.13), channel_id=1, source_target_pairs={{0,8},{8,0},{16,24},{24,16},{1,9},{9,1},{17,25},{25,17},{2,10},{10... | collective-permute-start | bytes 6291464 | tf_op jit(solution)/shard_map/ppermute | solution.py:18
  189.8 45.1 %collective-permute-start.13 = (bf16[512,2048]{1,0:T(8,128)(2,1)}, bf16[512,2048]{1,0:T(8,128)(2,1)}, u32[]{:S(2)}, u32[]{:S(2)}) collective-permute-start(bf16[512,2048]{1,0:T(8,128)(2,1)} %fusion.14), channel_id=1, source_target_pairs={{0,16},{8,24},{16,0},{24,8},{1,17},{9,25},{17,1},{25,9},{2,18},{10... | collective-permute-start | bytes 6291464 | tf_op jit(solution)/shard_map/ppermute | solution.py:18
  191.8 39.0 %collective-permute-start.14 = (f32[512]{0:T(512)S(1)}, f32[512]{0:T(512)S(1)}, u32[]{:S(2)}, u32[]{:S(2)}) collective-permute-start(f32[512]{0:T(512)S(1)} %bitcast.146), channel_id=1, source_target_pairs={{0,8},{8,0},{16,24},{24,16},{1,9},{9,1},{17,25},{25,17},{2,10},{10... | collective-permute-start | bytes 6152 | tf_op jit(solution)/shard_map/ppermute | solution.py:18
  193.3 41.6 %collective-permute-start.15 = (f32[512]{0:T(512)S(1)}, f32[512]{0:T(512)S(1)}, u32[]{:S(2)}, u32[]{:S(2)}) collective-permute-start(f32[512]{0:T(512)S(1)} %bitcast.147), channel_id=1, source_target_pairs={{0,16},{8,24},{16,0},{24,8},{1,17},{9,25},{17,1},{25,9},{2,18},{10... | collective-permute-start | bytes 6152 | tf_op jit(solution)/shard_map/ppermute | solution.py:18
  193.9 41.0 %collective-permute-start.16 = (f32[512]{0:T(512)S(1)}, f32[512]{0:T(512)S(1)}, u32[]{:S(2)}, u32[]{:S(2)}) collective-permute-start(f32[512]{0:T(512)S(1)} %bitcast.148), channel_id=1, source_target_pairs={{0,24},{8,16},{16,8},{24,0},{1,25},{9,17},{17,9},{25,1},{2,26},{10... | collective-permute-start | bytes 6152 | tf_op jit(solution)/shard_map/ppermute | solution.py:18
  196.3 434.8 %reduce-scatter.6.cloned.1.call-start = ((), (), s32[]{:S(2)}) async-start(), calls=%async_computation.9 | async-start | bytes 6488064 | tf_op jit(solution)/shard_map/reduce_scatter | solution.py:752
  245.1 44.2 %collective-permute-start.17 = (bf16[512,2048]{1,0:T(8,128)(2,1)}, bf16[512,2048]{1,0:T(8,128)(2,1)}, u32[]{:S(2)}, u32[]{:S(2)}) collective-permute-start(bf16[512,2048]{1,0:T(8,128)(2,1)} %get-tuple-element.133.refs_0_), channel_id=1, source_target_pairs={{0,8},{8,0},{16,24},{24,16},{1,9},{9,1},{17,25},{25,17},{2,10},{10... | collective-permute-start | bytes 6291464 | tf_op jit(solution)/shard_map/ppermute | solution.py:18
  245.8 46.1 %collective-permute-start.19 = (bf16[512,2048]{1,0:T(8,128)(2,1)}, bf16[512,2048]{1,0:T(8,128)(2,1)S(1)}, u32[]{:S(2)}, u32[]{:S(2)}) collective-permute-start(bf16[512,2048]{1,0:T(8,128)(2,1)} %get-tuple-element.133.refs_0_), channel_id=1, source_target_pairs={{0,16},{8,24},{16,0},{24,8},{1,17},{9,25},{17,1},{25,9},{2,18},{10... | collective-permute-start | bytes 6291464 | tf_op jit(solution)/shard_map/ppermute | solution.py:18
  290.6 31.5 %collective-permute-start.18 = (bf16[256,2048]{1,0:T(8,128)(2,1)S(1)}, bf16[256,2048]{1,0:T(8,128)(2,1)S(1)}, u32[]{:S(2)}, u32[]{:S(2)}) collective-permute-start(bf16[256,2048]{1,0:T(8,128)(2,1)S(1)} %slice.376), channel_id=1, source_target_pairs={{0,16},{8,24},{16,0},{24,8},{1,17},{9,25},{17,1},{25,9},{2,18},{10... | collective-permute-start | bytes 3145736 | tf_op jit(solution)/shard_map/ppermute | solution.py:18
  292.0 30.1 %collective-permute-start.20 = (bf16[256,2048]{1,0:T(8,128)(2,1)S(1)}, bf16[256,2048]{1,0:T(8,128)(2,1)S(1)}, u32[]{:S(2)}, u32[]{:S(2)}) collective-permute-start(bf16[256,2048]{1,0:T(8,128)(2,1)S(1)} %slice.377), channel_id=1, source_target_pairs={{0,8},{8,0},{16,24},{24,16},{1,9},{9,1},{17,25},{25,17},{2,10},{10... | collective-permute-start | bytes 3145736 | tf_op jit(solution)/shard_map/ppermute | solution.py:18
  323.5 27.9 %collective-permute-start.21 = (bf16[256,2048]{1,0:T(8,128)(2,1)S(1)}, bf16[256,2048]{1,0:T(8,128)(2,1)S(1)}, u32[]{:S(2)}, u32[]{:S(2)}) collective-permute-start(bf16[256,2048]{1,0:T(8,128)(2,1)S(1)} %slice.296), channel_id=1, source_target_pairs={{0,16},{8,24},{16,0},{24,8},{1,17},{9,25},{17,1},{25,9},{2,18},{10... | collective-permute-start | bytes 3145736 | tf_op jit(solution)/shard_map/ppermute | solution.py:18
  324.9 27.6 %collective-permute-start.22 = (bf16[256,2048]{1,0:T(8,128)(2,1)S(1)}, bf16[256,2048]{1,0:T(8,128)(2,1)S(1)}, u32[]{:S(2)}, u32[]{:S(2)}) collective-permute-start(bf16[256,2048]{1,0:T(8,128)(2,1)S(1)} %slice.297), channel_id=1, source_target_pairs={{0,8},{8,0},{16,24},{24,16},{1,9},{9,1},{17,25},{25,17},{2,10},{10... | collective-permute-start | bytes 3145736 | tf_op jit(solution)/shard_map/ppermute | solution.py:18
  371.7 268.9 %reduce-scatter.10.cloned.1.call-start = ((), (), s32[]{:S(2)}) async-start(), calls=%async_computation.11 | async-start | bytes 6488064 | tf_op jit(solution)/shard_map/reduce_scatter | solution.py:752
  392.8 47.8 %collective-permute-start.23 = (bf16[256,2048]{1,0:T(8,128)(2,1)S(1)}, bf16[256,2048]{1,0:T(8,128)(2,1)S(1)}, u32[]{:S(2)}, u32[]{:S(2)}) collective-permute-start(bf16[256,2048]{1,0:T(8,128)(2,1)S(1)} %get-tuple-element.144), channel_id=1, source_target_pairs={{0,8},{8,0},{16,24},{24,16},{1,9},{9,1},{17,25},{25,17},{2,10},{10... | collective-permute-start | bytes 3145736 | tf_op jit(solution)/shard_map/ppermute | solution.py:18
  393.3 47.3 %collective-permute-start.24 = (bf16[256,2048]{1,0:T(8,128)(2,1)S(1)}, bf16[256,2048]{1,0:T(8,128)(2,1)S(1)}, u32[]{:S(2)}, u32[]{:S(2)}) collective-permute-start(bf16[256,2048]{1,0:T(8,128)(2,1)S(1)} %get-tuple-element.143), channel_id=1, source_target_pairs={{0,16},{8,24},{16,0},{24,8},{1,17},{9,25},{17,1},{25,9},{2,18},{10... | collective-permute-start | bytes 3145736 | tf_op jit(solution)/shard_map/ppermute | solution.py:18
  395.5 45.0 %collective-permute-start.25 = (bf16[256,2048]{1,0:T(8,128)(2,1)S(1)}, bf16[256,2048]{1,0:T(8,128)(2,1)S(1)}, u32[]{:S(2)}, u32[]{:S(2)}) collective-permute-start(bf16[256,2048]{1,0:T(8,128)(2,1)S(1)} %get-tuple-element.142), channel_id=1, source_target_pairs={{0,8},{8,0},{16,24},{24,16},{1,9},{9,1},{17,25},{25,17},{2,10},{10... | collective-permute-start | bytes 3145736 | tf_op jit(solution)/shard_map/ppermute | solution.py:18
  395.9 44.7 %collective-permute-start.26 = (bf16[256,2048]{1,0:T(8,128)(2,1)S(1)}, bf16[256,2048]{1,0:T(8,128)(2,1)S(1)}, u32[]{:S(2)}, u32[]{:S(2)}) collective-permute-start(bf16[256,2048]{1,0:T(8,128)(2,1)S(1)} %get-tuple-element.141), channel_id=1, source_target_pairs={{0,16},{8,24},{16,0},{24,8},{1,17},{9,25},{17,1},{25,9},{2,18},{10... | collective-permute-start | bytes 3145736 | tf_op jit(solution)/shard_map/ppermute | solution.py:18
  444.0 42.5 %collective-permute-start.27 = (bf16[512,2048]{1,0:T(8,128)(2,1)}, bf16[512,2048]{1,0:T(8,128)(2,1)}, u32[]{:S(2)}, u32[]{:S(2)}) collective-permute-start(bf16[512,2048]{1,0:T(8,128)(2,1)} %fusion.15), channel_id=1, source_target_pairs={{0,8},{8,0},{16,24},{24,16},{1,9},{9,1},{17,25},{25,17},{2,10},{10... | collective-permute-start | bytes 6291464 | tf_op jit(solution)/shard_map/ppermute | solution.py:18
  447.1 41.6 %collective-permute-start.28 = (bf16[512,2048]{1,0:T(8,128)(2,1)}, bf16[512,2048]{1,0:T(8,128)(2,1)}, u32[]{:S(2)}, u32[]{:S(2)}) collective-permute-start(bf16[512,2048]{1,0:T(8,128)(2,1)} %fusion.16), channel_id=1, source_target_pairs={{0,16},{8,24},{16,0},{24,8},{1,17},{9,25},{17,1},{25,9},{2,18},{10... | collective-permute-start | bytes 6291464 | tf_op jit(solution)/shard_map/ppermute | solution.py:18
  515.4 190.8 %reduce-scatter.8.cloned.1.call-start = ((), (), s32[]{:S(2)}) async-start(), calls=%async_computation.10 | async-start | bytes 6488064 | tf_op jit(solution)/shard_map/reduce_scatter | solution.py:752
  516.1 297.2 %reduce-scatter.12.cloned.1.call-start = ((), (), s32[]{:S(2)}) async-start(), calls=%async_computation.12 | async-start | bytes 2359296 | tf_op jit(solution)/shard_map/reduce_scatter | solution.py:752
  516.2 41.3 %collective-permute-start.29 = (bf16[512,2048]{1,0:T(8,128)(2,1)S(1)}, bf16[512,2048]{1,0:T(8,128)(2,1)S(1)}, u32[]{:S(2)}, u32[]{:S(2)}) collective-permute-start(bf16[512,2048]{1,0:T(8,128)(2,1)S(1)} %get-tuple-element.113), channel_id=1, source_target_pairs={{0,8},{8,0},{16,24},{24,16},{1,9},{9,1},{17,25},{25,17},{2,10},{10... | collective-permute-start | bytes 6291464 | tf_op jit(solution)/shard_map/ppermute | solution.py:18
  516.7 42.7 %collective-permute-start.30 = (bf16[512,2048]{1,0:T(8,128)(2,1)S(1)}, bf16[512,2048]{1,0:T(8,128)(2,1)S(1)}, u32[]{:S(2)}, u32[]{:S(2)}) collective-permute-start(bf16[512,2048]{1,0:T(8,128)(2,1)S(1)} %get-tuple-element.113), channel_id=1, source_target_pairs={{0,16},{8,24},{16,0},{24,8},{1,17},{9,25},{17,1},{25,9},{2,18},{10... | collective-permute-start | bytes 6291464 | tf_op jit(solution)/shard_map/ppermute | solution.py:18
  560.5 22.7 %collective-permute-start.31 = (bf16[256,2048]{1,0:T(8,128)(2,1)}, bf16[256,2048]{1,0:T(8,128)(2,1)}, u32[]{:S(2)}, u32[]{:S(2)}) collective-permute-start(bf16[256,2048]{1,0:T(8,128)(2,1)} %slice.304), channel_id=1, source_target_pairs={{0,16},{8,24},{16,0},{24,8},{1,17},{9,25},{17,1},{25,9},{2,18},{10... | collective-permute-start | bytes 3145736 | tf_op jit(solution)/shard_map/ppermute | solution.py:18
  563.4 19.9 %collective-permute-start.32 = (bf16[256,2048]{1,0:T(8,128)(2,1)}, bf16[256,2048]{1,0:T(8,128)(2,1)}, u32[]{:S(2)}, u32[]{:S(2)}) collective-permute-start(bf16[256,2048]{1,0:T(8,128)(2,1)} %slice.305), channel_id=1, source_target_pairs={{0,8},{8,0},{16,24},{24,16},{1,9},{9,1},{17,25},{25,17},{2,10},{10... | collective-permute-start | bytes 3145736 | tf_op jit(solution)/shard_map/ppermute | solution.py:18
  566.1 14.8 %collective-permute-start.35 = (f32[512]{0:T(512)S(1)}, f32[512]{0:T(512)S(1)}, u32[]{:S(2)}, u32[]{:S(2)}) collective-permute-start(f32[512]{0:T(512)S(1)} %multiply_multiply_fusion.1), channel_id=1, source_target_pairs={{0,8},{8,0},{16,24},{24,16},{1,9},{9,1},{17,25},{25,17},{2,10},{10... | collective-permute-start | bytes 6152 | tf_op jit(solution)/shard_map/ppermute | solution.py:18
  566.1 14.8 %collective-permute-start.36 = (f32[512]{0:T(512)S(1)}, f32[512]{0:T(512)S(1)}, u32[]{:S(2)}, u32[]{:S(2)}) collective-permute-start(f32[512]{0:T(512)S(1)} %multiply_multiply_fusion.1), channel_id=1, source_target_pairs={{0,16},{8,24},{16,0},{24,8},{1,17},{9,25},{17,1},{25,9},{2,18},{10... | collective-permute-start | bytes 6152 | tf_op jit(solution)/shard_map/ppermute | solution.py:18
  566.8 14.1 %collective-permute-start.37 = (f32[512]{0:T(512)S(1)}, f32[512]{0:T(512)S(1)}, u32[]{:S(2)}, u32[]{:S(2)}) collective-permute-start(f32[512]{0:T(512)S(1)} %multiply_multiply_fusion.1), channel_id=1, source_target_pairs={{0,24},{8,16},{16,8},{24,0},{1,25},{9,17},{17,9},{25,1},{2,26},{10... | collective-permute-start | bytes 6152 | tf_op jit(solution)/shard_map/ppermute | solution.py:18
  585.0 43.0 %collective-permute-start.33 = (bf16[512,2048]{1,0:T(8,128)(2,1)S(1)}, bf16[512,2048]{1,0:T(8,128)(2,1)S(1)}, u32[]{:S(2)}, u32[]{:S(2)}) collective-permute-start(bf16[512,2048]{1,0:T(8,128)(2,1)S(1)} %fusion.17), channel_id=1, source_target_pairs={{0,8},{8,0},{16,24},{24,16},{1,9},{9,1},{17,25},{25,17},{2,10},{10... | collective-permute-start | bytes 6291464 | tf_op jit(solution)/shard_map/ppermute | solution.py:18
  590.3 37.7 %collective-permute-start.34 = (bf16[512,2048]{1,0:T(8,128)(2,1)}, bf16[512,2048]{1,0:T(8,128)(2,1)S(1)}, u32[]{:S(2)}, u32[]{:S(2)}) collective-permute-start(bf16[512,2048]{1,0:T(8,128)(2,1)} %fusion.18), channel_id=1, source_target_pairs={{0,16},{8,24},{16,0},{24,8},{1,17},{9,25},{17,1},{25,9},{2,18},{10... | collective-permute-start | bytes 6291464 | tf_op jit(solution)/shard_map/ppermute | solution.py:18
  640.6 200.6 %reduce-scatter.14.cloned.1.call-start = ((), (), s32[]{:S(2)}) async-start(), calls=%async_computation.13 | async-start | bytes 9437184 | tf_op jit(solution)/shard_map/reduce_scatter | solution.py:752
  666.1 17.6 %collective-permute-start.38 = (bf16[176,2048]{1,0:T(8,128)(2,1)S(1)}, bf16[176,2048]{1,0:T(8,128)(2,1)S(1)}, u32[]{:S(2)}, u32[]{:S(2)}) collective-permute-start(bf16[176,2048]{1,0:T(8,128)(2,1)S(1)} %copy-done.44), channel_id=1, source_target_pairs={{0,8},{8,0},{16,24},{24,16},{1,9},{9,1},{17,25},{25,17},{2,10},{10... | collective-permute-start | bytes 2162696 | tf_op jit(solution)/shard_map/ppermute | solution.py:18
  666.2 14.8 %collective-permute-start.39 = (bf16[176,2048]{1,0:T(8,128)(2,1)S(1)}, bf16[176,2048]{1,0:T(8,128)(2,1)S(1)}, u32[]{:S(2)}, u32[]{:S(2)}) collective-permute-start(bf16[176,2048]{1,0:T(8,128)(2,1)S(1)} %copy-done.44), channel_id=1, source_target_pairs={{0,16},{8,24},{16,0},{24,8},{1,17},{9,25},{17,1},{25,9},{2,18},{10... | collective-permute-start | bytes 2162696 | tf_op jit(solution)/shard_map/ppermute | solution.py:18
  681.8 55.9 %collective-permute-start.59 = (bf16[96,2048]{1,0:T(8,128)(2,1)}, bf16[96,2048]{1,0:T(8,128)(2,1)S(1)}, u32[]{:S(2)}, u32[]{:S(2)}) collective-permute-start(bf16[96,2048]{1,0:T(8,128)(2,1)} %slice.419), channel_id=1, source_target_pairs={{0,8},{8,0},{16,24},{24,16},{1,9},{9,1},{17,25},{25,17},{2,10},{10... | collective-permute-start | bytes 1179656 | tf_op jit(solution)/shard_map/ppermute | solution.py:18
  684.6 53.1 %collective-permute-start.58 = (bf16[80,2048]{1,0:T(8,128)(2,1)}, bf16[80,2048]{1,0:T(8,128)(2,1)}, u32[]{:S(2)}, u32[]{:S(2)}) collective-permute-start(bf16[80,2048]{1,0:T(8,128)(2,1)} %slice.418), channel_id=1, source_target_pairs={{0,16},{8,24},{16,0},{24,8},{1,17},{9,25},{17,1},{25,9},{2,18},{10... | collective-permute-start | bytes 983048 | tf_op jit(solution)/shard_map/ppermute | solution.py:18
  706.4 26.1 %collective-permute-start.40 = (bf16[256,2048]{1,0:T(8,128)(2,1)S(1)}, bf16[256,2048]{1,0:T(8,128)(2,1)S(1)}, u32[]{:S(2)}, u32[]{:S(2)}) collective-permute-start(bf16[256,2048]{1,0:T(8,128)(2,1)S(1)} %get-tuple-element.139), channel_id=1, source_target_pairs={{0,16},{8,24},{16,0},{24,8},{1,17},{9,25},{17,1},{25,9},{2,18},{10... | collective-permute-start | bytes 3145736 | tf_op jit(solution)/shard_map/ppermute | solution.py:18
  707.9 26.1 %collective-permute-start.42 = (bf16[256,2048]{1,0:T(8,128)(2,1)S(1)}, bf16[256,2048]{1,0:T(8,128)(2,1)S(1)}, u32[]{:S(2)}, u32[]{:S(2)}) collective-permute-start(bf16[256,2048]{1,0:T(8,128)(2,1)S(1)} %get-tuple-element.140), channel_id=1, source_target_pairs={{0,8},{8,0},{16,24},{24,16},{1,9},{9,1},{17,25},{25,17},{2,10},{10... | collective-permute-start | bytes 3145736 | tf_op jit(solution)/shard_map/ppermute | solution.py:18
  733.0 45.5 %collective-permute-start.41 = (bf16[512,2048]{1,0:T(8,128)(2,1)S(1)}, bf16[512,2048]{1,0:T(8,128)(2,1)S(1)}, u32[]{:S(2)}, u32[]{:S(2)}) collective-permute-start(bf16[512,2048]{1,0:T(8,128)(2,1)S(1)} %fusion.19), channel_id=1, source_target_pairs={{0,8},{8,0},{16,24},{24,16},{1,9},{9,1},{17,25},{25,17},{2,10},{10... | collective-permute-start | bytes 6291464 | tf_op jit(solution)/shard_map/ppermute | solution.py:18
  734.5 45.9 %collective-permute-start.43 = (bf16[512,2048]{1,0:T(8,128)(2,1)S(1)}, bf16[512,2048]{1,0:T(8,128)(2,1)S(1)}, u32[]{:S(2)}, u32[]{:S(2)}) collective-permute-start(bf16[512,2048]{1,0:T(8,128)(2,1)S(1)} %fusion.20), channel_id=1, source_target_pairs={{0,16},{8,24},{16,0},{24,8},{1,17},{9,25},{17,1},{25,9},{2,18},{10... | collective-permute-start | bytes 6291464 | tf_op jit(solution)/shard_map/ppermute | solution.py:18
  740.1 68.9 %collective-permute-start.44 = (bf16[352,2048]{1,0:T(8,128)(2,1)S(1)}, bf16[352,2048]{1,0:T(8,128)(2,1)S(1)}, u32[]{:S(2)}, u32[]{:S(2)}) collective-permute-start(bf16[352,2048]{1,0:T(8,128)(2,1)S(1)} %pad_maximum_fusion.1), channel_id=1, source_target_pairs={{0,8},{8,0},{16,24},{24,16},{1,9},{9,1},{17,25},{25,17},{2,10},{10... | collective-permute-start | bytes 4325384 | tf_op jit(solution)/shard_map/ppermute | solution.py:18
  742.1 65.2 %collective-permute-start.45 = (bf16[352,2048]{1,0:T(8,128)(2,1)S(1)}, bf16[352,2048]{1,0:T(8,128)(2,1)S(1)}, u32[]{:S(2)}, u32[]{:S(2)}) collective-permute-start(bf16[352,2048]{1,0:T(8,128)(2,1)S(1)} %pad_maximum_fusion.1), channel_id=1, source_target_pairs={{0,16},{8,24},{16,0},{24,8},{1,17},{9,25},{17,1},{25,9},{2,18},{10... | collective-permute-start | bytes 4325384 | tf_op jit(solution)/shard_map/ppermute | solution.py:18
  808.2 19.2 %collective-permute-start.57 = (bf16[176,2048]{1,0:T(8,128)(2,1)}, bf16[176,2048]{1,0:T(8,128)(2,1)}, u32[]{:S(2)}, u32[]{:S(2)}) collective-permute-start(bf16[176,2048]{1,0:T(8,128)(2,1)} %slice.417), channel_id=1, source_target_pairs={{0,8},{8,0},{16,24},{24,16},{1,9},{9,1},{17,25},{25,17},{2,10},{10... | collective-permute-start | bytes 2162696 | tf_op jit(solution)/shard_map/ppermute | solution.py:18
  809.1 25.9 %collective-permute-start.56 = (bf16[176,2048]{1,0:T(8,128)(2,1)S(1)}, bf16[176,2048]{1,0:T(8,128)(2,1)S(1)}, u32[]{:S(2)}, u32[]{:S(2)}) collective-permute-start(bf16[176,2048]{1,0:T(8,128)(2,1)S(1)} %slice.414), channel_id=1, source_target_pairs={{0,16},{8,24},{16,0},{24,8},{1,17},{9,25},{17,1},{25,9},{2,18},{10... | collective-permute-start | bytes 2162696 | tf_op jit(solution)/shard_map/ppermute | solution.py:18
  813.3 19.6 %collective-permute-start.52 = (bf16[256,512]{1,0:T(8,128)(2,1)}, bf16[256,512]{1,0:T(8,128)(2,1)S(1)}, u32[]{:S(2)}, u32[]{:S(2)}) collective-permute-start(bf16[256,512]{1,0:T(8,128)(2,1)} %reduce-scatter.12.cloned.1.call-done), channel_id=1, source_target_pairs={{0,8},{8,0},{16,24},{24,16},{1,9},{9,1},{17,25},{25,17},{2,10},{10... | collective-permute-start | bytes 786440 | tf_op jit(solution)/shard_map/ppermute | solution.py:18
  814.8 18.9 %collective-permute-start.54 = (bf16[256,512]{1,0:T(8,128)(2,1)}, bf16[256,512]{1,0:T(8,128)(2,1)S(1)}, u32[]{:S(2)}, u32[]{:S(2)}) collective-permute-start(bf16[256,512]{1,0:T(8,128)(2,1)} %reduce-scatter.12.cloned.1.call-done), channel_id=1, source_target_pairs={{0,16},{8,24},{16,0},{24,8},{1,17},{9,25},{17,1},{25,9},{2,18},{10... | collective-permute-start | bytes 786440 | tf_op jit(solution)/shard_map/ppermute | solution.py:18
  841.2 15.1 %collective-permute-start.47 = (bf16[256,2048]{1,0:T(8,128)(2,1)}, bf16[256,2048]{1,0:T(8,128)(2,1)S(1)}, u32[]{:S(2)}, u32[]{:S(2)}) collective-permute-start(bf16[256,2048]{1,0:T(8,128)(2,1)} %reduce-scatter.14.cloned.1.call-done), channel_id=1, source_target_pairs={{0,8},{8,0},{16,24},{24,16},{1,9},{9,1},{17,25},{25,17},{2,10},{10... | collective-permute-start | bytes 3145736 | tf_op jit(solution)/shard_map/ppermute | solution.py:18
  842.5 15.2 %collective-permute-start.46 = (bf16[256,2048]{1,0:T(8,128)(2,1)}, bf16[256,2048]{1,0:T(8,128)(2,1)S(1)}, u32[]{:S(2)}, u32[]{:S(2)}) collective-permute-start(bf16[256,2048]{1,0:T(8,128)(2,1)} %reduce-scatter.14.cloned.1.call-done), channel_id=1, source_target_pairs={{0,16},{8,24},{16,0},{24,8},{1,17},{9,25},{17,1},{25,9},{2,18},{10... | collective-permute-start | bytes 3145736 | tf_op jit(solution)/shard_map/ppermute | solution.py:18
  856.4 9.2 %collective-permute-start.48 = (bf16[128,2048]{1,0:T(8,128)(2,1)S(1)}, bf16[128,2048]{1,0:T(8,128)(2,1)S(1)}, u32[]{:S(2)}, u32[]{:S(2)}) collective-permute-start(bf16[128,2048]{1,0:T(8,128)(2,1)S(1)} %slice.380), channel_id=1, source_target_pairs={{0,16},{8,24},{16,0},{24,8},{1,17},{9,25},{17,1},{25,9},{2,18},{10... | collective-permute-start | bytes 1572872 | tf_op jit(solution)/shard_map/ppermute | solution.py:18
  858.8 12.7 %collective-permute-start.50 = (bf16[256,2048]{1,0:T(8,128)(2,1)S(1)}, bf16[256,2048]{1,0:T(8,128)(2,1)S(1)}, u32[]{:S(2)}, u32[]{:S(2)}) collective-permute-start(bf16[256,2048]{1,0:T(8,128)(2,1)S(1)} %broadcast_select_fusion.1), channel_id=1, source_target_pairs={{0,1},{1,0},{2,3},{3,2},{4,5},{5,4},{6,7},{7,6},{8,9},{9,8},{10,11... | collective-permute-start | bytes 3145736 | tf_op jit(solution)/shard_map/ppermute | solution.py:23
  (72 other events, 776.5 us)
Sparse Core Ops, SparseCore 0:
  20.0 85.5 all-gather.4
  107.7 29.3 all-gather.6
  139.4 107.1 all-gather.8
  248.7 58.6 all-gather.10
  371.8 65.3 reduce-scatter.5
  515.5 65.0 reduce-scatter.9
  583.5 63.2 reduce-scatter.7
  649.6 34.2 reduce-scatter.11
  686.2 88.3 reduce-scatter.13

commit v3 on v2

--- a/solution.py
+++ b/solution.py
@@ -46,20 +46,22 @@
     return spread_far(spread_near(x))
 
 
+def halves(rows):
+    cut = halfway(rows)
+    return [slice(0, cut), slice(cut, rows)] if lax.axis_size("seq") == 4 else [slice(0, rows)]
+
+
 def collect_far(part):
     if lax.axis_size("seq") != 4:
         return ()
-    cut = halfway(part.shape[0])
-    return swap_seq(part[:cut], 1), swap_seq(part[cut:], 2)
-
-
-def collect_near(parts, passed):
+    top, rest = part
+    return swap_seq(top, 1), swap_seq(rest, 2)
+
+
+def join_near(parts, passed):
     wide = lambda x: x.astype(F32)
     if not passed:
-        total = wide(parts[0])
-        for i in range(1, len(parts)):
-            total = total + wide(swap_seq(parts[i], i))
-        return total
+        return [part[0] if isinstance(part, list) else part for part in parts[1:]]
     by_x, by_y = passed
     cut = by_x.shape[0]
     to_x = lax.dynamic_update_slice_in_dim(
@@ -68,7 +70,18 @@
     to_y = lax.dynamic_update_slice_in_dim(
         parts[2], (wide(parts[2][:cut]) + wide(by_x)).astype(LOW), 0, 0
     )
-    return wide(parts[0]) + wide(swap_seq(to_x, 1)) + wide(swap_seq(to_y, 2))
+    return [to_x, to_y]
+
+
+def collect_joined(own, joined):
+    total = own.astype(F32)
+    for i, part in enumerate(joined):
+        total = total + swap_seq(part, i + 1).astype(F32)
+    return total
+
+
+def collect_near(parts, passed):
+    return collect_joined(parts[0], join_near(parts, passed))
 
 
 def after(value, *others):
@@ -397,8 +410,10 @@
     sides, down_ref = refs[inputs : inputs + 2]
     saved = refs[inputs + 2 : inputs + 5]
     kept = refs[refs_in : refs_in + 2]
-    head_ref, out_ref = refs[refs_in + 2 : refs_in + 4]
-    gs, left, right, down, low_left, low_right, prod, gl, gr, hs, fs = refs[refs_in + 4 : -5]
+    outs = len(refs) - refs_in - 18
+    head_refs = refs[refs_in + 2 : refs_in + 2 + outs // 2]
+    out_refs = refs[refs_in + 2 + outs // 2 : refs_in + 2 + outs]
+    gs, left, right, down, low_left, low_right, prod, gl, gr, hs, fs = refs[refs_in + 2 + outs : -5]
     row_sem, down_sem, side_sem, prod_sem, out_sem = refs[-5:]
     hidden, feat = left.shape
     spans = [(n, n * WIDE) for n in range(feat // WIDE)]
@@ -428,9 +443,18 @@
         ]
 
     def store_wide(k, n, start):
-        source, to = ((hs, head_ref), (fs, out_ref))[k]
+        source, targets = ((hs, head_refs), (fs, out_refs))[k]
         here = pl.ds(start, WIDE)
-        return pltpu.make_async_copy(source.at[:, here], to.at[:, here], out_sem.at[2 + k, n])
+        copies, first = [], 0
+        for part, to in enumerate(targets):
+            rows = pl.ds(first, to.shape[0])
+            copies.append(
+                pltpu.make_async_copy(
+                    source.at[rows, here], to.at[:, here], out_sem.at[2 + 2 * k + part, n]
+                )
+            )
+            first += to.shape[0]
+        return copies
 
     loads = row_copies(rows, gs, row_sem, 0)
     load_prod = pltpu.make_async_copy(saved[2].at[piece], prod, prod_sem)
@@ -463,7 +487,8 @@
         start = pl.multiple_of(n * WIDE, WIDE)
         here = pl.ds(start, WIDE)
         fs[:, here] = dot_nn(prod[...], down[:, here]).astype(LOW)
-        store_wide(1, n, start).start()
+        for copy in store_wide(1, n, start):
+            copy.start()
         return carry
 
     lax.fori_loop(0, len(spans), outs, 0)
@@ -474,7 +499,8 @@
         for copy in fetch_sides(n, start):
             copy.wait()
         hs[:, here] = (dot_nn(gl[...], left[:, here]) + dot_nn(gr[...], right[:, here])).astype(LOW)
-        store_wide(0, n, start).start()
+        for copy in store_wide(0, n, start):
+            copy.start()
         return carry
 
     lax.fori_loop(0, len(spans), heads, 0)
@@ -482,8 +508,8 @@
         for copy in store(c, start, length):
             copy.wait()
     for n, start in spans:
-        store_wide(1, n, start).wait()
-        store_wide(0, n, start).wait()
+        for copy in store_wide(1, n, start) + store_wide(0, n, start):
+            copy.wait()
 
 
 def unit_forward(piece, size, rows, sides, kept):
@@ -536,12 +562,13 @@
     wide = pltpu.VMEM((count, feat), LOW)
     side = pltpu.VMEM((hidden, feat), LOW)
     inner = pltpu.VMEM((count, hidden), LOW)
+    spans = halves(count) if piece == size - 1 else [slice(0, count)]
+    pieces = [jax.ShapeDtypeStruct((span.stop - span.start, feat), LOW) for span in spans]
     outs = pl.pallas_call(
         functools.partial(unit_backward_kernel, piece, len(rows), len(inputs)),
         in_specs=[anywhere] * len(inputs),
-        out_specs=[anywhere] * 4,
-        out_shape=[jax.ShapeDtypeStruct((size, count, hidden), LOW)] * 2
-        + [jax.ShapeDtypeStruct((count, feat), LOW)] * 2,
+        out_specs=[anywhere] * (2 + 2 * len(pieces)),
+        out_shape=[jax.ShapeDtypeStruct((size, count, hidden), LOW)] * 2 + pieces * 2,
         input_output_aliases=aliases,
         scratch_shapes=[
             wide,
@@ -559,7 +586,7 @@
             pltpu.SemaphoreType.DMA((3, parts)),
             pltpu.SemaphoreType.DMA((2, feat // WIDE)),
             pltpu.SemaphoreType.DMA,
-            pltpu.SemaphoreType.DMA((4, max(parts, feat // WIDE))),
+            pltpu.SemaphoreType.DMA((6, max(parts, feat // WIDE))),
         ],
         compiler_params=pltpu.CompilerParams(vmem_limit_bytes=50 << 20),
         cost_estimate=pl.CostEstimate(
@@ -569,7 +596,8 @@
         ),
         name="unit_backward",
     )(*inputs)
-    return outs[:2], outs[2], outs[3]
+    parts = [list(outs[2 : 2 + len(pieces)]), list(outs[2 + len(pieces) :])]
+    return (outs[:2], *(part if piece == size - 1 else part[0] for part in parts))
 
 
 def paired_heads(rows):
@@ -601,9 +629,9 @@
 
 
 def scatter_projections(grad, rows, me_seq, me_fsdp):
-    feat = grad.shape[1]
     size = lax.axis_size("seq")
     if not paired_heads(rows):
+        feat = grad.shape[1]
         parts = grad.reshape(-1, 1, 4, HEAD, feat)
         result = []
         for which in range(4):
@@ -615,22 +643,26 @@
             result.append(lax.psum(part, "seq").astype(F32))
         return result
     core = me_fsdp % 2
-    pieces = [jnp.concatenate(p, 0) for p in spread(grad)]
-    straight = (core ^ (me_seq // 2)) == 0
-    keep = [jnp.where(straight, pieces[j], pieces[2 + j]) for j in range(2)]
-    give = [jnp.where(straight, pieces[2 + j], pieces[j]) for j in range(2)]
+    near = spread_far(grad)
+    far = jnp.concatenate(near[3], 0)
+    pieces = [near[0][0], near[1][0], near[2][0], far]
+    turned = core ^ (me_seq // 2)
+    give = [jnp.where(turned == 0, pieces[2 + j], pieces[j]) for j in range(2)]
     got = [swap_core(g) for g in give]
-    even = me_seq % 2 == 0
-    keep = [jnp.where(even, keep[0], keep[1]), jnp.where(even, keep[1], keep[0])]
-    got = [jnp.where(even, got[0], got[1]), jnp.where(even, got[1], got[0])]
-    first = [jnp.where(core == 0, k, g) for k, g in zip(keep, got)]
-    second = [jnp.where(core == 0, g, k) for k, g in zip(keep, got)]
-    result = []
-    for pair in (first, second):
-        for part in range(2):
-            span = slice(part * HEAD, (part + 1) * HEAD)
-            result.append(jnp.concatenate([p[span] for p in pair], 0).astype(F32))
-    return result
+    feat = far.shape[1]
+    where = jnp.stack([core, turned, me_seq % 2]).astype(jnp.int32)
+    return pl.pallas_call(
+        sort_kernel,
+        in_specs=[pl.BlockSpec(memory_space=pltpu.SMEM)]
+        + [pl.BlockSpec(memory_space=pltpu.VMEM)] * 7,
+        out_specs=[pl.BlockSpec(memory_space=pltpu.VMEM)] * 4,
+        out_shape=[jax.ShapeDtypeStruct((rows, feat), F32)] * 4,
+        compiler_params=pltpu.CompilerParams(vmem_limit_bytes=40 << 20),
+        cost_estimate=pl.CostEstimate(
+            flops=0, bytes_accessed=24 * rows * feat, transcendentals=0
+        ),
+        name="sort_rows",
+    )(where, *pieces[:3], *near[3], *got)
 
 
 def in_order(pieces, me_seq):
@@ -645,19 +677,96 @@
     return [stack[i] for i in range(size)]
 
 
+def place_kernel(groups, s_ref, *refs):
+    out_ref = refs[-1]
+    step = pl.program_id(0)
+    first = 0
+    for i, group in enumerate(groups):
+        parts = refs[first : first + group]
+        first += group
+
+        @pl.when(step == i)
+        def _(parts=parts):
+            start = 0
+            for part in parts:
+                rows = part.shape[0]
+                out_ref[start : start + rows] = part[...].astype(F32)
+                start += rows
+
+
 def place_rows(pieces, me_seq, count):
-    pieces = [jnp.concatenate(p, 0) if len(p) > 1 else p[0] for p in pieces]
-    rows, feat = pieces[0].shape
-    rows //= count
+    size = len(pieces)
+    total, feat = pieces[0][0].shape
+    rows = total // count
     result = []
+    if rows % 16:
+        pieces = [jnp.concatenate(parts, 0) for parts in pieces]
+        for n in range(count):
+            out = jnp.zeros((rows * size, feat), F32)
+            for i, piece in enumerate(pieces):
+                part = piece[n * rows : (n + 1) * rows].astype(F32)
+                out = lax.dynamic_update_slice_in_dim(out, part, (me_seq ^ i) * rows, 0)
+            result.append(out)
+        return result
     for n in range(count):
-        out = jnp.zeros((rows * len(pieces), feat), F32)
-        for i, piece in enumerate(pieces):
-            out = lax.dynamic_update_slice_in_dim(
-                out, piece[n * rows : (n + 1) * rows].astype(F32), (me_seq ^ i) * rows, 0
-            )
-        result.append(out)
+        inputs, specs, groups = [], [], []
+        for parts in pieces:
+            if len(parts) == count > 1:
+                parts = parts[n : n + 1]
+                chosen = [(parts[0], 0)]
+            elif len(parts) == 1:
+                chosen = [(parts[0], n)]
+            else:
+                chosen = [(part, 0) for part in parts]
+            groups.append(len(chosen))
+            for part, block in chosen:
+                length = rows if len(chosen) == 1 else part.shape[0]
+                inputs.append(part)
+                specs.append(pl.BlockSpec((length, feat), lambda i, s, block=block: (block, 0)))
+        result.append(
+            pl.pallas_call(
+                functools.partial(place_kernel, groups),
+                grid_spec=pltpu.PrefetchScalarGridSpec(
+                    num_scalar_prefetch=1,
+                    grid=(size,),
+                    in_specs=specs,
+                    out_specs=pl.BlockSpec(
+                        (rows, feat), lambda i, s: (lax.bitwise_xor(i, s[0]), 0)
+                    ),
+                ),
+                out_shape=jax.ShapeDtypeStruct((rows * size, feat), F32),
+                compiler_params=pltpu.CompilerParams(
+                    dimension_semantics=("arbitrary",), vmem_limit_bytes=24 << 20
+                ),
+                cost_estimate=pl.CostEstimate(
+                    flops=0, bytes_accessed=6 * rows * size * feat, transcendentals=0
+                ),
+                name="place_rows",
+            )(me_seq.astype(jnp.int32).reshape(1), *inputs)
+        )
     return result
+
+
+def sort_kernel(where_ref, *refs):
+    core, turned, odd = where_ref[0], where_ref[1], where_ref[2]
+    pieces = refs[:3] + (refs[3:5],)
+    got = refs[5:7]
+    outs = refs[7:]
+
+    def put(out, part, source, which):
+        here = pl.ds(pl.multiple_of(lax.bitwise_xor(jnp.int32(part), odd) * HEAD, HEAD), HEAD)
+        rows = source[which][...] if isinstance(source, tuple) else source[which * HEAD : (which + 1) * HEAD]
+        out[here] = rows.astype(F32)
+
+    for own in range(2):
+        for turn in range(2):
+
+            @pl.when((core == own) & (turned == turn))
+            def _(own=own, turn=turn):
+                for part in range(2):
+                    for which in range(2):
+                        put(outs[2 * own + which], part, pieces[2 * turn + part], which)
+                        put(outs[2 * (1 - own) + which], part, got[part], which)
 
 
 def on_device(
@@ -731,7 +840,11 @@
     ungated, attn, squares = attend(me, pre, down, across)
     ungated = after(ungated.reshape(rows_all, -1), grad_near[1:])
     branch = lambda i: times_rows(cut(ungated, i), out_slice).astype(LOW)
-    branch_parts = [None] * (size - 1) + [branch(size - 1)]
+    far_rows = lambda part, rows: [part(rows[span]) for span in halves(count)]
+    branch_parts = [None] * (size - 1)
+    branch_parts.append(
+        far_rows(lambda rows: times_rows(rows, out_slice).astype(LOW), cut(ungated, size - 1))
+    )
     branch_far = collect_far(branch_parts[-1])
     for i in reversed(range(size - 1)):
         branch_parts[i] = branch(i)
@@ -793,31 +906,44 @@
     grad_pre = attend_back(me, pre, attn, grad_gated, inner, down, across)
     ffn = collect_near([ffn_parts[0]] + after(ffn_parts[1:], branch_pieces[-1]), ffn_far)
     grad_pre = after(grad_pre.reshape(rows_all, -1), ffn, down_mine)
+    layer_out = (valid * (residual + ffn)).astype(LOW).reshape(tokens.shape)
     out_grad = rows_outer(branch_all, after(ungated, grad_pre)).astype(LOW)
     out_mine = own_rows(after(out_grad, right_mine))
-    project_grad = rows_outer(after(grad_pre, out_grad), normed_all).astype(LOW)
+    both_near = spread_near(after(jnp.concatenate([down_mine, right_mine], 0), ffn))
+    project_grad = rows_outer(after(grad_pre, out_grad, both_near), normed_all).astype(LOW)
+    both_pieces = spread_far(both_near)
+    left_near = spread_near(after(left_mine, both_near))
+    normed_part = lambda i, rows: times(cut(rows, i), project).astype(LOW)
+    normed_parts = [None] * (size - 1)
+    normed_parts.append(
+        far_rows(
+            lambda rows: times(rows, project).astype(LOW),
+            cut(after(grad_pre, project_grad, both_pieces), size - 1),
+        )
+    )
+    normed_far = collect_far(normed_parts[-1])
     project_mine = own_rows(project_grad) if paired_heads(query_weight.shape[0]) else project_grad
-    layer_out = (valid * (residual + ffn)).astype(LOW).reshape(tokens.shape)
-
-    down_near = spread_near(after(down_mine, ffn))
-    normed_part = lambda i, rows: times(cut(rows, i), project).astype(LOW)
-    normed_parts = [None] * (size - 1) + [normed_part(size - 1, after(grad_pre, project_grad, down_near))]
-    normed_far = collect_far(after(normed_parts[-1], left_mine))
+    rows = after(grad_pre, normed_parts[-1])
     for i in reversed(range(size - 1)):
-        normed_parts[i] = normed_part(i, after(grad_pre, normed_parts[-1]))
-    grad_normed = collect_near(normed_parts, normed_far)
-    sides_near = spread_near(after(jnp.concatenate([left_mine, right_mine], 0), ffn))
-    grad_normed = after(grad_normed, sides_near, out_mine, project_mine)
+        normed_parts[i] = normed_part(i, rows)
+    left_pieces = spread_far(after(left_near, normed_parts[-1]))
+    normed_parts[1] = after(normed_parts[1], left_pieces, out_mine)
+    normed_joined = join_near(normed_parts, normed_far)
+    grad_normed = collect_joined(normed_parts[0], normed_joined)
+    paired = paired_heads(query_weight.shape[0])
+    project_near = spread_near(project_mine) if paired else project_mine
+    if paired:
+        grad_normed = after(grad_normed, project_near[1:])
+    down_out, right_out = place_rows(after(both_pieces, project_near), me_seq, 2)
+    (left_out,) = place_rows(after(left_pieces, project_near), me_seq, 1)
     input_grad = grad_resid + norm_back(wide, factor_in, grad_normed)
     input_grad = input_grad.astype(LOW).reshape(tokens.shape)
 
-    (down_out,) = place_rows(spread_far(down_near), me_seq, 1)
-    left_out, right_out = place_rows(spread_far(sides_near), me_seq, 2)
 
     query_out, key_out, value_out, outgate_out = scatter_projections(
-        project_mine, query_weight.shape[0], me_seq, me_fsdp
-    )
-    out_pieces = [jnp.concatenate(p, 0) for p in spread(out_mine)]
+        project_near, query_weight.shape[0], me_seq, me_fsdp
+    )
+    out_pieces = [jnp.concatenate(p, 0) for p in spread(after(out_mine, project_near))]
     out_cols = in_order(out_pieces, me_seq)
     out_out = jnp.concatenate(
         [

time: 890 us -> 852 us (0.957)
  waiting for transfers between devices: 306 us -> 272 us
  Pallas kernels: 172 us -> 190 us
  other arithmetic: 83.6 us -> 67 us
  matrix products: 154 us -> 165 us
  local copies, waits for them, and re-layouts: 85.4 us -> 74.6 us
    ppermute x57, waiting for transfers between devices: 305 us -> 249 us  [swap_seq(): return lax.ppermute(x, 'seq', [(i, i ^ bit) for i in range(size)])]
    reduce_scatter x5, waiting for transfers between devices: 0.05 us -> 19.7 us  [own_rows(): return lax.psum_scatter(grad, 'fsdp', scatter_dimension=0, tiled=True)]
    pallas_call x0 -> x4, Pallas kernels: none -> 16.1 us  [the longest x3 11.7 us: place_rows(): pl.pallas_call(functools.partial(place_kernel, groups), grid_spec=pltpu.P...]
    dynamic_update_slice x18 -> x8, other arithmetic: 31.3 us -> 19.9 us  [the longest x4 11.4 us: join_near(): lax.dynamic_update_slice_in_dim(parts[2], (wide(parts[2][:cut]) + wide(by...]
    another operation x6 -> x3, local copies, waits for them, and re-layouts: 9.88 us -> 0.14 us
    dot_general x5 -> x6, matrix products: 34.4 us -> 41.1 us  [times(): lax.dot_general(left_side, weight, (((1,), (0,)), ((), ())), preferred_el...]
    dot_general x5 -> x6, matrix products: 37.5 us -> 39.4 us  [times_rows(): lax.dot_general(left_side, weight, (((1,), (1,)), ((), ())), preferred_el...]
    unnamed x172 -> x163, local copies, waits for them, and re-layouts: 44.3 us -> 44.6 us
  transfers between devices with their start and end apart: 69 -> 69, of which waited for: 28 -> 26; matrix products, arithmetic and copies ran while one was open for 33% -> 34% of each run, Pallas kernels for 19% -> 22%
where the time goes in v3:
time: 852 us; the launch traced here: 847 us
  waiting for transfers between devices  272 us (32%)
  Pallas kernels  190 us (22%)
  matrix products  165 us (19%)
  local copies, waits for them, and re-layouts  74.6 us (9%)
  other arithmetic  67 us (8%)
  starting transfers between devices  63.4 us (7%)
  between operations  15.2 us (2%)
    ppermute x57, waiting for transfers between devices, swap_seq(): return lax.ppermute(x, 'seq', [(i, i ^ bit) for i in range(size)])  249 us
    pallas_call x4, Pallas kernels, unit_backward(): pl.pallas_call(functools.partial(unit_backward_kernel, piece, len(rows),...  84.6 us
    dot_general x5, matrix products, rows_outer(): lax.dot_general(left_side, right_side, (((0,), (0,)), ((), ())), preferre...  84 us
    ppermute x57, starting transfers between devices, swap_seq(): return lax.ppermute(x, 'seq', [(i, i ^ bit) for i in range(size)])  62.1 us
    pallas_call x4, Pallas kernels, unit_forward(): pl.pallas_call(functools.partial(unit_forward_kernel, piece, len(rows), l...  47.2 us
    unnamed x163, local copies, waits for them, and re-layouts  44.6 us
    dot_general x6, matrix products, times(): lax.dot_general(left_side, weight, (((1,), (0,)), ((), ())), preferred_el...  41.1 us
    dot_general x6, matrix products, times_rows(): lax.dot_general(left_side, weight, (((1,), (1,)), ((), ())), preferred_el...  39.4 us
  transfers between devices with their start and end apart: 69, of which 26 were waited for; matrix products, arithmetic and copies ran while one was open for 34% of the time, Pallas kernels for 22%

profile of v3, /device:TPU:0, one launch (start us, length us, event | category | flops | bytes accessed | tf_op | source)
XLA Modules:
  0.0 846.9 jit_solution(3889242313113780327)
XLA Ops:
  14.8 4.0 constant_dynamic-update-slice_fusion.4
  27.2 3.9 collective-permute-start.1
  33.2 2.9 collective-permute-start.6
  36.8 3.3 fusion.1.refs_0_
  40.1 37.8 %collective-permute-done.5 = f32[1,1024]{1,0:T(1,128)S(1)} collective-permute-done((f32[1,1024]{1,0:T(1,128)S(1)}, f32[1,1024]{1,0:T(1,128)S(1)}, u32[]{:S(2)}, u32[]{:S(2)}) %collective-permute-start.5) | collective-permute-done | bytes 4128 | tf_op jit(solution)/shard_map/ppermute | solution.py:18
  85.9 5.1 reduce-window.6
  91.5 3.2 constant_dynamic-update-slice_fusion.3
  94.7 3.2 constant_dynamic-update-slice_fusion.2
  97.9 8.7 %collective-permute-done.3 = bf16[256,2048]{1,0:T(8,128)(2,1)} collective-permute-done((bf16[256,2048]{1,0:T(8,128)(2,1)}, bf16[256,2048]{1,0:T(8,128)(2,1)}, u32[]{:S(2)}, u32[]{:S(2)}) %collective-permute-start.3) | collective-permute-done | bytes 1048608 | tf_op jit(solution)/shard_map/ppermute | solution.py:18
  106.5 3.8 collective-permute-done.2
  115.8 22.3 %convolution_convert_fusion.1 = bf16[2048,2048]{1,0:T(8,128)(2,1)S(1)} fusion(bf16[2048,2048]{1,0:T(8,128)(2,1)} %constant_dynamic-update-slice_fusion, bf16[2048,2048]{1,0:T(8,128)(2,1)} %all-gather.5.cloned.1.call-done), kind=kOutput, calls=%fused_computation.1 | convolution fusion | flops 17184063488 | bytes 25165824 | tf_op jit(solution)/shard_map/dot_general | solution.py:92
  138.7 14.2 %attend.1 = (bf16[4,2,256,512]{3,2,1,0:T(8,128)(2,1)S(1)}, bf16[4,2,256,512]{3,2,1,0:T(8,128)(2,1)S(1)}, f32[4,2,256,128]{3,2,1,0:T(8,128)S(1)}) custom-call(s32[1]{0:T(128)} %bitcast.1.s_ref, bf16[4,2,256,2048]{3,2,1,0:T(8,128)(2,1)S(1)} %bitcast.107, f32[4,4,256,128]{3,2,1,0:T(8,128)S(1)} %broadcast_in_dim.6.down_ref, ...), custom_call_target="tpu_custom_call" | custom-call | flops 2500000000 | bytes 16777216 | tf_op jit(solution)/shard_map/attend/pallas_call | solution.py:254
  154.3 2.6 collective-permute-done.9.refs_0_
  164.4 2.6 convolution_convert_fusion.9
  167.0 2.6 convolution_convert_fusion.10
  169.6 12.9 %collective-permute-done.10 = bf16[256,2048]{1,0:T(8,128)(2,1)S(1)} collective-permute-done((bf16[256,2048]{1,0:T(8,128)(2,1)S(1)}, bf16[256,2048]{1,0:T(8,128)(2,1)S(1)}, u32[]{:S(2)}, u32[]{:S(2)}) %collective-permute-start.10) | collective-permute-done | bytes 1048608 | tf_op jit(solution)/shard_map/ppermute | solution.py:18
  182.5 2.6 fusion.12
  187.3 2.6 fusion.13
  196.7 37.3 %collective-permute-done.15 = f32[512]{0:T(512)S(1)} collective-permute-done((f32[512]{0:T(512)S(1)}, f32[512]{0:T(512)S(1)}, u32[]{:S(2)}, u32[]{:S(2)}) %collective-permute-start.15) | collective-permute-done | bytes 2080 | tf_op jit(solution)/shard_map/ppermute | solution.py:18
  234.1 7.0 multiply_reduce_fusion.2
  247.1 13.2 %unit_forward.4 = (bf16[4,512,1408]{2,1,0:T(8,128)(2,1)S(1)}, bf16[4,512,1408]{2,1,0:T(8,128)(2,1)S(1)}, bf16[4,512,1408]{2,1,0:T(8,128)(2,1)}) custom-call(bf16[512,2048]{1,0:T(8,128)(2,1)} %get-tuple-element.170.refs_0_, bf16[1408,4096]{1,0:T(8,128)(2,1)} %all-gather.9.cloned.1.call-done.refs_1_.refs_2_), custom_call_target="tpu_custom_call" | custom-call | flops 5905580032 | bytes 17956864 | tf_op jit(solution)/shard_map/unit_forward/pallas_call | solution.py:525
  260.3 28.4 %collective-permute-done.19.refs_0_ = bf16[512,2048]{1,0:T(8,128)(2,1)S(1)} collective-permute-done((bf16[512,2048]{1,0:T(8,128)(2,1)}, bf16[512,2048]{1,0:T(8,128)(2,1)S(1)}, u32[]{:S(2)}, u32[]{:S(2)}) %collective-permute-start.19) | collective-permute-done | bytes 2097184 | tf_op jit(solution)/shard_map/ppermute | solution.py:18
  289.0 4.1 collective-permute-done.17.refs_0_
  294.5 3.2 constant_dynamic-update-slice_fusion.13
  299.3 12.7 %unit_forward.5 = (bf16[4,512,1408]{2,1,0:T(8,128)(2,1)S(1)}, bf16[4,512,1408]{2,1,0:T(8,128)(2,1)S(1)}, bf16[4,512,1408]{2,1,0:T(8,128)(2,1)}) custom-call(bf16[512,2048]{1,0:T(8,128)(2,1)} %collective-permute-done.17.refs_0_, ...), custom_call_target="tpu_custom_call", output_to_operand_aliasing={{0}: (2, {}), {1}: (3, {}), {2}: (4, {})} | custom-call | flops 5905580032 | bytes 17956864 | tf_op jit(solution)/shard_map/unit_forward/pallas_call | solution.py:525
  312.1 10.7 %unit_forward.6 = (bf16[4,512,1408]{2,1,0:T(8,128)(2,1)S(1)}, bf16[4,512,1408]{2,1,0:T(8,128)(2,1)S(1)}, bf16[4,512,1408]{2,1,0:T(8,128)(2,1)}) custom-call(bf16[512,2048]{1,0:T(8,128)(2,1)S(1)} %collective-permute-done.19.refs_0_, ...), custom_call_target="tpu_custom_call", output_to_operand_aliasing={{0}: (2, {}), {1}: (3, {}), {2}: (4, {})} | custom-call | flops 5905580032 | bytes 17956864 | tf_op jit(solution)/shard_map/unit_forward/pallas_call | solution.py:525
  337.2 10.6 %unit_forward.7 = (bf16[4,512,1408]{2,1,0:T(8,128)(2,1)S(1)}, bf16[4,512,1408]{2,1,0:T(8,128)(2,1)S(1)}, bf16[4,512,1408]{2,1,0:T(8,128)(2,1)}) custom-call(bf16[256,2048]{1,0:T(8,128)(2,1)S(1)} %collective-permute-done.18.refs_0_, bf16[256,2048]{1,0:T(8,128)(2,1)S(1)} %collective-permute-done.20.refs_1_, ...), custom_call_target="tpu_custom_call", output_to_operand_aliasing={{0}: (3, {}), {1}: (4, {}), {2}: (5, {})} | custom-call | flops 5905580032 | bytes 17956864 | tf_op jit(solution)/shard_map/unit_forward/pallas_call | solution.py:525
  355.3 17.9 %convolution_convert_fusion.4 = bf16[1408,2048]{1,0:T(8,128)(2,1)} fusion(bf16[2048,1408]{1,0:T(8,128)(2,1)} %bitcast.116, bf16[2048,2048]{1,0:T(8,128)(2,1)} %constant_dynamic-update-slice_fusion.5), kind=kOutput, calls=%fused_computation.4 | convolution fusion | flops 11814043648 | bytes 19922944 | tf_op jit(solution)/shard_map/dot_general | solution.py:104
  373.3 20.6 %unit_backward.4 = (bf16[4,512,1408]{2,1,0:T(8,128)(2,1)}, bf16[4,512,1408]{2,1,0:T(8,128)(2,1)}, bf16[256,2048]{1,0:T(8,128)(2,1)S(1)}, bf16[256,2048]{1,0:T(8,...) custom-call(bf16[256,2048]{1,0:T(8,128)(2,1)} %copy-done.46, bf16[256,2048]{1,0:T(8,128)(2,1)} %copy-done.45, ...), custom_call_target="tpu_custom_call" | custom-call | flops 11811160064 | bytes 30801920 | tf_op jit(solution)/shard_map/unit_backward/pallas_call | solution.py:567
  398.0 21.9 %unit_backward.5 = (bf16[4,512,1408]{2,1,0:T(8,128)(2,1)}, bf16[4,512,1408]{2,1,0:T(8,128)(2,1)}, bf16[512,2048]{1,0:T(8,128)(2,1)}, bf16[512,2048]{1,0:T(8,128)(2,1)}) custom-call(bf16[512,2048]{1,0:T(8,128)(2,1)} %collective-permute-done.8.refs_0_, ...), custom_call_target="tpu_custom_call", output_to_operand_aliasing={{0}: (6, {}), {1}: (7, {})} | custom-call | flops 11811160064 | bytes 30801920 | tf_op jit(solution)/shard_map/unit_backward/pallas_call | solution.py:567
  419.9 21.7 %unit_backward.6 = (bf16[4,512,1408]{2,1,0:T(8,128)(2,1)}, bf16[4,512,1408]{2,1,0:T(8,128)(2,1)}, bf16[512,2048]{1,0:T(8,128)(2,1)}, bf16[512,2048]{1,0:T(8,128)(2,1)}) custom-call(bf16[512,2048]{1,0:T(8,128)(2,1)} %collective-permute-done.9.refs_0_, ...), custom_call_target="tpu_custom_call", output_to_operand_aliasing={{0}: (6, {}), {1}: (7, {})} | custom-call | flops 11811160064 | bytes 30801920 | tf_op jit(solution)/shard_map/unit_backward/pallas_call | solution.py:567
  441.7 3.3 fusion.15
  445.1 2.6 fusion.14
  449.3 20.4 %unit_backward.7 = (bf16[4,512,1408]{2,1,0:T(8,128)(2,1)}, bf16[4,512,1408]{2,1,0:T(8,128)(2,1)}, bf16[512,2048]{1,0:T(8,128)(2,1)S(1)}, bf16[512,2048]{1,0:T(8,128)(2,1)}) custom-call(bf16[512,2048]{1,0:T(8,128)(2,1)} %fusion.1.refs_0_, ...), custom_call_target="tpu_custom_call", output_to_operand_aliasing={{0}: (6, {}), {1}: (7, {})} | custom-call | flops 11811160064 | bytes 30801920 | tf_op jit(solution)/shard_map/unit_backward/pallas_call | solution.py:567
  469.8 18.3 %convolution_convert_fusion.3 = bf16[1408,2048]{1,0:T(8,128)(2,1)} fusion(bf16[2048,1408]{1,0:T(8,128)(2,1)} %bitcast.117, bf16[2048,2048]{1,0:T(8,128)(2,1)} %constant_dynamic-update-slice_fusion.10), kind=kOutput, calls=%fused_computation.3 | convolution fusion | flops 11814043648 | bytes 19922944 | tf_op jit(solution)/shard_map/dot_general | solution.py:104
  488.1 3.6 convert_add_fusion.2
  494.0 6.3 multiply_reduce_fusion
  500.5 14.0 %convolution_convert_fusion.2 = bf16[1408,2048]{1,0:T(8,128)(2,1)} fusion(bf16[2048,1408]{1,0:T(8,128)(2,1)S(1)} %bitcast.120, bf16[2048,2048]{1,0:T(8,128)(2,1)S(1)} %bitcast.132), kind=kOutput, calls=%fused_computation.2 | convolution fusion | flops 11814043648 | bytes 19922944 | tf_op jit(solution)/shard_map/dot_general | solution.py:104
  517.9 38.6 %collective-permute-done.30 = bf16[512,2048]{1,0:T(8,128)(2,1)S(1)} collective-permute-done((bf16[512,2048]{1,0:T(8,128)(2,1)S(1)}, bf16[512,2048]{1,0:T(8,128)(2,1)S(1)}, u32[]{:S(2)}, u32[]{:S(2)}) %collective-permute-start.30) | collective-permute-done | bytes 2097184 | tf_op jit(solution)/shard_map/ppermute | solution.py:18
  567.0 11.0 %collective-permute-done.37 = f32[512]{0:T(512)S(1)} collective-permute-done((f32[512]{0:T(512)S(1)}, f32[512]{0:T(512)S(1)}, u32[]{:S(2)}, u32[]{:S(2)}) %collective-permute-start.37) | collective-permute-done | bytes 2080 | tf_op jit(solution)/shard_map/ppermute | solution.py:18
  583.3 2.9 fusion.17
  593.2 7.2 fusion.35
  600.8 28.3 %attend_back.1 = bf16[4,2,256,2048]{3,2,1,0:T(8,128)(2,1)} custom-call(s32[1]{0:T(128)} %bitcast.1.s_ref, bf16[4,2,256,2048]{3,2,1,0:T(8,128)(2,1)} %bitcast.108, bf16[4,2,256,512]{3,2,1,0:T(8,128)(2,1)S(1)} %copy-done.19, f32[4,2,256,512]{3,2,1,0:T(8,128)S(1)} %bitcast.115, f32[4,2,256,128]{3,2,1,0:T(8,128)S(1)} %broadcast_in_dim.8.inner_ref, ...), custom_call_target="tpu_custom_call" | custom-call | flops 8000000000 | bytes 33554432 | tf_op jit(solution)/shard_map/attend_back/pallas_call | solution.py:292
  629.2 3.1 multiply_convert_fusion
  636.0 9.9 %convolution_convert_fusion.8 = bf16[2048,512]{1,0:T(8,128)(2,1)} fusion(bf16[2048,2048]{1,0:T(8,128)(2,1)} %constant_dynamic-update-slice_fusion.15, bf16[2048,512]{1,0:T(8,128)(2,1)} %bitcast.112), kind=kOutput, calls=%fused_computation.33 | convolution fusion | flops 4296015872 | bytes 12582912 | tf_op jit(solution)/shard_map/dot_general | solution.py:104
  646.2 10.7 %collective-permute-done.39.refs_2_ = bf16[352,2048]{1,0:T(8,128)(2,1)S(1)} collective-permute-done((bf16[352,2048]{1,0:T(8,128)(2,1)S(1)}, bf16[352,2048]{1,0:T(8,128)(2,1)S(1)}, u32[]{:S(2)}, u32[]{:S(2)}) %collective-permute-start.39) | collective-permute-done | bytes 1441824 | tf_op jit(solution)/shard_map/ppermute | solution.py:18
  658.1 23.8 %convolution_convert_fusion = bf16[2048,2048]{1,0:T(8,128)(2,1)} fusion(bf16[2048,2048]{1,0:T(8,128)(2,1)} %bitcast.155, bf16[2048,2048]{1,0:T(8,128)(2,1)} %constant_dynamic-update-slice_fusion), kind=kOutput, calls=%fused_computation | convolution fusion | flops 17184063488 | bytes 25165824 | tf_op jit(solution)/shard_map/dot_general | solution.py:104
  689.0 12.8 %collective-permute-done.41.refs_3_ = bf16[176,2048]{1,0:T(8,128)(2,1)} collective-permute-done((bf16[176,2048]{1,0:T(8,128)(2,1)}, bf16[176,2048]{1,0:T(8,128)(2,1)}, u32[]{:S(2)}, u32[]{:S(2)}) %collective-permute-start.41) | collective-permute-done | bytes 720928 | tf_op jit(solution)/shard_map/ppermute | solution.py:18
  701.8 6.3 convolution_convert_fusion.15
  708.2 7.2 convolution_convert_fusion.14
  720.4 5.7 convolution_convert_fusion.5
  726.1 6.1 convolution_convert_fusion.6
  732.3 2.6 fusion.19
  735.6 13.2 %collective-permute-done.44.refs_3_ = bf16[80,2048]{1,0:T(8,128)(2,1)S(1)} collective-permute-done((bf16[80,2048]{1,0:T(8,128)(2,1)S(1)}, bf16[80,2048]{1,0:T(8,128)(2,1)S(1)}, u32[]{:S(2)}, u32[]{:S(2)}) %collective-permute-start.44) | collective-permute-done | bytes 327712 | tf_op jit(solution)/shard_map/ppermute | solution.py:18
  749.5 2.9 fusion.18
  754.4 19.7 %reduce-scatter.14.cloned.1.call-done.refs_0_ = bf16[256,2048]{1,0:T(8,128)(2,1)} async-done(((bf16[2048,2048]{1,0:T(8,128)(2,1)}), bf16[256,2048]{1,0:T(8,128)(2,1)}) %reduce-scatter.14.cloned.1.call-update) | async-done | bytes 1048592 | tf_op jit(solution)/shard_map/reduce_scatter | solution.py:865
  777.0 8.5 %convolution_convert_fusion.7 = bf16[512,2048]{1,0:T(8,128)(2,1)S(1)} fusion(bf16[2048,2048]{1,0:T(8,128)(2,1)} %all-gather.5.cloned.1.call-done, bf16[2048,2048]{1,0:T(8,128)(2,1)} %bitcast.158), kind=kOutput, calls=%fused_computation.32 | convolution fusion | flops 4296015872 | bytes 12582912 | tf_op jit(solution)/shard_map/dot_general | solution.py:98
  785.6 2.7 collective-permute-done.49
  788.2 3.4 convert_add_fusion
  791.7 14.9 %collective-permute-done.51.refs_2_ = bf16[256,2048]{1,0:T(8,128)(2,1)S(1)} collective-permute-done((bf16[256,2048]{1,0:T(8,128)(2,1)}, bf16[256,2048]{1,0:T(8,128)(2,1)S(1)}, u32[]{:S(2)}, u32[]{:S(2)}) %collective-permute-start.51) | collective-permute-done | bytes 1048608 | tf_op jit(solution)/shard_map/ppermute | solution.py:18
  819.7 4.2 place_rows.4
  824.0 4.4 place_rows.5
  828.4 3.1 place_rows.3
  835.7 4.4 sort_rows.1
  (370 shorter events, 157.7 us)
Async XLA Ops:
  7.2 108.6 %all-gather.5.cloned.1.call-start = ((), (), s32[]{:S(2)}) async-start(), calls=%async_computation.5 | async-start | bytes 9437184 | tf_op jit(solution)/shard_map/all_gather | solution.py:626
  20.4 136.6 %all-gather.7.cloned.1.call-start = ((), (), s32[]{:S(2)}) async-start(), calls=%async_computation.6 | async-start | bytes 2359296 | tf_op jit(solution)/shard_map/all_gather | solution.py:813
  24.4 222.6 %all-gather.9.cloned.1.call-start = ((), (), s32[]{:S(2)}) async-start(), calls=%async_computation.7 | async-start | bytes 12976128 | tf_op jit(solution)/shard_map/all_gather | solution.py:816
  27.1 346.2 %all-gather.11.cloned.1.call-start = ((), (), s32[]{:S(2)}) async-start(), calls=%async_computation.8 | async-start | bytes 6488064 | tf_op jit(solution)/shard_map/all_gather | solution.py:819
  27.2 51.8 %collective-permute-start.1 = (bf16[512,2048]{1,0:T(8,128)(2,1)}, bf16[512,2048]{1,0:T(8,128)(2,1)}, u32[]{:S(2)}, u32[]{:S(2)}) collective-permute-start(bf16[512,2048]{1,0:T(8,128)(2,1)} %get-tuple-element.196), channel_id=1, source_target_pairs={{0,16},{8,24},{16,0},{24,8},{1,17},{9,25},{17,1},{25,9},{2,18},{10... | collective-permute-start | bytes 6291464 | tf_op jit(solution)/shard_map/ppermute | solution.py:18
  31.0 51.9 %collective-permute-start = (bf16[512,2048]{1,0:T(8,128)(2,1)}, bf16[512,2048]{1,0:T(8,128)(2,1)}, u32[]{:S(2)}, u32[]{:S(2)}) collective-permute-start(bf16[512,2048]{1,0:T(8,128)(2,1)} %get-tuple-element.196), channel_id=1, source_target_pairs={{0,8},{8,0},{16,24},{24,16},{1,9},{9,1},{17,25},{25,17},{2,10},{10... | collective-permute-start | bytes 6291464 | tf_op jit(solution)/shard_map/ppermute | solution.py:18
  32.5 45.4 %collective-permute-start.5 = (f32[1,1024]{1,0:T(1,128)S(1)}, f32[1,1024]{1,0:T(1,128)S(1)}, u32[]{:S(2)}, u32[]{:S(2)}) collective-permute-start(f32[1,1024]{1,0:T(1,128)S(1)} %get-tuple-element.185), channel_id=1, source_target_pairs={{0,8},{8,0},{16,24},{24,16},{1,9},{9,1},{17,25},{25,17},{2,10},{10... | collective-permute-start | bytes 12296 | tf_op jit(solution)/shard_map/ppermute | solution.py:18
  33.1 44.8 %collective-permute-start.7 = (f32[1,1024]{1,0:T(1,128)S(1)}, f32[1,1024]{1,0:T(1,128)S(1)}, u32[]{:S(2)}, u32[]{:S(2)}) collective-permute-start(f32[1,1024]{1,0:T(1,128)S(1)} %get-tuple-element.187), channel_id=1, source_target_pairs={{0,16},{8,24},{16,0},{24,8},{1,17},{9,25},{17,1},{25,9},{2,18},{10... | collective-permute-start | bytes 12296 | tf_op jit(solution)/shard_map/ppermute | solution.py:18
  33.2 45.6 %collective-permute-start.6 = (f32[1,1024]{1,0:T(1,128)S(1)}, f32[1,1024]{1,0:T(1,128)S(1)}, u32[]{:S(2)}, u32[]{:S(2)}) collective-permute-start(f32[1,1024]{1,0:T(1,128)S(1)} %get-tuple-element.188), channel_id=1, source_target_pairs={{0,24},{8,16},{16,8},{24,0},{1,25},{9,17},{17,9},{25,1},{2,26},{10... | collective-permute-start | bytes 12296 | tf_op jit(solution)/shard_map/ppermute | solution.py:18
  81.3 25.3 %collective-permute-start.3 = (bf16[256,2048]{1,0:T(8,128)(2,1)}, bf16[256,2048]{1,0:T(8,128)(2,1)}, u32[]{:S(2)}, u32[]{:S(2)}) collective-permute-start(bf16[256,2048]{1,0:T(8,128)(2,1)} %slice.291), channel_id=1, source_target_pairs={{0,8},{8,0},{16,24},{24,16},{1,9},{9,1},{17,25},{25,17},{2,10},{10... | collective-permute-start | bytes 3145736 | tf_op jit(solution)/shard_map/ppermute | solution.py:18
  85.3 25.0 %collective-permute-start.2 = (bf16[256,2048]{1,0:T(8,128)(2,1)}, bf16[256,2048]{1,0:T(8,128)(2,1)}, u32[]{:S(2)}, u32[]{:S(2)}) collective-permute-start(bf16[256,2048]{1,0:T(8,128)(2,1)} %slice.290), channel_id=1, source_target_pairs={{0,16},{8,24},{16,0},{24,8},{1,17},{9,25},{17,1},{25,9},{2,18},{10... | collective-permute-start | bytes 3145736 | tf_op jit(solution)/shard_map/ppermute | solution.py:18
  110.3 46.6 %collective-permute-start.9 = (bf16[512,2048]{1,0:T(8,128)(2,1)}, bf16[512,2048]{1,0:T(8,128)(2,1)}, u32[]{:S(2)}, u32[]{:S(2)}) collective-permute-start(bf16[512,2048]{1,0:T(8,128)(2,1)} %fusion.1.refs_0_), channel_id=1, source_target_pairs={{0,16},{8,24},{16,0},{24,8},{1,17},{9,25},{17,1},{25,9},{2,18},{10... | collective-permute-start | bytes 6291464 | tf_op jit(solution)/shard_map/ppermute | solution.py:18
  110.8 46.2 %collective-permute-start.8 = (bf16[512,2048]{1,0:T(8,128)(2,1)}, bf16[512,2048]{1,0:T(8,128)(2,1)}, u32[]{:S(2)}, u32[]{:S(2)}) collective-permute-start(bf16[512,2048]{1,0:T(8,128)(2,1)} %fusion.1.refs_0_), channel_id=1, source_target_pairs={{0,8},{8,0},{16,24},{24,16},{1,9},{9,1},{17,25},{25,17},{2,10},{10... | collective-permute-start | bytes 6291464 | tf_op jit(solution)/shard_map/ppermute | solution.py:18
  159.6 23.0 %collective-permute-start.10 = (bf16[256,2048]{1,0:T(8,128)(2,1)S(1)}, bf16[256,2048]{1,0:T(8,128)(2,1)S(1)}, u32[]{:S(2)}, u32[]{:S(2)}) collective-permute-start(bf16[256,2048]{1,0:T(8,128)(2,1)S(1)} %convolution_convert_fusion.13), channel_id=1, source_target_pairs={{0,16},{8,24},{16,0},{24,8},{1,17},{9,25},{17,1},{25,9},{2,18},{10... | collective-permute-start | bytes 3145736 | tf_op jit(solution)/shard_map/ppermute | solution.py:18
  163.7 23.5 %collective-permute-start.12 = (bf16[256,2048]{1,0:T(8,128)(2,1)S(1)}, bf16[256,2048]{1,0:T(8,128)(2,1)S(1)}, u32[]{:S(2)}, u32[]{:S(2)}) collective-permute-start(bf16[256,2048]{1,0:T(8,128)(2,1)S(1)} %convolution_convert_fusion.12), channel_id=1, source_target_pairs={{0,8},{8,0},{16,24},{24,16},{1,9},{9,1},{17,25},{25,17},{2,10},{10... | collective-permute-start | bytes 3145736 | tf_op jit(solution)/shard_map/ppermute | solution.py:18
  185.1 49.0 %collective-permute-start.11 = (bf16[512,2048]{1,0:T(8,128)(2,1)}, bf16[512,2048]{1,0:T(8,128)(2,1)}, u32[]{:S(2)}, u32[]{:S(2)}) collective-permute-start(bf16[512,2048]{1,0:T(8,128)(2,1)} %fusion.12), channel_id=1, source_target_pairs={{0,8},{8,0},{16,24},{24,16},{1,9},{9,1},{17,25},{25,17},{2,10},{10... | collective-permute-start | bytes 6291464 | tf_op jit(solution)/shard_map/ppermute | solution.py:18
  189.9 44.2 %collective-permute-start.13 = (bf16[512,2048]{1,0:T(8,128)(2,1)}, bf16[512,2048]{1,0:T(8,128)(2,1)}, u32[]{:S(2)}, u32[]{:S(2)}) collective-permute-start(bf16[512,2048]{1,0:T(8,128)(2,1)} %fusion.13), channel_id=1, source_target_pairs={{0,16},{8,24},{16,0},{24,8},{1,17},{9,25},{17,1},{25,9},{2,18},{10... | collective-permute-start | bytes 6291464 | tf_op jit(solution)/shard_map/ppermute | solution.py:18
  192.1 41.9 %collective-permute-start.15 = (f32[512]{0:T(512)S(1)}, f32[512]{0:T(512)S(1)}, u32[]{:S(2)}, u32[]{:S(2)}) collective-permute-start(f32[512]{0:T(512)S(1)} %bitcast.152), channel_id=1, source_target_pairs={{0,16},{8,24},{16,0},{24,8},{1,17},{9,25},{17,1},{25,9},{2,18},{10... | collective-permute-start | bytes 6152 | tf_op jit(solution)/shard_map/ppermute | solution.py:18
  193.6 40.5 %collective-permute-start.16 = (f32[512]{0:T(512)S(1)}, f32[512]{0:T(512)S(1)}, u32[]{:S(2)}, u32[]{:S(2)}) collective-permute-start(f32[512]{0:T(512)S(1)} %bitcast.151), channel_id=1, source_target_pairs={{0,24},{8,16},{16,8},{24,0},{1,25},{9,17},{17,9},{25,1},{2,26},{10... | collective-permute-start | bytes 6152 | tf_op jit(solution)/shard_map/ppermute | solution.py:18
  194.3 39.8 %collective-permute-start.14 = (f32[512]{0:T(512)S(1)}, f32[512]{0:T(512)S(1)}, u32[]{:S(2)}, u32[]{:S(2)}) collective-permute-start(f32[512]{0:T(512)S(1)} %bitcast.150), channel_id=1, source_target_pairs={{0,8},{8,0},{16,24},{24,16},{1,9},{9,1},{17,25},{25,17},{2,10},{10... | collective-permute-start | bytes 6152 | tf_op jit(solution)/shard_map/ppermute | solution.py:18
  196.7 435.6 %reduce-scatter.6.cloned.1.call-start = ((), (), s32[]{:S(2)}) async-start(), calls=%async_computation.9 | async-start | bytes 6488064 | tf_op jit(solution)/shard_map/reduce_scatter | solution.py:865
  244.4 44.3 %collective-permute-start.19 = (bf16[512,2048]{1,0:T(8,128)(2,1)}, bf16[512,2048]{1,0:T(8,128)(2,1)S(1)}, u32[]{:S(2)}, u32[]{:S(2)}) collective-permute-start(bf16[512,2048]{1,0:T(8,128)(2,1)} %get-tuple-element.170.refs_0_), channel_id=1, source_target_pairs={{0,16},{8,24},{16,0},{24,8},{1,17},{9,25},{17,1},{25,9},{2,18},{10... | collective-permute-start | bytes 6291464 | tf_op jit(solution)/shard_map/ppermute | solution.py:18
  246.1 47.0 %collective-permute-start.17 = (bf16[512,2048]{1,0:T(8,128)(2,1)}, bf16[512,2048]{1,0:T(8,128)(2,1)}, u32[]{:S(2)}, u32[]{:S(2)}) collective-permute-start(bf16[512,2048]{1,0:T(8,128)(2,1)} %get-tuple-element.170.refs_0_), channel_id=1, source_target_pairs={{0,8},{8,0},{16,24},{24,16},{1,9},{9,1},{17,25},{25,17},{2,10},{10... | collective-permute-start | bytes 6291464 | tf_op jit(solution)/shard_map/ppermute | solution.py:18
  288.8 34.0 %collective-permute-start.20 = (bf16[256,2048]{1,0:T(8,128)(2,1)S(1)}, bf16[256,2048]{1,0:T(8,128)(2,1)S(1)}, u32[]{:S(2)}, u32[]{:S(2)}) collective-permute-start(bf16[256,2048]{1,0:T(8,128)(2,1)S(1)} %slice.307), channel_id=1, source_target_pairs={{0,8},{8,0},{16,24},{24,16},{1,9},{9,1},{17,25},{25,17},{2,10},{10... | collective-permute-start | bytes 3145736 | tf_op jit(solution)/shard_map/ppermute | solution.py:18
  294.5 28.3 %collective-permute-start.18 = (bf16[256,2048]{1,0:T(8,128)(2,1)S(1)}, bf16[256,2048]{1,0:T(8,128)(2,1)S(1)}, u32[]{:S(2)}, u32[]{:S(2)}) collective-permute-start(bf16[256,2048]{1,0:T(8,128)(2,1)S(1)} %slice.306), channel_id=1, source_target_pairs={{0,16},{8,24},{16,0},{24,8},{1,17},{9,25},{17,1},{25,9},{2,18},{10... | collective-permute-start | bytes 3145736 | tf_op jit(solution)/shard_map/ppermute | solution.py:18
  325.5 28.6 %collective-permute-start.22 = (bf16[256,2048]{1,0:T(8,128)(2,1)S(1)}, bf16[256,2048]{1,0:T(8,128)(2,1)S(1)}, u32[]{:S(2)}, u32[]{:S(2)}) collective-permute-start(bf16[256,2048]{1,0:T(8,128)(2,1)S(1)} %slice.246), channel_id=1, source_target_pairs={{0,8},{8,0},{16,24},{24,16},{1,9},{9,1},{17,25},{25,17},{2,10},{10... | collective-permute-start | bytes 3145736 | tf_op jit(solution)/shard_map/ppermute | solution.py:18
  326.0 26.9 %collective-permute-start.21 = (bf16[256,2048]{1,0:T(8,128)(2,1)S(1)}, bf16[256,2048]{1,0:T(8,128)(2,1)S(1)}, u32[]{:S(2)}, u32[]{:S(2)}) collective-permute-start(bf16[256,2048]{1,0:T(8,128)(2,1)S(1)} %slice.245), channel_id=1, source_target_pairs={{0,16},{8,24},{16,0},{24,8},{1,17},{9,25},{17,1},{25,9},{2,18},{10... | collective-permute-start | bytes 3145736 | tf_op jit(solution)/shard_map/ppermute | solution.py:18
  373.2 259.0 %reduce-scatter.8.cloned.1.call-start = ((), (), s32[]{:S(2)}) async-start(), calls=%async_computation.10 | async-start | bytes 6488064 | tf_op jit(solution)/shard_map/reduce_scatter | solution.py:865
  393.9 47.7 %collective-permute-start.23 = (bf16[256,2048]{1,0:T(8,128)(2,1)S(1)}, bf16[256,2048]{1,0:T(8,128)(2,1)S(1)}, u32[]{:S(2)}, u32[]{:S(2)}) collective-permute-start(bf16[256,2048]{1,0:T(8,128)(2,1)S(1)} %get-tuple-element.109), channel_id=1, source_target_pairs={{0,8},{8,0},{16,24},{24,16},{1,9},{9,1},{17,25},{25,17},{2,10},{10... | collective-permute-start | bytes 3145736 | tf_op jit(solution)/shard_map/ppermute | solution.py:18
  395.6 46.0 %collective-permute-start.24 = (bf16[256,2048]{1,0:T(8,128)(2,1)S(1)}, bf16[256,2048]{1,0:T(8,128)(2,1)S(1)}, u32[]{:S(2)}, u32[]{:S(2)}) collective-permute-start(bf16[256,2048]{1,0:T(8,128)(2,1)S(1)} %get-tuple-element.110), channel_id=1, source_target_pairs={{0,16},{8,24},{16,0},{24,8},{1,17},{9,25},{17,1},{25,9},{2,18},{10... | collective-permute-start | bytes 3145736 | tf_op jit(solution)/shard_map/ppermute | solution.py:18
  395.7 46.0 %collective-permute-start.25 = (bf16[256,2048]{1,0:T(8,128)(2,1)S(1)}, bf16[256,2048]{1,0:T(8,128)(2,1)S(1)}, u32[]{:S(2)}, u32[]{:S(2)}) collective-permute-start(bf16[256,2048]{1,0:T(8,128)(2,1)S(1)} %get-tuple-element.111), channel_id=1, source_target_pairs={{0,8},{8,0},{16,24},{24,16},{1,9},{9,1},{17,25},{25,17},{2,10},{10... | collective-permute-start | bytes 3145736 | tf_op jit(solution)/shard_map/ppermute | solution.py:18
  396.0 45.7 %collective-permute-start.26 = (bf16[256,2048]{1,0:T(8,128)(2,1)}, bf16[256,2048]{1,0:T(8,128)(2,1)S(1)}, u32[]{:S(2)}, u32[]{:S(2)}) collective-permute-start(bf16[256,2048]{1,0:T(8,128)(2,1)} %get-tuple-element.112), channel_id=1, source_target_pairs={{0,16},{8,24},{16,0},{24,8},{1,17},{9,25},{17,1},{25,9},{2,18},{10... | collective-permute-start | bytes 3145736 | tf_op jit(solution)/shard_map/ppermute | solution.py:18
  445.0 43.1 %collective-permute-start.28 = (bf16[512,2048]{1,0:T(8,128)(2,1)}, bf16[512,2048]{1,0:T(8,128)(2,1)}, u32[]{:S(2)}, u32[]{:S(2)}) collective-permute-start(bf16[512,2048]{1,0:T(8,128)(2,1)} %fusion.15), channel_id=1, source_target_pairs={{0,16},{8,24},{16,0},{24,8},{1,17},{9,25},{17,1},{25,9},{2,18},{10... | collective-permute-start | bytes 6291464 | tf_op jit(solution)/shard_map/ppermute | solution.py:18
  447.7 40.4 %collective-permute-start.27 = (bf16[512,2048]{1,0:T(8,128)(2,1)}, bf16[512,2048]{1,0:T(8,128)(2,1)}, u32[]{:S(2)}, u32[]{:S(2)}) collective-permute-start(bf16[512,2048]{1,0:T(8,128)(2,1)} %fusion.14), channel_id=1, source_target_pairs={{0,8},{8,0},{16,24},{24,16},{1,9},{9,1},{17,25},{25,17},{2,10},{10... | collective-permute-start | bytes 6291464 | tf_op jit(solution)/shard_map/ppermute | solution.py:18
  514.6 171.7 %reduce-scatter.10.cloned.1.call-start = ((), (), s32[]{:S(2)}) async-start(), calls=%async_computation.11 | async-start | bytes 6488064 | tf_op jit(solution)/shard_map/reduce_scatter | solution.py:865
  515.3 234.2 %reduce-scatter.12.cloned.1.call-start = ((), (), s32[]{:S(2)}) async-start(), calls=%async_computation.12 | async-start | bytes 2359296 | tf_op jit(solution)/shard_map/reduce_scatter | solution.py:865
  515.5 41.0 %collective-permute-start.30 = (bf16[512,2048]{1,0:T(8,128)(2,1)S(1)}, bf16[512,2048]{1,0:T(8,128)(2,1)S(1)}, u32[]{:S(2)}, u32[]{:S(2)}) collective-permute-start(bf16[512,2048]{1,0:T(8,128)(2,1)S(1)} %get-tuple-element.135), channel_id=1, source_target_pairs={{0,16},{8,24},{16,0},{24,8},{1,17},{9,25},{17,1},{25,9},{2,18},{10... | collective-permute-start | bytes 6291464 | tf_op jit(solution)/shard_map/ppermute | solution.py:18
  517.6 41.4 %collective-permute-start.29 = (bf16[512,2048]{1,0:T(8,128)(2,1)S(1)}, bf16[512,2048]{1,0:T(8,128)(2,1)S(1)}, u32[]{:S(2)}, u32[]{:S(2)}) collective-permute-start(bf16[512,2048]{1,0:T(8,128)(2,1)S(1)} %get-tuple-element.135), channel_id=1, source_target_pairs={{0,8},{8,0},{16,24},{24,16},{1,9},{9,1},{17,25},{25,17},{2,10},{10... | collective-permute-start | bytes 6291464 | tf_op jit(solution)/shard_map/ppermute | solution.py:18
  561.2 22.1 %collective-permute-start.32 = (bf16[256,2048]{1,0:T(8,128)(2,1)}, bf16[256,2048]{1,0:T(8,128)(2,1)}, u32[]{:S(2)}, u32[]{:S(2)}) collective-permute-start(bf16[256,2048]{1,0:T(8,128)(2,1)} %slice.250), channel_id=1, source_target_pairs={{0,8},{8,0},{16,24},{24,16},{1,9},{9,1},{17,25},{25,17},{2,10},{10... | collective-permute-start | bytes 3145736 | tf_op jit(solution)/shard_map/ppermute | solution.py:18
  561.4 21.9 %collective-permute-start.31 = (bf16[256,2048]{1,0:T(8,128)(2,1)}, bf16[256,2048]{1,0:T(8,128)(2,1)}, u32[]{:S(2)}, u32[]{:S(2)}) collective-permute-start(bf16[256,2048]{1,0:T(8,128)(2,1)} %slice.249), channel_id=1, source_target_pairs={{0,16},{8,24},{16,0},{24,8},{1,17},{9,25},{17,1},{25,9},{2,18},{10... | collective-permute-start | bytes 3145736 | tf_op jit(solution)/shard_map/ppermute | solution.py:18
  563.5 14.5 %collective-permute-start.37 = (f32[512]{0:T(512)S(1)}, f32[512]{0:T(512)S(1)}, u32[]{:S(2)}, u32[]{:S(2)}) collective-permute-start(f32[512]{0:T(512)S(1)} %multiply_multiply_fusion.1), channel_id=1, source_target_pairs={{0,24},{8,16},{16,8},{24,0},{1,25},{9,17},{17,9},{25,1},{2,26},{10... | collective-permute-start | bytes 6152 | tf_op jit(solution)/shard_map/ppermute | solution.py:18
  564.7 13.4 %collective-permute-start.36 = (f32[512]{0:T(512)S(1)}, f32[512]{0:T(512)S(1)}, u32[]{:S(2)}, u32[]{:S(2)}) collective-permute-start(f32[512]{0:T(512)S(1)} %multiply_multiply_fusion.1), channel_id=1, source_target_pairs={{0,16},{8,24},{16,0},{24,8},{1,17},{9,25},{17,1},{25,9},{2,18},{10... | collective-permute-start | bytes 6152 | tf_op jit(solution)/shard_map/ppermute | solution.py:18
  586.2 43.0 %collective-permute-start.34 = (bf16[512,2048]{1,0:T(8,128)(2,1)}, bf16[512,2048]{1,0:T(8,128)(2,1)S(1)}, u32[]{:S(2)}, u32[]{:S(2)}) collective-permute-start(bf16[512,2048]{1,0:T(8,128)(2,1)} %fusion.17), channel_id=1, source_target_pairs={{0,16},{8,24},{16,0},{24,8},{1,17},{9,25},{17,1},{25,9},{2,18},{10... | collective-permute-start | bytes 6291464 | tf_op jit(solution)/shard_map/ppermute | solution.py:18
  587.5 41.7 %collective-permute-start.33 = (bf16[512,2048]{1,0:T(8,128)(2,1)S(1)}, bf16[512,2048]{1,0:T(8,128)(2,1)S(1)}, u32[]{:S(2)}, u32[]{:S(2)}) collective-permute-start(bf16[512,2048]{1,0:T(8,128)(2,1)S(1)} %fusion.16), channel_id=1, source_target_pairs={{0,8},{8,0},{16,24},{24,16},{1,9},{9,1},{17,25},{25,17},{2,10},{10... | collective-permute-start | bytes 6291464 | tf_op jit(solution)/shard_map/ppermute | solution.py:18
  633.8 23.2 %collective-permute-start.39 = (bf16[352,2048]{1,0:T(8,128)(2,1)S(1)}, bf16[352,2048]{1,0:T(8,128)(2,1)S(1)}, u32[]{:S(2)}, u32[]{:S(2)}) collective-permute-start(bf16[352,2048]{1,0:T(8,128)(2,1)S(1)} %pad_maximum_fusion.1.refs_0_), channel_id=1, source_target_pairs={{0,16},{8,24},{16,0},{24,8},{1,17},{9,25},{17,1},{25,9},{2,18},{10... | collective-permute-start | bytes 4325384 | tf_op jit(solution)/shard_map/ppermute | solution.py:18
  635.2 22.9 %collective-permute-start.38 = (bf16[352,2048]{1,0:T(8,128)(2,1)S(1)}, bf16[352,2048]{1,0:T(8,128)(2,1)}, u32[]{:S(2)}, u32[]{:S(2)}) collective-permute-start(bf16[352,2048]{1,0:T(8,128)(2,1)S(1)} %pad_maximum_fusion.1.refs_0_), channel_id=1, source_target_pairs={{0,8},{8,0},{16,24},{24,16},{1,9},{9,1},{17,25},{25,17},{2,10},{10... | collective-permute-start | bytes 4325384 | tf_op jit(solution)/shard_map/ppermute | solution.py:18
  646.0 128.1 %reduce-scatter.14.cloned.1.call-start = ((), (), s32[]{:S(2)}) async-start(), calls=%async_computation.13 | async-start | bytes 9437184 | tf_op jit(solution)/shard_map/reduce_scatter | solution.py:865
  682.9 18.9 %collective-permute-start.41 = (bf16[176,2048]{1,0:T(8,128)(2,1)}, bf16[176,2048]{1,0:T(8,128)(2,1)}, u32[]{:S(2)}, u32[]{:S(2)}) collective-permute-start(bf16[176,2048]{1,0:T(8,128)(2,1)} %slice.309), channel_id=1, source_target_pairs={{0,8},{8,0},{16,24},{24,16},{1,9},{9,1},{17,25},{25,17},{2,10},{10... | collective-permute-start | bytes 2162696 | tf_op jit(solution)/shard_map/ppermute | solution.py:18
  685.3 16.5 %collective-permute-start.40 = (bf16[176,2048]{1,0:T(8,128)(2,1)}, bf16[176,2048]{1,0:T(8,128)(2,1)}, u32[]{:S(2)}, u32[]{:S(2)}) collective-permute-start(bf16[176,2048]{1,0:T(8,128)(2,1)} %slice.308), channel_id=1, source_target_pairs={{0,16},{8,24},{16,0},{24,8},{1,17},{9,25},{17,1},{25,9},{2,18},{10... | collective-permute-start | bytes 2162696 | tf_op jit(solution)/shard_map/ppermute | solution.py:18
  686.3 29.8 %collective-permute-start.43 = (bf16[176,2048]{1,0:T(8,128)(2,1)}, bf16[176,2048]{1,0:T(8,128)(2,1)S(1)}, u32[]{:S(2)}, u32[]{:S(2)}) collective-permute-start(bf16[176,2048]{1,0:T(8,128)(2,1)} %reduce-scatter.10.cloned.1.call-done.refs_0_), channel_id=1, source_target_pairs={{0,16},{8,24},{16,0},{24,8},{1,17},{9,25},{17,1},{25,9},{2,18},{10... | collective-permute-start | bytes 2162696 | tf_op jit(solution)/shard_map/ppermute | solution.py:18
  687.3 29.8 %collective-permute-start.42 = (bf16[176,2048]{1,0:T(8,128)(2,1)}, bf16[176,2048]{1,0:T(8,128)(2,1)S(1)}, u32[]{:S(2)}, u32[]{:S(2)}) collective-permute-start(bf16[176,2048]{1,0:T(8,128)(2,1)} %reduce-scatter.10.cloned.1.call-done.refs_0_), channel_id=1, source_target_pairs={{0,8},{8,0},{16,24},{24,16},{1,9},{9,1},{17,25},{25,17},{2,10},{10... | collective-permute-start | bytes 2162696 | tf_op jit(solution)/shard_map/ppermute | solution.py:18
  708.1 24.2 %collective-permute-start.48 = (bf16[256,2048]{1,0:T(8,128)(2,1)S(1)}, bf16[256,2048]{1,0:T(8,128)(2,1)S(1)}, u32[]{:S(2)}, u32[]{:S(2)}) collective-permute-start(bf16[256,2048]{1,0:T(8,128)(2,1)S(1)} %convolution_convert_fusion.15), channel_id=1, source_target_pairs={{0,8},{8,0},{16,24},{24,16},{1,9},{9,1},{17,25},{25,17},{2,10},{10... | collective-permute-start | bytes 3145736 | tf_op jit(solution)/shard_map/ppermute | solution.py:18
  715.4 34.1 %collective-permute-start.46 = (bf16[256,2048]{1,0:T(8,128)(2,1)}, bf16[256,2048]{1,0:T(8,128)(2,1)}, u32[]{:S(2)}, u32[]{:S(2)}) collective-permute-start(bf16[256,2048]{1,0:T(8,128)(2,1)} %convolution_convert_fusion.14), channel_id=1, source_target_pairs={{0,16},{8,24},{16,0},{24,8},{1,17},{9,25},{17,1},{25,9},{2,18},{10... | collective-permute-start | bytes 3145736 | tf_op jit(solution)/shard_map/ppermute | solution.py:18
  717.2 31.6 %collective-permute-start.44 = (bf16[80,2048]{1,0:T(8,128)(2,1)S(1)}, bf16[80,2048]{1,0:T(8,128)(2,1)S(1)}, u32[]{:S(2)}, u32[]{:S(2)}) collective-permute-start(bf16[80,2048]{1,0:T(8,128)(2,1)S(1)} %slice.259), channel_id=1, source_target_pairs={{0,16},{8,24},{16,0},{24,8},{1,17},{9,25},{17,1},{25,9},{2,18},{10... | collective-permute-start | bytes 983048 | tf_op jit(solution)/shard_map/ppermute | solution.py:18
  718.9 30.6 %collective-permute-start.45 = (bf16[96,2048]{1,0:T(8,128)(2,1)S(1)}, bf16[96,2048]{1,0:T(8,128)(2,1)S(1)}, u32[]{:S(2)}, u32[]{:S(2)}) collective-permute-start(bf16[96,2048]{1,0:T(8,128)(2,1)S(1)} %slice.260), channel_id=1, source_target_pairs={{0,8},{8,0},{16,24},{24,16},{1,9},{9,1},{17,25},{25,17},{2,10},{10... | collective-permute-start | bytes 1179656 | tf_op jit(solution)/shard_map/ppermute | solution.py:18
  734.9 53.3 %collective-permute-start.49 = (bf16[512,2048]{1,0:T(8,128)(2,1)}, bf16[512,2048]{1,0:T(8,128)(2,1)}, u32[]{:S(2)}, u32[]{:S(2)}) collective-permute-start(bf16[512,2048]{1,0:T(8,128)(2,1)} %fusion.19), channel_id=1, source_target_pairs={{0,16},{8,24},{16,0},{24,8},{1,17},{9,25},{17,1},{25,9},{2,18},{10... | collective-permute-start | bytes 6291464 | tf_op jit(solution)/shard_map/ppermute | solution.py:18
  752.4 35.8 %collective-permute-start.47 = (bf16[512,2048]{1,0:T(8,128)(2,1)}, bf16[512,2048]{1,0:T(8,128)(2,1)}, u32[]{:S(2)}, u32[]{:S(2)}) collective-permute-start(bf16[512,2048]{1,0:T(8,128)(2,1)} %fusion.18), channel_id=1, source_target_pairs={{0,8},{8,0},{16,24},{24,16},{1,9},{9,1},{17,25},{25,17},{2,10},{10... | collective-permute-start | bytes 6291464 | tf_op jit(solution)/shard_map/ppermute | solution.py:18
  774.1 32.5 %collective-permute-start.51 = (bf16[256,2048]{1,0:T(8,128)(2,1)}, bf16[256,2048]{1,0:T(8,128)(2,1)S(1)}, u32[]{:S(2)}, u32[]{:S(2)}) collective-permute-start(bf16[256,2048]{1,0:T(8,128)(2,1)} %reduce-scatter.14.cloned.1.call-done.refs_0_), channel_id=1, source_target_pairs={{0,16},{8,24},{16,0},{24,8},{1,17},{9,25},{17,1},{25,9},{2,18},{10... | collective-permute-start | bytes 3145736 | tf_op jit(solution)/shard_map/ppermute | solution.py:18
  775.6 31.1 %collective-permute-start.50 = (bf16[256,2048]{1,0:T(8,128)(2,1)}, bf16[256,2048]{1,0:T(8,128)(2,1)S(1)}, u32[]{:S(2)}, u32[]{:S(2)}) collective-permute-start(bf16[256,2048]{1,0:T(8,128)(2,1)} %reduce-scatter.14.cloned.1.call-done.refs_0_), channel_id=1, source_target_pairs={{0,8},{8,0},{16,24},{24,16},{1,9},{9,1},{17,25},{25,17},{2,10},{10... | collective-permute-start | bytes 3145736 | tf_op jit(solution)/shard_map/ppermute | solution.py:18
  809.2 23.4 %collective-permute-start.53 = (bf16[128,2048]{1,0:T(8,128)(2,1)S(1)}, bf16[128,2048]{1,0:T(8,128)(2,1)S(1)}, u32[]{:S(2)}, u32[]{:S(2)}) collective-permute-start(bf16[128,2048]{1,0:T(8,128)(2,1)S(1)} %slice.312), channel_id=1, source_target_pairs={{0,8},{8,0},{16,24},{24,16},{1,9},{9,1},{17,25},{25,17},{2,10},{10... | collective-permute-start | bytes 1572872 | tf_op jit(solution)/shard_map/ppermute | solution.py:18
  809.8 25.0 %collective-permute-start.54 = (bf16[256,2048]{1,0:T(8,128)(2,1)S(1)}, bf16[256,2048]{1,0:T(8,128)(2,1)S(1)}, u32[]{:S(2)}, u32[]{:S(2)}) collective-permute-start(bf16[256,2048]{1,0:T(8,128)(2,1)S(1)} %broadcast_select_fusion), channel_id=1, source_target_pairs={{0,1},{1,0},{2,3},{3,2},{4,5},{5,4},{6,7},{7,6},{8,9},{9,8},{10,11... | collective-permute-start | bytes 3145736 | tf_op jit(solution)/shard_map/ppermute | solution.py:23
  813.0 18.4 %collective-permute-start.59 = (bf16[128,512]{1,0:T(8,128)(2,1)S(1)}, bf16[128,512]{1,0:T(8,128)(2,1)S(1)}, u32[]{:S(2)}, u32[]{:S(2)}) collective-permute-start(bf16[128,512]{1,0:T(8,128)(2,1)S(1)} %slice.314), channel_id=1, source_target_pairs={{0,8},{8,0},{16,24},{24,16},{1,9},{9,1},{17,25},{25,17},{2,10},{10... | collective-permute-start | bytes 393224 | tf_op jit(solution)/shard_map/ppermute | solution.py:18
  815.2 16.3 %collective-permute-start.57 = (bf16[128,512]{1,0:T(8,128)(2,1)S(1)}, bf16[128,512]{1,0:T(8,128)(2,1)S(1)}, u32[]{:S(2)}, u32[]{:S(2)}) collective-permute-start(bf16[128,512]{1,0:T(8,128)(2,1)S(1)} %slice.313), channel_id=1, source_target_pairs={{0,16},{8,24},{16,0},{24,8},{1,17},{9,25},{17,1},{25,9},{2,18},{10... | collective-permute-start | bytes 393224 | tf_op jit(solution)/shard_map/ppermute | solution.py:18
  818.0 14.5 %collective-permute-start.52 = (bf16[128,2048]{1,0:T(8,128)(2,1)S(1)}, bf16[128,2048]{1,0:T(8,128)(2,1)S(1)}, u32[]{:S(2)}, u32[]{:S(2)}) collective-permute-start(bf16[128,2048]{1,0:T(8,128)(2,1)S(1)} %slice.311), channel_id=1, source_target_pairs={{0,16},{8,24},{16,0},{24,8},{1,17},{9,25},{17,1},{25,9},{2,18},{10... | collective-permute-start | bytes 1572872 | tf_op jit(solution)/shard_map/ppermute | solution.py:18
  (68 other events, 757.7 us)
Sparse Core Ops, SparseCore 0:
  20.5 85.5 all-gather.4
  108.3 29.3 all-gather.6
  139.9 107.1 all-gather.8
  249.1 58.7 all-gather.10
  373.3 65.2 reduce-scatter.5
  514.7 65.5 reduce-scatter.7
  583.2 63.1 reduce-scatter.9
  649.3 34.1 reduce-scatter.11
  685.8 88.2 reduce-scatter.13

commit v4 on v3

--- a/solution.py
+++ b/solution.py
@@ -926,9 +926,9 @@
     rows = after(grad_pre, normed_parts[-1])
     for i in reversed(range(size - 1)):
         normed_parts[i] = normed_part(i, rows)
-    left_pieces = spread_far(after(left_near, normed_parts[-1]))
-    normed_parts[1] = after(normed_parts[1], left_pieces, out_mine)
+    normed_parts[1] = after(normed_parts[1], left_near, out_mine)
     normed_joined = join_near(normed_parts, normed_far)
+    left_pieces = spread_far(after(left_near, normed_joined))
     grad_normed = collect_joined(normed_parts[0], normed_joined)
     paired = paired_heads(query_weight.shape[0])
     project_near = spread_near(project_mine) if paired else project_mine

time: 852 us -> 851 us (level)
    ppermute x57, waiting for transfers between devices: 249 us -> 240 us  [swap_seq(): return lax.ppermute(x, 'seq', [(i, i ^ bit) for i in range(size)])]
    reduce_scatter x5, waiting for transfers between devices: 19.7 us -> 29 us  [own_rows(): return lax.psum_scatter(grad, 'fsdp', scatter_dimension=0, tiled=True)]
    unnamed x163 -> x151, local copies, waits for them, and re-layouts: 44.6 us -> 42.7 us
where the time goes in v4:
time: 851 us; the launch traced here: 846 us
  waiting for transfers between devices  272 us (32%)
  Pallas kernels  191 us (22%)
  matrix products  165 us (19%)
  local copies, waits for them, and re-layouts  74.8 us (9%)
  other arithmetic  67.1 us (8%)
  starting transfers between devices  62 us (7%)
  between operations  15.2 us (2%)
    ppermute x57, waiting for transfers between devices, swap_seq(): return lax.ppermute(x, 'seq', [(i, i ^ bit) for i in range(size)])  240 us
    pallas_call x4, Pallas kernels, unit_backward(): pl.pallas_call(functools.partial(unit_backward_kernel, piece, len(rows),...  84.4 us
    dot_general x5, matrix products, rows_outer(): lax.dot_general(left_side, right_side, (((0,), (0,)), ((), ())), preferre...  84 us
    ppermute x57, starting transfers between devices, swap_seq(): return lax.ppermute(x, 'seq', [(i, i ^ bit) for i in range(size)])  60.5 us
    pallas_call x4, Pallas kernels, unit_forward(): pl.pallas_call(functools.partial(unit_forward_kernel, piece, len(rows), l...  47.2 us
    unnamed x151, local copies, waits for them, and re-layouts  42.7 us
    dot_general x6, matrix products, times(): lax.dot_general(left_side, weight, (((1,), (0,)), ((), ())), preferred_el...  41.1 us
    dot_general x6, matrix products, times_rows(): lax.dot_general(left_side, weight, (((1,), (1,)), ((), ())), preferred_el...  39.4 us
  transfers between devices with their start and end apart: 69, of which 26 were waited for; matrix products, arithmetic and copies ran while one was open for 34% of the time, Pallas kernels for 22%

profile of v4, /device:TPU:0, one launch (start us, length us, event | category | flops | bytes accessed | tf_op | source)
XLA Modules:
  0.0 846.5 jit_solution(4873334999238482545)
XLA Ops:
  14.9 4.0 constant_dynamic-update-slice_fusion.4
  27.2 3.9 collective-permute-start.1
  33.2 2.9 collective-permute-start.6
  36.8 3.3 fusion.1.refs_0_
  40.1 37.8 %collective-permute-done.5 = f32[1,1024]{1,0:T(1,128)S(1)} collective-permute-done((f32[1,1024]{1,0:T(1,128)S(1)}, f32[1,1024]{1,0:T(1,128)S(1)}, u32[]{:S(2)}, u32[]{:S(2)}) %collective-permute-start.5) | collective-permute-done | bytes 4128 | tf_op jit(solution)/shard_map/ppermute | solution.py:18
  85.9 5.1 reduce-window.6
  91.5 3.2 constant_dynamic-update-slice_fusion.3
  94.7 3.2 constant_dynamic-update-slice_fusion.2
  97.9 8.7 %collective-permute-done.3 = bf16[256,2048]{1,0:T(8,128)(2,1)} collective-permute-done((bf16[256,2048]{1,0:T(8,128)(2,1)}, bf16[256,2048]{1,0:T(8,128)(2,1)}, u32[]{:S(2)}, u32[]{:S(2)}) %collective-permute-start.3) | collective-permute-done | bytes 1048608 | tf_op jit(solution)/shard_map/ppermute | solution.py:18
  106.6 3.8 collective-permute-done.2
  115.8 22.3 %convolution_convert_fusion.1 = bf16[2048,2048]{1,0:T(8,128)(2,1)S(1)} fusion(bf16[2048,2048]{1,0:T(8,128)(2,1)} %constant_dynamic-update-slice_fusion, bf16[2048,2048]{1,0:T(8,128)(2,1)} %all-gather.5.cloned.1.call-done), kind=kOutput, calls=%fused_computation.1 | convolution fusion | flops 17184063488 | bytes 25165824 | tf_op jit(solution)/shard_map/dot_general | solution.py:92
  138.8 14.2 %attend.1 = (bf16[4,2,256,512]{3,2,1,0:T(8,128)(2,1)S(1)}, bf16[4,2,256,512]{3,2,1,0:T(8,128)(2,1)S(1)}, f32[4,2,256,128]{3,2,1,0:T(8,128)S(1)}) custom-call(s32[1]{0:T(128)} %bitcast.1.s_ref, bf16[4,2,256,2048]{3,2,1,0:T(8,128)(2,1)S(1)} %bitcast.107, f32[4,4,256,128]{3,2,1,0:T(8,128)S(1)} %broadcast_in_dim.6.down_ref, ...), custom_call_target="tpu_custom_call" | custom-call | flops 2500000000 | bytes 16777216 | tf_op jit(solution)/shard_map/attend/pallas_call | solution.py:254
  154.3 2.7 collective-permute-done.9.refs_0_
  164.4 2.6 convolution_convert_fusion.9
  169.6 13.0 %collective-permute-done.10 = bf16[256,2048]{1,0:T(8,128)(2,1)S(1)} collective-permute-done((bf16[256,2048]{1,0:T(8,128)(2,1)S(1)}, bf16[256,2048]{1,0:T(8,128)(2,1)S(1)}, u32[]{:S(2)}, u32[]{:S(2)}) %collective-permute-start.10) | collective-permute-done | bytes 1048608 | tf_op jit(solution)/shard_map/ppermute | solution.py:18
  182.5 2.6 fusion.12
  187.3 2.6 fusion.13
  196.7 37.3 %collective-permute-done.15 = f32[512]{0:T(512)S(1)} collective-permute-done((f32[512]{0:T(512)S(1)}, f32[512]{0:T(512)S(1)}, u32[]{:S(2)}, u32[]{:S(2)}) %collective-permute-start.15) | collective-permute-done | bytes 2080 | tf_op jit(solution)/shard_map/ppermute | solution.py:18
  234.1 7.0 multiply_reduce_fusion.2
  247.1 13.2 %unit_forward.4 = (bf16[4,512,1408]{2,1,0:T(8,128)(2,1)S(1)}, bf16[4,512,1408]{2,1,0:T(8,128)(2,1)S(1)}, bf16[4,512,1408]{2,1,0:T(8,128)(2,1)}) custom-call(bf16[512,2048]{1,0:T(8,128)(2,1)} %get-tuple-element.170.refs_0_, bf16[1408,4096]{1,0:T(8,128)(2,1)} %all-gather.9.cloned.1.call-done.refs_1_.refs_2_), custom_call_target="tpu_custom_call" | custom-call | flops 5905580032 | bytes 17956864 | tf_op jit(solution)/shard_map/unit_forward/pallas_call | solution.py:525
  260.3 28.3 %collective-permute-done.19.refs_0_ = bf16[512,2048]{1,0:T(8,128)(2,1)S(1)} collective-permute-done((bf16[512,2048]{1,0:T(8,128)(2,1)}, bf16[512,2048]{1,0:T(8,128)(2,1)S(1)}, u32[]{:S(2)}, u32[]{:S(2)}) %collective-permute-start.19) | collective-permute-done | bytes 2097184 | tf_op jit(solution)/shard_map/ppermute | solution.py:18
  289.0 4.1 collective-permute-done.17.refs_0_
  294.5 3.2 constant_dynamic-update-slice_fusion.13
  299.3 12.7 %unit_forward.5 = (bf16[4,512,1408]{2,1,0:T(8,128)(2,1)S(1)}, bf16[4,512,1408]{2,1,0:T(8,128)(2,1)S(1)}, bf16[4,512,1408]{2,1,0:T(8,128)(2,1)}) custom-call(bf16[512,2048]{1,0:T(8,128)(2,1)} %collective-permute-done.17.refs_0_, ...), custom_call_target="tpu_custom_call", output_to_operand_aliasing={{0}: (2, {}), {1}: (3, {}), {2}: (4, {})} | custom-call | flops 5905580032 | bytes 17956864 | tf_op jit(solution)/shard_map/unit_forward/pallas_call | solution.py:525
  312.1 10.7 %unit_forward.6 = (bf16[4,512,1408]{2,1,0:T(8,128)(2,1)S(1)}, bf16[4,512,1408]{2,1,0:T(8,128)(2,1)S(1)}, bf16[4,512,1408]{2,1,0:T(8,128)(2,1)}) custom-call(bf16[512,2048]{1,0:T(8,128)(2,1)S(1)} %collective-permute-done.19.refs_0_, ...), custom_call_target="tpu_custom_call", output_to_operand_aliasing={{0}: (2, {}), {1}: (3, {}), {2}: (4, {})} | custom-call | flops 5905580032 | bytes 17956864 | tf_op jit(solution)/shard_map/unit_forward/pallas_call | solution.py:525
  337.2 10.6 %unit_forward.7 = (bf16[4,512,1408]{2,1,0:T(8,128)(2,1)S(1)}, bf16[4,512,1408]{2,1,0:T(8,128)(2,1)S(1)}, bf16[4,512,1408]{2,1,0:T(8,128)(2,1)}) custom-call(bf16[256,2048]{1,0:T(8,128)(2,1)S(1)} %collective-permute-done.18.refs_0_, bf16[256,2048]{1,0:T(8,128)(2,1)S(1)} %collective-permute-done.20.refs_1_, ...), custom_call_target="tpu_custom_call", output_to_operand_aliasing={{0}: (3, {}), {1}: (4, {}), {2}: (5, {})} | custom-call | flops 5905580032 | bytes 17956864 | tf_op jit(solution)/shard_map/unit_forward/pallas_call | solution.py:525
  355.2 17.9 %convolution_convert_fusion.4 = bf16[1408,2048]{1,0:T(8,128)(2,1)} fusion(bf16[2048,1408]{1,0:T(8,128)(2,1)} %bitcast.116, bf16[2048,2048]{1,0:T(8,128)(2,1)} %constant_dynamic-update-slice_fusion.5), kind=kOutput, calls=%fused_computation.4 | convolution fusion | flops 11814043648 | bytes 19922944 | tf_op jit(solution)/shard_map/dot_general | solution.py:104
  373.3 20.4 %unit_backward.4 = (bf16[4,512,1408]{2,1,0:T(8,128)(2,1)}, bf16[4,512,1408]{2,1,0:T(8,128)(2,1)}, bf16[256,2048]{1,0:T(8,128)(2,1)S(1)}, bf16[256,2048]{1,0:T(8,...) custom-call(bf16[256,2048]{1,0:T(8,128)(2,1)} %copy-done.40, bf16[256,2048]{1,0:T(8,128)(2,1)} %copy-done.39, ...), custom_call_target="tpu_custom_call" | custom-call | flops 11811160064 | bytes 30801920 | tf_op jit(solution)/shard_map/unit_backward/pallas_call | solution.py:567
  397.8 21.9 %unit_backward.5 = (bf16[4,512,1408]{2,1,0:T(8,128)(2,1)}, bf16[4,512,1408]{2,1,0:T(8,128)(2,1)}, bf16[512,2048]{1,0:T(8,128)(2,1)}, bf16[512,2048]{1,0:T(8,128)(2,1)}) custom-call(bf16[512,2048]{1,0:T(8,128)(2,1)} %collective-permute-done.8.refs_0_, ...), custom_call_target="tpu_custom_call", output_to_operand_aliasing={{0}: (6, {}), {1}: (7, {})} | custom-call | flops 11811160064 | bytes 30801920 | tf_op jit(solution)/shard_map/unit_backward/pallas_call | solution.py:567
  419.7 21.7 %unit_backward.6 = (bf16[4,512,1408]{2,1,0:T(8,128)(2,1)}, bf16[4,512,1408]{2,1,0:T(8,128)(2,1)}, bf16[512,2048]{1,0:T(8,128)(2,1)}, bf16[512,2048]{1,0:T(8,128)(2,1)}) custom-call(bf16[512,2048]{1,0:T(8,128)(2,1)} %collective-permute-done.9.refs_0_, ...), custom_call_target="tpu_custom_call", output_to_operand_aliasing={{0}: (6, {}), {1}: (7, {})} | custom-call | flops 11811160064 | bytes 30801920 | tf_op jit(solution)/shard_map/unit_backward/pallas_call | solution.py:567
  441.5 3.3 fusion.15
  444.9 2.6 fusion.14
  449.2 20.4 %unit_backward.7 = (bf16[4,512,1408]{2,1,0:T(8,128)(2,1)}, bf16[4,512,1408]{2,1,0:T(8,128)(2,1)}, bf16[512,2048]{1,0:T(8,128)(2,1)S(1)}, bf16[512,2048]{1,0:T(8,128)(2,1)}) custom-call(bf16[512,2048]{1,0:T(8,128)(2,1)} %fusion.1.refs_0_, ...), custom_call_target="tpu_custom_call", output_to_operand_aliasing={{0}: (6, {}), {1}: (7, {})} | custom-call | flops 11811160064 | bytes 30801920 | tf_op jit(solution)/shard_map/unit_backward/pallas_call | solution.py:567
  469.6 18.3 %convolution_convert_fusion.3 = bf16[1408,2048]{1,0:T(8,128)(2,1)} fusion(bf16[2048,1408]{1,0:T(8,128)(2,1)} %bitcast.117, bf16[2048,2048]{1,0:T(8,128)(2,1)} %constant_dynamic-update-slice_fusion.10), kind=kOutput, calls=%fused_computation.3 | convolution fusion | flops 11814043648 | bytes 19922944 | tf_op jit(solution)/shard_map/dot_general | solution.py:104
  488.0 3.6 convert_add_fusion.2
  493.8 6.3 multiply_reduce_fusion
  500.4 14.0 %convolution_convert_fusion.2 = bf16[1408,2048]{1,0:T(8,128)(2,1)} fusion(bf16[2048,1408]{1,0:T(8,128)(2,1)S(1)} %bitcast.120, bf16[2048,2048]{1,0:T(8,128)(2,1)S(1)} %bitcast.132), kind=kOutput, calls=%fused_computation.2 | convolution fusion | flops 11814043648 | bytes 19922944 | tf_op jit(solution)/shard_map/dot_general | solution.py:104
  517.7 38.6 %collective-permute-done.30 = bf16[512,2048]{1,0:T(8,128)(2,1)S(1)} collective-permute-done((bf16[512,2048]{1,0:T(8,128)(2,1)S(1)}, bf16[512,2048]{1,0:T(8,128)(2,1)S(1)}, u32[]{:S(2)}, u32[]{:S(2)}) %collective-permute-start.30) | collective-permute-done | bytes 2097184 | tf_op jit(solution)/shard_map/ppermute | solution.py:18
  566.8 11.0 %collective-permute-done.37 = f32[512]{0:T(512)S(1)} collective-permute-done((f32[512]{0:T(512)S(1)}, f32[512]{0:T(512)S(1)}, u32[]{:S(2)}, u32[]{:S(2)}) %collective-permute-start.37) | collective-permute-done | bytes 2080 | tf_op jit(solution)/shard_map/ppermute | solution.py:18
  583.1 2.8 fusion.17
  593.0 7.2 fusion.35
  600.6 28.3 %attend_back.1 = bf16[4,2,256,2048]{3,2,1,0:T(8,128)(2,1)} custom-call(s32[1]{0:T(128)} %bitcast.1.s_ref, bf16[4,2,256,2048]{3,2,1,0:T(8,128)(2,1)} %bitcast.108, bf16[4,2,256,512]{3,2,1,0:T(8,128)(2,1)S(1)} %copy-done.13, f32[4,2,256,512]{3,2,1,0:T(8,128)S(1)} %bitcast.115, f32[4,2,256,128]{3,2,1,0:T(8,128)S(1)} %broadcast_in_dim.8.inner_ref, ...), custom_call_target="tpu_custom_call" | custom-call | flops 8000000000 | bytes 33554432 | tf_op jit(solution)/shard_map/attend_back/pallas_call | solution.py:292
  628.9 3.1 multiply_convert_fusion
  635.8 9.9 %convolution_convert_fusion.8 = bf16[2048,512]{1,0:T(8,128)(2,1)} fusion(bf16[2048,2048]{1,0:T(8,128)(2,1)} %constant_dynamic-update-slice_fusion.15, bf16[2048,512]{1,0:T(8,128)(2,1)} %bitcast.112), kind=kOutput, calls=%fused_computation.33 | convolution fusion | flops 4296015872 | bytes 12582912 | tf_op jit(solution)/shard_map/dot_general | solution.py:104
  646.0 10.7 %collective-permute-done.39.refs_2_ = bf16[352,2048]{1,0:T(8,128)(2,1)S(1)} collective-permute-done((bf16[352,2048]{1,0:T(8,128)(2,1)S(1)}, bf16[352,2048]{1,0:T(8,128)(2,1)S(1)}, u32[]{:S(2)}, u32[]{:S(2)}) %collective-permute-start.39) | collective-permute-done | bytes 1441824 | tf_op jit(solution)/shard_map/ppermute | solution.py:18
  657.9 23.8 %convolution_convert_fusion = bf16[2048,2048]{1,0:T(8,128)(2,1)} fusion(bf16[2048,2048]{1,0:T(8,128)(2,1)} %bitcast.155, bf16[2048,2048]{1,0:T(8,128)(2,1)} %constant_dynamic-update-slice_fusion), kind=kOutput, calls=%fused_computation | convolution fusion | flops 17184063488 | bytes 25165824 | tf_op jit(solution)/shard_map/dot_general | solution.py:104
  688.8 12.8 %collective-permute-done.41.refs_3_ = bf16[176,2048]{1,0:T(8,128)(2,1)} collective-permute-done((bf16[176,2048]{1,0:T(8,128)(2,1)}, bf16[176,2048]{1,0:T(8,128)(2,1)}, u32[]{:S(2)}, u32[]{:S(2)}) %collective-permute-start.41) | collective-permute-done | bytes 720928 | tf_op jit(solution)/shard_map/ppermute | solution.py:18
  701.6 6.3 convolution_convert_fusion.15
  708.0 7.2 convolution_convert_fusion.14
  715.8 5.7 convolution_convert_fusion.5
  721.6 6.1 convolution_convert_fusion.6
  730.2 2.6 fusion.19
  733.0 7.0 collective-permute-done.44
  739.9 2.9 fusion.18
  744.9 29.0 %reduce-scatter.14.cloned.1.call-done.refs_0_ = bf16[256,2048]{1,0:T(8,128)(2,1)} async-done(((bf16[2048,2048]{1,0:T(8,128)(2,1)}), bf16[256,2048]{1,0:T(8,128)(2,1)}) %reduce-scatter.14.cloned.1.call-update) | async-done | bytes 1048592 | tf_op jit(solution)/shard_map/reduce_scatter | solution.py:865
  776.8 8.5 %convolution_convert_fusion.7 = bf16[512,2048]{1,0:T(8,128)(2,1)S(1)} fusion(bf16[2048,2048]{1,0:T(8,128)(2,1)} %all-gather.5.cloned.1.call-done, bf16[2048,2048]{1,0:T(8,128)(2,1)} %bitcast.158), kind=kOutput, calls=%fused_computation.32 | convolution fusion | flops 4296015872 | bytes 12582912 | tf_op jit(solution)/shard_map/dot_general | solution.py:98
  788.6 3.5 convert_add_fusion
  792.1 8.1 collective-permute-done.49.refs_2_
  807.2 3.0 collective-permute-done.56
  812.2 3.5 collective-permute-done.54
  818.2 4.2 place_rows.4
  822.4 4.3 place_rows.5
  826.7 4.4 place_rows.3
  835.3 4.4 sort_rows.1
  (358 shorter events, 158.9 us)
Async XLA Ops:
  7.2 108.6 %all-gather.5.cloned.1.call-start = ((), (), s32[]{:S(2)}) async-start(), calls=%async_computation.5 | async-start | bytes 9437184 | tf_op jit(solution)/shard_map/all_gather | solution.py:626
  20.4 136.6 %all-gather.7.cloned.1.call-start = ((), (), s32[]{:S(2)}) async-start(), calls=%async_computation.6 | async-start | bytes 2359296 | tf_op jit(solution)/shard_map/all_gather | solution.py:813
  24.4 222.6 %all-gather.9.cloned.1.call-start = ((), (), s32[]{:S(2)}) async-start(), calls=%async_computation.7 | async-start | bytes 12976128 | tf_op jit(solution)/shard_map/all_gather | solution.py:816
  27.1 346.1 %all-gather.11.cloned.1.call-start = ((), (), s32[]{:S(2)}) async-start(), calls=%async_computation.8 | async-start | bytes 6488064 | tf_op jit(solution)/shard_map/all_gather | solution.py:819
  27.2 51.8 %collective-permute-start.1 = (bf16[512,2048]{1,0:T(8,128)(2,1)}, bf16[512,2048]{1,0:T(8,128)(2,1)}, u32[]{:S(2)}, u32[]{:S(2)}) collective-permute-start(bf16[512,2048]{1,0:T(8,128)(2,1)} %get-tuple-element.196), channel_id=1, source_target_pairs={{0,16},{8,24},{16,0},{24,8},{1,17},{9,25},{17,1},{25,9},{2,18},{10... | collective-permute-start | bytes 6291464 | tf_op jit(solution)/shard_map/ppermute | solution.py:18
  31.0 51.9 %collective-permute-start = (bf16[512,2048]{1,0:T(8,128)(2,1)}, bf16[512,2048]{1,0:T(8,128)(2,1)}, u32[]{:S(2)}, u32[]{:S(2)}) collective-permute-start(bf16[512,2048]{1,0:T(8,128)(2,1)} %get-tuple-element.196), channel_id=1, source_target_pairs={{0,8},{8,0},{16,24},{24,16},{1,9},{9,1},{17,25},{25,17},{2,10},{10... | collective-permute-start | bytes 6291464 | tf_op jit(solution)/shard_map/ppermute | solution.py:18
  32.6 45.4 %collective-permute-start.5 = (f32[1,1024]{1,0:T(1,128)S(1)}, f32[1,1024]{1,0:T(1,128)S(1)}, u32[]{:S(2)}, u32[]{:S(2)}) collective-permute-start(f32[1,1024]{1,0:T(1,128)S(1)} %get-tuple-element.185), channel_id=1, source_target_pairs={{0,8},{8,0},{16,24},{24,16},{1,9},{9,1},{17,25},{25,17},{2,10},{10... | collective-permute-start | bytes 12296 | tf_op jit(solution)/shard_map/ppermute | solution.py:18
  33.2 44.8 %collective-permute-start.7 = (f32[1,1024]{1,0:T(1,128)S(1)}, f32[1,1024]{1,0:T(1,128)S(1)}, u32[]{:S(2)}, u32[]{:S(2)}) collective-permute-start(f32[1,1024]{1,0:T(1,128)S(1)} %get-tuple-element.187), channel_id=1, source_target_pairs={{0,16},{8,24},{16,0},{24,8},{1,17},{9,25},{17,1},{25,9},{2,18},{10... | collective-permute-start | bytes 12296 | tf_op jit(solution)/shard_map/ppermute | solution.py:18
  33.2 45.6 %collective-permute-start.6 = (f32[1,1024]{1,0:T(1,128)S(1)}, f32[1,1024]{1,0:T(1,128)S(1)}, u32[]{:S(2)}, u32[]{:S(2)}) collective-permute-start(f32[1,1024]{1,0:T(1,128)S(1)} %get-tuple-element.188), channel_id=1, source_target_pairs={{0,24},{8,16},{16,8},{24,0},{1,25},{9,17},{17,9},{25,1},{2,26},{10... | collective-permute-start | bytes 12296 | tf_op jit(solution)/shard_map/ppermute | solution.py:18
  81.3 25.3 %collective-permute-start.3 = (bf16[256,2048]{1,0:T(8,128)(2,1)}, bf16[256,2048]{1,0:T(8,128)(2,1)}, u32[]{:S(2)}, u32[]{:S(2)}) collective-permute-start(bf16[256,2048]{1,0:T(8,128)(2,1)} %slice.291), channel_id=1, source_target_pairs={{0,8},{8,0},{16,24},{24,16},{1,9},{9,1},{17,25},{25,17},{2,10},{10... | collective-permute-start | bytes 3145736 | tf_op jit(solution)/shard_map/ppermute | solution.py:18
  85.3 25.0 %collective-permute-start.2 = (bf16[256,2048]{1,0:T(8,128)(2,1)}, bf16[256,2048]{1,0:T(8,128)(2,1)}, u32[]{:S(2)}, u32[]{:S(2)}) collective-permute-start(bf16[256,2048]{1,0:T(8,128)(2,1)} %slice.290), channel_id=1, source_target_pairs={{0,16},{8,24},{16,0},{24,8},{1,17},{9,25},{17,1},{25,9},{2,18},{10... | collective-permute-start | bytes 3145736 | tf_op jit(solution)/shard_map/ppermute | solution.py:18
  110.3 46.6 %collective-permute-start.9 = (bf16[512,2048]{1,0:T(8,128)(2,1)}, bf16[512,2048]{1,0:T(8,128)(2,1)}, u32[]{:S(2)}, u32[]{:S(2)}) collective-permute-start(bf16[512,2048]{1,0:T(8,128)(2,1)} %fusion.1.refs_0_), channel_id=1, source_target_pairs={{0,16},{8,24},{16,0},{24,8},{1,17},{9,25},{17,1},{25,9},{2,18},{10... | collective-permute-start | bytes 6291464 | tf_op jit(solution)/shard_map/ppermute | solution.py:18
  110.8 46.2 %collective-permute-start.8 = (bf16[512,2048]{1,0:T(8,128)(2,1)}, bf16[512,2048]{1,0:T(8,128)(2,1)}, u32[]{:S(2)}, u32[]{:S(2)}) collective-permute-start(bf16[512,2048]{1,0:T(8,128)(2,1)} %fusion.1.refs_0_), channel_id=1, source_target_pairs={{0,8},{8,0},{16,24},{24,16},{1,9},{9,1},{17,25},{25,17},{2,10},{10... | collective-permute-start | bytes 6291464 | tf_op jit(solution)/shard_map/ppermute | solution.py:18
  159.6 23.0 %collective-permute-start.10 = (bf16[256,2048]{1,0:T(8,128)(2,1)S(1)}, bf16[256,2048]{1,0:T(8,128)(2,1)S(1)}, u32[]{:S(2)}, u32[]{:S(2)}) collective-permute-start(bf16[256,2048]{1,0:T(8,128)(2,1)S(1)} %convolution_convert_fusion.13), channel_id=1, source_target_pairs={{0,16},{8,24},{16,0},{24,8},{1,17},{9,25},{17,1},{25,9},{2,18},{10... | collective-permute-start | bytes 3145736 | tf_op jit(solution)/shard_map/ppermute | solution.py:18
  163.7 23.6 %collective-permute-start.12 = (bf16[256,2048]{1,0:T(8,128)(2,1)S(1)}, bf16[256,2048]{1,0:T(8,128)(2,1)S(1)}, u32[]{:S(2)}, u32[]{:S(2)}) collective-permute-start(bf16[256,2048]{1,0:T(8,128)(2,1)S(1)} %convolution_convert_fusion.12), channel_id=1, source_target_pairs={{0,8},{8,0},{16,24},{24,16},{1,9},{9,1},{17,25},{25,17},{2,10},{10... | collective-permute-start | bytes 3145736 | tf_op jit(solution)/shard_map/ppermute | solution.py:18
  185.1 48.9 %collective-permute-start.11 = (bf16[512,2048]{1,0:T(8,128)(2,1)}, bf16[512,2048]{1,0:T(8,128)(2,1)}, u32[]{:S(2)}, u32[]{:S(2)}) collective-permute-start(bf16[512,2048]{1,0:T(8,128)(2,1)} %fusion.12), channel_id=1, source_target_pairs={{0,8},{8,0},{16,24},{24,16},{1,9},{9,1},{17,25},{25,17},{2,10},{10... | collective-permute-start | bytes 6291464 | tf_op jit(solution)/shard_map/ppermute | solution.py:18
  189.9 44.2 %collective-permute-start.13 = (bf16[512,2048]{1,0:T(8,128)(2,1)}, bf16[512,2048]{1,0:T(8,128)(2,1)}, u32[]{:S(2)}, u32[]{:S(2)}) collective-permute-start(bf16[512,2048]{1,0:T(8,128)(2,1)} %fusion.13), channel_id=1, source_target_pairs={{0,16},{8,24},{16,0},{24,8},{1,17},{9,25},{17,1},{25,9},{2,18},{10... | collective-permute-start | bytes 6291464 | tf_op jit(solution)/shard_map/ppermute | solution.py:18
  192.1 41.9 %collective-permute-start.15 = (f32[512]{0:T(512)S(1)}, f32[512]{0:T(512)S(1)}, u32[]{:S(2)}, u32[]{:S(2)}) collective-permute-start(f32[512]{0:T(512)S(1)} %bitcast.152), channel_id=1, source_target_pairs={{0,16},{8,24},{16,0},{24,8},{1,17},{9,25},{17,1},{25,9},{2,18},{10... | collective-permute-start | bytes 6152 | tf_op jit(solution)/shard_map/ppermute | solution.py:18
  193.6 40.4 %collective-permute-start.16 = (f32[512]{0:T(512)S(1)}, f32[512]{0:T(512)S(1)}, u32[]{:S(2)}, u32[]{:S(2)}) collective-permute-start(f32[512]{0:T(512)S(1)} %bitcast.151), channel_id=1, source_target_pairs={{0,24},{8,16},{16,8},{24,0},{1,25},{9,17},{17,9},{25,1},{2,26},{10... | collective-permute-start | bytes 6152 | tf_op jit(solution)/shard_map/ppermute | solution.py:18
  194.3 39.7 %collective-permute-start.14 = (f32[512]{0:T(512)S(1)}, f32[512]{0:T(512)S(1)}, u32[]{:S(2)}, u32[]{:S(2)}) collective-permute-start(f32[512]{0:T(512)S(1)} %bitcast.150), channel_id=1, source_target_pairs={{0,8},{8,0},{16,24},{24,16},{1,9},{9,1},{17,25},{25,17},{2,10},{10... | collective-permute-start | bytes 6152 | tf_op jit(solution)/shard_map/ppermute | solution.py:18
  196.6 435.4 %reduce-scatter.6.cloned.1.call-start = ((), (), s32[]{:S(2)}) async-start(), calls=%async_computation.9 | async-start | bytes 6488064 | tf_op jit(solution)/shard_map/reduce_scatter | solution.py:865
  244.3 44.3 %collective-permute-start.19 = (bf16[512,2048]{1,0:T(8,128)(2,1)}, bf16[512,2048]{1,0:T(8,128)(2,1)S(1)}, u32[]{:S(2)}, u32[]{:S(2)}) collective-permute-start(bf16[512,2048]{1,0:T(8,128)(2,1)} %get-tuple-element.170.refs_0_), channel_id=1, source_target_pairs={{0,16},{8,24},{16,0},{24,8},{1,17},{9,25},{17,1},{25,9},{2,18},{10... | collective-permute-start | bytes 6291464 | tf_op jit(solution)/shard_map/ppermute | solution.py:18
  246.1 47.0 %collective-permute-start.17 = (bf16[512,2048]{1,0:T(8,128)(2,1)}, bf16[512,2048]{1,0:T(8,128)(2,1)}, u32[]{:S(2)}, u32[]{:S(2)}) collective-permute-start(bf16[512,2048]{1,0:T(8,128)(2,1)} %get-tuple-element.170.refs_0_), channel_id=1, source_target_pairs={{0,8},{8,0},{16,24},{24,16},{1,9},{9,1},{17,25},{25,17},{2,10},{10... | collective-permute-start | bytes 6291464 | tf_op jit(solution)/shard_map/ppermute | solution.py:18
  288.7 34.0 %collective-permute-start.20 = (bf16[256,2048]{1,0:T(8,128)(2,1)S(1)}, bf16[256,2048]{1,0:T(8,128)(2,1)S(1)}, u32[]{:S(2)}, u32[]{:S(2)}) collective-permute-start(bf16[256,2048]{1,0:T(8,128)(2,1)S(1)} %slice.307), channel_id=1, source_target_pairs={{0,8},{8,0},{16,24},{24,16},{1,9},{9,1},{17,25},{25,17},{2,10},{10... | collective-permute-start | bytes 3145736 | tf_op jit(solution)/shard_map/ppermute | solution.py:18
  294.4 28.4 %collective-permute-start.18 = (bf16[256,2048]{1,0:T(8,128)(2,1)S(1)}, bf16[256,2048]{1,0:T(8,128)(2,1)S(1)}, u32[]{:S(2)}, u32[]{:S(2)}) collective-permute-start(bf16[256,2048]{1,0:T(8,128)(2,1)S(1)} %slice.306), channel_id=1, source_target_pairs={{0,16},{8,24},{16,0},{24,8},{1,17},{9,25},{17,1},{25,9},{2,18},{10... | collective-permute-start | bytes 3145736 | tf_op jit(solution)/shard_map/ppermute | solution.py:18
  325.5 28.6 %collective-permute-start.22 = (bf16[256,2048]{1,0:T(8,128)(2,1)S(1)}, bf16[256,2048]{1,0:T(8,128)(2,1)S(1)}, u32[]{:S(2)}, u32[]{:S(2)}) collective-permute-start(bf16[256,2048]{1,0:T(8,128)(2,1)S(1)} %slice.246), channel_id=1, source_target_pairs={{0,8},{8,0},{16,24},{24,16},{1,9},{9,1},{17,25},{25,17},{2,10},{10... | collective-permute-start | bytes 3145736 | tf_op jit(solution)/shard_map/ppermute | solution.py:18
  325.9 26.9 %collective-permute-start.21 = (bf16[256,2048]{1,0:T(8,128)(2,1)S(1)}, bf16[256,2048]{1,0:T(8,128)(2,1)S(1)}, u32[]{:S(2)}, u32[]{:S(2)}) collective-permute-start(bf16[256,2048]{1,0:T(8,128)(2,1)S(1)} %slice.245), channel_id=1, source_target_pairs={{0,16},{8,24},{16,0},{24,8},{1,17},{9,25},{17,1},{25,9},{2,18},{10... | collective-permute-start | bytes 3145736 | tf_op jit(solution)/shard_map/ppermute | solution.py:18
  373.2 258.8 %reduce-scatter.8.cloned.1.call-start = ((), (), s32[]{:S(2)}) async-start(), calls=%async_computation.10 | async-start | bytes 6488064 | tf_op jit(solution)/shard_map/reduce_scatter | solution.py:865
  393.7 47.7 %collective-permute-start.23 = (bf16[256,2048]{1,0:T(8,128)(2,1)S(1)}, bf16[256,2048]{1,0:T(8,128)(2,1)S(1)}, u32[]{:S(2)}, u32[]{:S(2)}) collective-permute-start(bf16[256,2048]{1,0:T(8,128)(2,1)S(1)} %get-tuple-element.109), channel_id=1, source_target_pairs={{0,8},{8,0},{16,24},{24,16},{1,9},{9,1},{17,25},{25,17},{2,10},{10... | collective-permute-start | bytes 3145736 | tf_op jit(solution)/shard_map/ppermute | solution.py:18
  395.5 46.0 %collective-permute-start.24 = (bf16[256,2048]{1,0:T(8,128)(2,1)S(1)}, bf16[256,2048]{1,0:T(8,128)(2,1)S(1)}, u32[]{:S(2)}, u32[]{:S(2)}) collective-permute-start(bf16[256,2048]{1,0:T(8,128)(2,1)S(1)} %get-tuple-element.110), channel_id=1, source_target_pairs={{0,16},{8,24},{16,0},{24,8},{1,17},{9,25},{17,1},{25,9},{2,18},{10... | collective-permute-start | bytes 3145736 | tf_op jit(solution)/shard_map/ppermute | solution.py:18
  395.5 46.0 %collective-permute-start.25 = (bf16[256,2048]{1,0:T(8,128)(2,1)S(1)}, bf16[256,2048]{1,0:T(8,128)(2,1)S(1)}, u32[]{:S(2)}, u32[]{:S(2)}) collective-permute-start(bf16[256,2048]{1,0:T(8,128)(2,1)S(1)} %get-tuple-element.111), channel_id=1, source_target_pairs={{0,8},{8,0},{16,24},{24,16},{1,9},{9,1},{17,25},{25,17},{2,10},{10... | collective-permute-start | bytes 3145736 | tf_op jit(solution)/shard_map/ppermute | solution.py:18
  395.8 45.6 %collective-permute-start.26 = (bf16[256,2048]{1,0:T(8,128)(2,1)}, bf16[256,2048]{1,0:T(8,128)(2,1)S(1)}, u32[]{:S(2)}, u32[]{:S(2)}) collective-permute-start(bf16[256,2048]{1,0:T(8,128)(2,1)} %get-tuple-element.112), channel_id=1, source_target_pairs={{0,16},{8,24},{16,0},{24,8},{1,17},{9,25},{17,1},{25,9},{2,18},{10... | collective-permute-start | bytes 3145736 | tf_op jit(solution)/shard_map/ppermute | solution.py:18
  444.8 43.1 %collective-permute-start.28 = (bf16[512,2048]{1,0:T(8,128)(2,1)}, bf16[512,2048]{1,0:T(8,128)(2,1)}, u32[]{:S(2)}, u32[]{:S(2)}) collective-permute-start(bf16[512,2048]{1,0:T(8,128)(2,1)} %fusion.15), channel_id=1, source_target_pairs={{0,16},{8,24},{16,0},{24,8},{1,17},{9,25},{17,1},{25,9},{2,18},{10... | collective-permute-start | bytes 6291464 | tf_op jit(solution)/shard_map/ppermute | solution.py:18
  447.5 40.5 %collective-permute-start.27 = (bf16[512,2048]{1,0:T(8,128)(2,1)}, bf16[512,2048]{1,0:T(8,128)(2,1)}, u32[]{:S(2)}, u32[]{:S(2)}) collective-permute-start(bf16[512,2048]{1,0:T(8,128)(2,1)} %fusion.14), channel_id=1, source_target_pairs={{0,8},{8,0},{16,24},{24,16},{1,9},{9,1},{17,25},{25,17},{2,10},{10... | collective-permute-start | bytes 6291464 | tf_op jit(solution)/shard_map/ppermute | solution.py:18
  514.4 171.6 %reduce-scatter.10.cloned.1.call-start = ((), (), s32[]{:S(2)}) async-start(), calls=%async_computation.11 | async-start | bytes 6488064 | tf_op jit(solution)/shard_map/reduce_scatter | solution.py:865
  515.2 217.8 %reduce-scatter.12.cloned.1.call-start = ((), (), s32[]{:S(2)}) async-start(), calls=%async_computation.12 | async-start | bytes 2359296 | tf_op jit(solution)/shard_map/reduce_scatter | solution.py:865
  515.4 40.9 %collective-permute-start.30 = (bf16[512,2048]{1,0:T(8,128)(2,1)S(1)}, bf16[512,2048]{1,0:T(8,128)(2,1)S(1)}, u32[]{:S(2)}, u32[]{:S(2)}) collective-permute-start(bf16[512,2048]{1,0:T(8,128)(2,1)S(1)} %get-tuple-element.135), channel_id=1, source_target_pairs={{0,16},{8,24},{16,0},{24,8},{1,17},{9,25},{17,1},{25,9},{2,18},{10... | collective-permute-start | bytes 6291464 | tf_op jit(solution)/shard_map/ppermute | solution.py:18
  517.4 41.5 %collective-permute-start.29 = (bf16[512,2048]{1,0:T(8,128)(2,1)S(1)}, bf16[512,2048]{1,0:T(8,128)(2,1)S(1)}, u32[]{:S(2)}, u32[]{:S(2)}) collective-permute-start(bf16[512,2048]{1,0:T(8,128)(2,1)S(1)} %get-tuple-element.135), channel_id=1, source_target_pairs={{0,8},{8,0},{16,24},{24,16},{1,9},{9,1},{17,25},{25,17},{2,10},{10... | collective-permute-start | bytes 6291464 | tf_op jit(solution)/shard_map/ppermute | solution.py:18
  561.0 22.1 %collective-permute-start.32 = (bf16[256,2048]{1,0:T(8,128)(2,1)}, bf16[256,2048]{1,0:T(8,128)(2,1)}, u32[]{:S(2)}, u32[]{:S(2)}) collective-permute-start(bf16[256,2048]{1,0:T(8,128)(2,1)} %slice.250), channel_id=1, source_target_pairs={{0,8},{8,0},{16,24},{24,16},{1,9},{9,1},{17,25},{25,17},{2,10},{10... | collective-permute-start | bytes 3145736 | tf_op jit(solution)/shard_map/ppermute | solution.py:18
  561.2 21.9 %collective-permute-start.31 = (bf16[256,2048]{1,0:T(8,128)(2,1)}, bf16[256,2048]{1,0:T(8,128)(2,1)}, u32[]{:S(2)}, u32[]{:S(2)}) collective-permute-start(bf16[256,2048]{1,0:T(8,128)(2,1)} %slice.249), channel_id=1, source_target_pairs={{0,16},{8,24},{16,0},{24,8},{1,17},{9,25},{17,1},{25,9},{2,18},{10... | collective-permute-start | bytes 3145736 | tf_op jit(solution)/shard_map/ppermute | solution.py:18
  563.3 14.5 %collective-permute-start.37 = (f32[512]{0:T(512)S(1)}, f32[512]{0:T(512)S(1)}, u32[]{:S(2)}, u32[]{:S(2)}) collective-permute-start(f32[512]{0:T(512)S(1)} %multiply_multiply_fusion.1), channel_id=1, source_target_pairs={{0,24},{8,16},{16,8},{24,0},{1,25},{9,17},{17,9},{25,1},{2,26},{10... | collective-permute-start | bytes 6152 | tf_op jit(solution)/shard_map/ppermute | solution.py:18
  586.0 42.9 %collective-permute-start.34 = (bf16[512,2048]{1,0:T(8,128)(2,1)}, bf16[512,2048]{1,0:T(8,128)(2,1)S(1)}, u32[]{:S(2)}, u32[]{:S(2)}) collective-permute-start(bf16[512,2048]{1,0:T(8,128)(2,1)} %fusion.17), channel_id=1, source_target_pairs={{0,16},{8,24},{16,0},{24,8},{1,17},{9,25},{17,1},{25,9},{2,18},{10... | collective-permute-start | bytes 6291464 | tf_op jit(solution)/shard_map/ppermute | solution.py:18
  587.3 41.6 %collective-permute-start.33 = (bf16[512,2048]{1,0:T(8,128)(2,1)S(1)}, bf16[512,2048]{1,0:T(8,128)(2,1)S(1)}, u32[]{:S(2)}, u32[]{:S(2)}) collective-permute-start(bf16[512,2048]{1,0:T(8,128)(2,1)S(1)} %fusion.16), channel_id=1, source_target_pairs={{0,8},{8,0},{16,24},{24,16},{1,9},{9,1},{17,25},{25,17},{2,10},{10... | collective-permute-start | bytes 6291464 | tf_op jit(solution)/shard_map/ppermute | solution.py:18
  633.5 23.2 %collective-permute-start.39 = (bf16[352,2048]{1,0:T(8,128)(2,1)S(1)}, bf16[352,2048]{1,0:T(8,128)(2,1)S(1)}, u32[]{:S(2)}, u32[]{:S(2)}) collective-permute-start(bf16[352,2048]{1,0:T(8,128)(2,1)S(1)} %pad_maximum_fusion.1.refs_0_), channel_id=1, source_target_pairs={{0,16},{8,24},{16,0},{24,8},{1,17},{9,25},{17,1},{25,9},{2,18},{10... | collective-permute-start | bytes 4325384 | tf_op jit(solution)/shard_map/ppermute | solution.py:18
  635.0 22.9 %collective-permute-start.38 = (bf16[352,2048]{1,0:T(8,128)(2,1)S(1)}, bf16[352,2048]{1,0:T(8,128)(2,1)}, u32[]{:S(2)}, u32[]{:S(2)}) collective-permute-start(bf16[352,2048]{1,0:T(8,128)(2,1)S(1)} %pad_maximum_fusion.1.refs_0_), channel_id=1, source_target_pairs={{0,8},{8,0},{16,24},{24,16},{1,9},{9,1},{17,25},{25,17},{2,10},{10... | collective-permute-start | bytes 4325384 | tf_op jit(solution)/shard_map/ppermute | solution.py:18
  645.7 128.2 %reduce-scatter.14.cloned.1.call-start = ((), (), s32[]{:S(2)}) async-start(), calls=%async_computation.13 | async-start | bytes 9437184 | tf_op jit(solution)/shard_map/reduce_scatter | solution.py:865
  682.7 18.9 %collective-permute-start.41 = (bf16[176,2048]{1,0:T(8,128)(2,1)}, bf16[176,2048]{1,0:T(8,128)(2,1)}, u32[]{:S(2)}, u32[]{:S(2)}) collective-permute-start(bf16[176,2048]{1,0:T(8,128)(2,1)} %slice.309), channel_id=1, source_target_pairs={{0,8},{8,0},{16,24},{24,16},{1,9},{9,1},{17,25},{25,17},{2,10},{10... | collective-permute-start | bytes 2162696 | tf_op jit(solution)/shard_map/ppermute | solution.py:18
  685.0 16.5 %collective-permute-start.40 = (bf16[176,2048]{1,0:T(8,128)(2,1)}, bf16[176,2048]{1,0:T(8,128)(2,1)}, u32[]{:S(2)}, u32[]{:S(2)}) collective-permute-start(bf16[176,2048]{1,0:T(8,128)(2,1)} %slice.308), channel_id=1, source_target_pairs={{0,16},{8,24},{16,0},{24,8},{1,17},{9,25},{17,1},{25,9},{2,18},{10... | collective-permute-start | bytes 2162696 | tf_op jit(solution)/shard_map/ppermute | solution.py:18
  686.0 47.0 %collective-permute-start.43 = (bf16[176,2048]{1,0:T(8,128)(2,1)}, bf16[176,2048]{1,0:T(8,128)(2,1)}, u32[]{:S(2)}, u32[]{:S(2)}) collective-permute-start(bf16[176,2048]{1,0:T(8,128)(2,1)} %reduce-scatter.10.cloned.1.call-done.refs_0_), channel_id=1, source_target_pairs={{0,16},{8,24},{16,0},{24,8},{1,17},{9,25},{17,1},{25,9},{2,18},{10... | collective-permute-start | bytes 2162696 | tf_op jit(solution)/shard_map/ppermute | solution.py:18
  687.1 45.9 %collective-permute-start.42 = (bf16[176,2048]{1,0:T(8,128)(2,1)}, bf16[176,2048]{1,0:T(8,128)(2,1)}, u32[]{:S(2)}, u32[]{:S(2)}) collective-permute-start(bf16[176,2048]{1,0:T(8,128)(2,1)} %reduce-scatter.10.cloned.1.call-done.refs_0_), channel_id=1, source_target_pairs={{0,8},{8,0},{16,24},{24,16},{1,9},{9,1},{17,25},{25,17},{2,10},{10... | collective-permute-start | bytes 2162696 | tf_op jit(solution)/shard_map/ppermute | solution.py:18
  707.9 22.3 %collective-permute-start.46 = (bf16[256,2048]{1,0:T(8,128)(2,1)S(1)}, bf16[256,2048]{1,0:T(8,128)(2,1)S(1)}, u32[]{:S(2)}, u32[]{:S(2)}) collective-permute-start(bf16[256,2048]{1,0:T(8,128)(2,1)S(1)} %convolution_convert_fusion.15), channel_id=1, source_target_pairs={{0,8},{8,0},{16,24},{24,16},{1,9},{9,1},{17,25},{25,17},{2,10},{10... | collective-permute-start | bytes 3145736 | tf_op jit(solution)/shard_map/ppermute | solution.py:18
  715.2 24.7 %collective-permute-start.44 = (bf16[256,2048]{1,0:T(8,128)(2,1)}, bf16[256,2048]{1,0:T(8,128)(2,1)}, u32[]{:S(2)}, u32[]{:S(2)}) collective-permute-start(bf16[256,2048]{1,0:T(8,128)(2,1)} %convolution_convert_fusion.14), channel_id=1, source_target_pairs={{0,16},{8,24},{16,0},{24,8},{1,17},{9,25},{17,1},{25,9},{2,18},{10... | collective-permute-start | bytes 3145736 | tf_op jit(solution)/shard_map/ppermute | solution.py:18
  732.8 55.2 %collective-permute-start.47 = (bf16[512,2048]{1,0:T(8,128)(2,1)}, bf16[512,2048]{1,0:T(8,128)(2,1)}, u32[]{:S(2)}, u32[]{:S(2)}) collective-permute-start(bf16[512,2048]{1,0:T(8,128)(2,1)} %fusion.19), channel_id=1, source_target_pairs={{0,16},{8,24},{16,0},{24,8},{1,17},{9,25},{17,1},{25,9},{2,18},{10... | collective-permute-start | bytes 6291464 | tf_op jit(solution)/shard_map/ppermute | solution.py:18
  742.9 45.8 %collective-permute-start.45 = (bf16[512,2048]{1,0:T(8,128)(2,1)}, bf16[512,2048]{1,0:T(8,128)(2,1)}, u32[]{:S(2)}, u32[]{:S(2)}) collective-permute-start(bf16[512,2048]{1,0:T(8,128)(2,1)} %fusion.18), channel_id=1, source_target_pairs={{0,8},{8,0},{16,24},{24,16},{1,9},{9,1},{17,25},{25,17},{2,10},{10... | collective-permute-start | bytes 6291464 | tf_op jit(solution)/shard_map/ppermute | solution.py:18
  773.9 26.3 %collective-permute-start.49 = (bf16[256,2048]{1,0:T(8,128)(2,1)}, bf16[256,2048]{1,0:T(8,128)(2,1)S(1)}, u32[]{:S(2)}, u32[]{:S(2)}) collective-permute-start(bf16[256,2048]{1,0:T(8,128)(2,1)} %reduce-scatter.14.cloned.1.call-done.refs_0_), channel_id=1, source_target_pairs={{0,16},{8,24},{16,0},{24,8},{1,17},{9,25},{17,1},{25,9},{2,18},{10... | collective-permute-start | bytes 3145736 | tf_op jit(solution)/shard_map/ppermute | solution.py:18
  775.3 26.3 %collective-permute-start.48 = (bf16[256,2048]{1,0:T(8,128)(2,1)}, bf16[256,2048]{1,0:T(8,128)(2,1)S(1)}, u32[]{:S(2)}, u32[]{:S(2)}) collective-permute-start(bf16[256,2048]{1,0:T(8,128)(2,1)} %reduce-scatter.14.cloned.1.call-done.refs_0_), channel_id=1, source_target_pairs={{0,8},{8,0},{16,24},{24,16},{1,9},{9,1},{17,25},{25,17},{2,10},{10... | collective-permute-start | bytes 3145736 | tf_op jit(solution)/shard_map/ppermute | solution.py:18
  786.3 30.2 %collective-permute-start.58 = (bf16[80,2048]{1,0:T(8,128)(2,1)S(1)}, bf16[80,2048]{1,0:T(8,128)(2,1)S(1)}, u32[]{:S(2)}, u32[]{:S(2)}) collective-permute-start(bf16[80,2048]{1,0:T(8,128)(2,1)S(1)} %slice.288), channel_id=1, source_target_pairs={{0,16},{8,24},{16,0},{24,8},{1,17},{9,25},{17,1},{25,9},{2,18},{10... | collective-permute-start | bytes 983048 | tf_op jit(solution)/shard_map/ppermute | solution.py:18
  788.0 28.6 %collective-permute-start.59 = (bf16[96,2048]{1,0:T(8,128)(2,1)S(1)}, bf16[96,2048]{1,0:T(8,128)(2,1)S(1)}, u32[]{:S(2)}, u32[]{:S(2)}) collective-permute-start(bf16[96,2048]{1,0:T(8,128)(2,1)S(1)} %slice.289), channel_id=1, source_target_pairs={{0,8},{8,0},{16,24},{24,16},{1,9},{9,1},{17,25},{25,17},{2,10},{10... | collective-permute-start | bytes 1179656 | tf_op jit(solution)/shard_map/ppermute | solution.py:18
  802.2 13.5 %collective-permute-start.54 = (bf16[256,512]{1,0:T(8,128)(2,1)S(1)}, bf16[256,512]{1,0:T(8,128)(2,1)S(1)}, u32[]{:S(2)}, u32[]{:S(2)}) collective-permute-start(bf16[256,512]{1,0:T(8,128)(2,1)S(1)} %copy-done.38), channel_id=1, source_target_pairs={{0,8},{8,0},{16,24},{24,16},{1,9},{9,1},{17,25},{25,17},{2,10},{10... | collective-permute-start | bytes 786440 | tf_op jit(solution)/shard_map/ppermute | solution.py:18
  803.7 28.4 %collective-permute-start.51 = (bf16[128,2048]{1,0:T(8,128)(2,1)S(1)}, bf16[128,2048]{1,0:T(8,128)(2,1)S(1)}, u32[]{:S(2)}, u32[]{:S(2)}) collective-permute-start(bf16[128,2048]{1,0:T(8,128)(2,1)S(1)} %slice.312), channel_id=1, source_target_pairs={{0,8},{8,0},{16,24},{24,16},{1,9},{9,1},{17,25},{25,17},{2,10},{10... | collective-permute-start | bytes 1572872 | tf_op jit(solution)/shard_map/ppermute | solution.py:18
  810.3 20.8 %collective-permute-start.57 = (bf16[128,512]{1,0:T(8,128)(2,1)S(1)}, bf16[128,512]{1,0:T(8,128)(2,1)S(1)}, u32[]{:S(2)}, u32[]{:S(2)}) collective-permute-start(bf16[128,512]{1,0:T(8,128)(2,1)S(1)} %slice.314), channel_id=1, source_target_pairs={{0,8},{8,0},{16,24},{24,16},{1,9},{9,1},{17,25},{25,17},{2,10},{10... | collective-permute-start | bytes 393224 | tf_op jit(solution)/shard_map/ppermute | solution.py:18
  815.7 15.3 %collective-permute-start.55 = (bf16[128,512]{1,0:T(8,128)(2,1)S(1)}, bf16[128,512]{1,0:T(8,128)(2,1)S(1)}, u32[]{:S(2)}, u32[]{:S(2)}) collective-permute-start(bf16[128,512]{1,0:T(8,128)(2,1)S(1)} %slice.313), channel_id=1, source_target_pairs={{0,16},{8,24},{16,0},{24,8},{1,17},{9,25},{17,1},{25,9},{2,18},{10... | collective-permute-start | bytes 393224 | tf_op jit(solution)/shard_map/ppermute | solution.py:18
  816.5 18.0 %collective-permute-start.52 = (bf16[256,2048]{1,0:T(8,128)(2,1)S(1)}, bf16[256,2048]{1,0:T(8,128)(2,1)S(1)}, u32[]{:S(2)}, u32[]{:S(2)}) collective-permute-start(bf16[256,2048]{1,0:T(8,128)(2,1)S(1)} %broadcast_select_fusion), channel_id=1, source_target_pairs={{0,1},{1,0},{2,3},{3,2},{4,5},{5,4},{6,7},{7,6},{8,9},{9,8},{10,11... | collective-permute-start | bytes 3145736 | tf_op jit(solution)/shard_map/ppermute | solution.py:23
  816.6 15.5 %collective-permute-start.50 = (bf16[128,2048]{1,0:T(8,128)(2,1)S(1)}, bf16[128,2048]{1,0:T(8,128)(2,1)S(1)}, u32[]{:S(2)}, u32[]{:S(2)}) collective-permute-start(bf16[128,2048]{1,0:T(8,128)(2,1)S(1)} %slice.311), channel_id=1, source_target_pairs={{0,16},{8,24},{16,0},{24,8},{1,17},{9,25},{17,1},{25,9},{2,18},{10... | collective-permute-start | bytes 1572872 | tf_op jit(solution)/shard_map/ppermute | solution.py:18
  (62 other events, 712.6 us)
Sparse Core Ops, SparseCore 0:
  20.5 85.5 all-gather.4
  108.3 29.3 all-gather.6
  139.9 107.1 all-gather.8
  249.1 58.7 all-gather.10
  373.3 65.2 reduce-scatter.5
  514.5 65.5 reduce-scatter.7
  583.0 63.2 reduce-scatter.9
  649.1 34.1 reduce-scatter.11
  685.5 88.3 reduce-scatter.13
